TPU v7x, 256 devices: a whole 4x4x8 slice. The times are simulated.
256 devices in a mesh: group: 16 (over z, core), blk: 16 (over y, x).
Axes of the slice: x: 4, y: 4, z: 8, core: 2. Of those that a mesh axis runs over, the one named last changes fastest.
Arguments:
- hamiltonian: bfloat16 [4096, 18, 64, 256], P(('group', 'blk')), may hold values from -0.09375 to 0.09375
- block_columns: int32 [4096, 18, 4], P(('group', 'blk')), may hold values from 0 to 15, as said below
- potential: float32 [262144], P(('group', 'blk')), may hold values from -1 to 1
- trial_slab: float32 [262144, 128], P(('group', 'blk')), may hold values from -40 to 40
Outputs:
- ortho_slab: float32 [262144, 128], P(('group', 'blk'))
- upper_factor: float32 [128, 128], replicated
Inputs may be any that keep to these rules, and one draw needn't show every extreme that they name: `block_columns`: for each row block and each source, the 4 entries are distinct.
All inputs are finite; a program needn't handle non-finite values.
Results may differ from a plain program's by a relative error of at most 0.0021.
Values may be sent and summed in bfloat16 or wider, within the bound.
A program may use at most 64 MiB of HBM per device.

v0:
```python
import jax
import jax.numpy as jnp
from jax import lax
from jax.sharding import PartitionSpec as P

precise = lax.Precision.HIGHEST


def padded(block, sides, width):
    for axis, dim in sides:
        count = lax.axis_size(axis)
        forward = [(i, i + 1) for i in range(count - 1)]
        backward = [(target, source) for source, target in forward]
        low = lax.ppermute(
            lax.slice_in_dim(block, block.shape[dim] - width, None, axis=dim), axis, forward
        )
        high = lax.ppermute(lax.slice_in_dim(block, 0, width, axis=dim), axis, backward)
        block = jnp.concatenate([low, block, high], axis=dim)
    return block


def shifted(value, axis, steps):
    count = lax.axis_size(axis)
    pairs = [(source, (source + steps) % count) for source in range(count)]
    return lax.ppermute(value, axis, pairs)


def from_partner(block, axis, bit):
    count = lax.axis_size(axis)
    route = []
    for low in range(count):
        high = low | 1 << bit
        if high != low and high < count:
            route += [(low, high), (high, low)]
    return lax.ppermute(block, axis, route)


def couple_source(hamiltonian, block_columns, piece, source):
    coupling = lax.dynamic_index_in_dim(hamiltonian, source, 1, keepdims=False)
    columns = lax.dynamic_index_in_dim(block_columns, source, 1, keepdims=False)
    rows_here, per_source = columns.shape
    picked = piece[columns].reshape(rows_here, per_source * piece.shape[1], piece.shape[2])
    return jnp.einsum("rik,rkn->rin", coupling, picked, preferred_element_type=jnp.float32)


def couple_all(hamiltonian, block_columns, rounded):
    cycle_size = lax.axis_size("blk")
    shard_blocks = rounded.shape[0]
    with_rims = padded(rounded, (("group", 0),), shard_blocks)
    summed = couple_source(hamiltonian, block_columns, with_rims[:shard_blocks], cycle_size)
    summed = summed + couple_source(
        hamiltonian, block_columns, with_rims[2 * shard_blocks :], cycle_size + 1
    )
    held_piece = rounded
    own_index = lax.axis_index("blk")
    for turn_index in range(cycle_size):
        source = (own_index - turn_index) % cycle_size
        summed = summed + couple_source(hamiltonian, block_columns, held_piece, source)
        if turn_index + 1 < cycle_size:
            held_piece = shifted(held_piece, "blk", 1)
    return summed


def on_device(hamiltonian, block_columns, potential, trial_slab):
    shard_blocks = hamiltonian.shape[0]
    block_size = hamiltonian.shape[2]
    states = trial_slab.shape[1]
    start_slab = trial_slab.reshape(shard_blocks, block_size, states)
    weights = potential.reshape(shard_blocks, block_size, 1)
    coupled_start = couple_all(hamiltonian, block_columns, start_slab.astype(jnp.bfloat16))
    filtered_once = 0.5 * (coupled_start + weights * start_slab)
    coupled_next = couple_all(hamiltonian, block_columns, filtered_once.astype(jnp.bfloat16))
    filtered = coupled_next + weights * filtered_once - start_slab
    flat = filtered.reshape(shard_blocks * block_size, states)
    rows_total = flat.shape[0] * lax.axis_size("group") * lax.axis_size("blk")
    local_gram = jnp.dot(flat.T, flat, precision=precise) / rows_total
    lower = jnp.linalg.cholesky(local_gram)
    for level in range(lax.axis_size("blk").bit_length() - 1):
        partner = from_partner(lower.astype(jnp.bfloat16), "blk", level).astype(lower.dtype)
        lower = jnp.linalg.cholesky(
            jnp.dot(lower, lower.T, precision=precise)
            + jnp.dot(partner, partner.T, precision=precise)
        )
    for level in range(lax.axis_size("group").bit_length() - 1):
        partner = from_partner(lower, "group", level)
        lower = jnp.linalg.cholesky(
            jnp.dot(lower, lower.T, precision=precise)
            + jnp.dot(partner, partner.T, precision=precise)
        )
    ortho_slab = lax.linalg.triangular_solve(
        lower, flat, left_side=False, lower=True, transpose_a=True
    )
    return (ortho_slab, jnp.transpose(lower))


def solution(mesh):
    placed = (
        P(("group", "blk"), None, None, None),
        P(("group", "blk"), None, None),
        P(("group", "blk")),
        P(("group", "blk"), None),
    )
    return jax.shard_map(
        on_device,
        mesh=mesh,
        in_specs=placed,
        out_specs=(P(("group", "blk"), None), P()),
        check_vma=False,
    )
```

profile of v0, /device:TPU:32, one launch (start us, length us, event | category | flops | bytes accessed | tf_op | source)
XLA Modules:
  0.0 521.9 jit_solution(1450984741439063487)
XLA Ops:
  1.7 1.6 collective-permute-start.2
  3.3 1.9 collective-permute-start.1
  5.2 2.4 collective-permute-start
  8.7 1.8 constant_dynamic-slice_fusion
  18.7 2.2 fusion.10
  25.3 1.5 fusion.7
  26.8 6.1 %collective-permute-done.3 = bf16[16,64,128]{2,1,0:T(8,128)(2,1)S(1)} collective-permute-done((bf16[16,64,128]{2,1,0:T(8,128)(2,1)S(1)}, bf16[16,64,128]{2,1,0:T(8,128)(2,1)S(1)}, u32[]{:S(2)}, u32[]{:S(2)}) %collective-permute-start.3) | collective-permute-done | bytes 262176 | tf_op jit(solution)/shard_map/ppermute | solution.py:25
  35.0 9.7 %collective-permute-done.4 = bf16[16,64,128]{2,1,0:T(8,128)(2,1)S(1)} collective-permute-done((bf16[16,64,128]{2,1,0:T(8,128)(2,1)S(1)}, bf16[16,64,128]{2,1,0:T(8,128)(2,1)S(1)}, u32[]{:S(2)}, u32[]{:S(2)}) %collective-permute-start.4) | collective-permute-done | bytes 262176 | tf_op jit(solution)/shard_map/ppermute | solution.py:25
  46.9 8.9 %collective-permute-done.5 = bf16[16,64,128]{2,1,0:T(8,128)(2,1)S(1)} collective-permute-done((bf16[16,64,128]{2,1,0:T(8,128)(2,1)S(1)}, bf16[16,64,128]{2,1,0:T(8,128)(2,1)S(1)}, u32[]{:S(2)}, u32[]{:S(2)}) %collective-permute-start.5) | collective-permute-done | bytes 262176 | tf_op jit(solution)/shard_map/ppermute | solution.py:25
  57.9 8.0 %collective-permute-done.6 = bf16[16,64,128]{2,1,0:T(8,128)(2,1)S(1)} collective-permute-done((bf16[16,64,128]{2,1,0:T(8,128)(2,1)S(1)}, bf16[16,64,128]{2,1,0:T(8,128)(2,1)S(1)}, u32[]{:S(2)}, u32[]{:S(2)}) %collective-permute-start.6) | collective-permute-done | bytes 262176 | tf_op jit(solution)/shard_map/ppermute | solution.py:25
  68.1 7.6 %collective-permute-done.7 = bf16[16,64,128]{2,1,0:T(8,128)(2,1)S(1)} collective-permute-done((bf16[16,64,128]{2,1,0:T(8,128)(2,1)S(1)}, bf16[16,64,128]{2,1,0:T(8,128)(2,1)S(1)}, u32[]{:S(2)}, u32[]{:S(2)}) %collective-permute-start.7) | collective-permute-done | bytes 262176 | tf_op jit(solution)/shard_map/ppermute | solution.py:25
  77.9 7.5 %collective-permute-done.8 = bf16[16,64,128]{2,1,0:T(8,128)(2,1)S(1)} collective-permute-done((bf16[16,64,128]{2,1,0:T(8,128)(2,1)S(1)}, bf16[16,64,128]{2,1,0:T(8,128)(2,1)S(1)}, u32[]{:S(2)}, u32[]{:S(2)}) %collective-permute-start.8) | collective-permute-done | bytes 262176 | tf_op jit(solution)/shard_map/ppermute | solution.py:25
  87.6 7.6 %collective-permute-done.9 = bf16[16,64,128]{2,1,0:T(8,128)(2,1)S(1)} collective-permute-done((bf16[16,64,128]{2,1,0:T(8,128)(2,1)S(1)}, bf16[16,64,128]{2,1,0:T(8,128)(2,1)S(1)}, u32[]{:S(2)}, u32[]{:S(2)}) %collective-permute-start.9) | collective-permute-done | bytes 262176 | tf_op jit(solution)/shard_map/ppermute | solution.py:25
  97.3 8.5 %collective-permute-done.10 = bf16[16,64,128]{2,1,0:T(8,128)(2,1)S(1)} collective-permute-done((bf16[16,64,128]{2,1,0:T(8,128)(2,1)S(1)}, bf16[16,64,128]{2,1,0:T(8,128)(2,1)S(1)}, u32[]{:S(2)}, u32[]{:S(2)}) %collective-permute-start.10) | collective-permute-done | bytes 262176 | tf_op jit(solution)/shard_map/ppermute | solution.py:25
  107.9 9.7 %collective-permute-done.11 = bf16[16,64,128]{2,1,0:T(8,128)(2,1)S(1)} collective-permute-done((bf16[16,64,128]{2,1,0:T(8,128)(2,1)S(1)}, bf16[16,64,128]{2,1,0:T(8,128)(2,1)S(1)}, u32[]{:S(2)}, u32[]{:S(2)}) %collective-permute-start.11) | collective-permute-done | bytes 262176 | tf_op jit(solution)/shard_map/ppermute | solution.py:25
  119.7 9.9 %collective-permute-done.12 = bf16[16,64,128]{2,1,0:T(8,128)(2,1)S(1)} collective-permute-done((bf16[16,64,128]{2,1,0:T(8,128)(2,1)S(1)}, bf16[16,64,128]{2,1,0:T(8,128)(2,1)S(1)}, u32[]{:S(2)}, u32[]{:S(2)}) %collective-permute-start.12) | collective-permute-done | bytes 262176 | tf_op jit(solution)/shard_map/ppermute | solution.py:25
  131.8 9.0 %collective-permute-done.13 = bf16[16,64,128]{2,1,0:T(8,128)(2,1)S(1)} collective-permute-done((bf16[16,64,128]{2,1,0:T(8,128)(2,1)S(1)}, bf16[16,64,128]{2,1,0:T(8,128)(2,1)S(1)}, u32[]{:S(2)}, u32[]{:S(2)}) %collective-permute-start.13) | collective-permute-done | bytes 262176 | tf_op jit(solution)/shard_map/ppermute | solution.py:25
  143.0 8.2 %collective-permute-done.14 = bf16[16,64,128]{2,1,0:T(8,128)(2,1)S(1)} collective-permute-done((bf16[16,64,128]{2,1,0:T(8,128)(2,1)S(1)}, bf16[16,64,128]{2,1,0:T(8,128)(2,1)S(1)}, u32[]{:S(2)}, u32[]{:S(2)}) %collective-permute-start.14) | collective-permute-done | bytes 262176 | tf_op jit(solution)/shard_map/ppermute | solution.py:25
  153.4 7.6 %collective-permute-done.15 = bf16[16,64,128]{2,1,0:T(8,128)(2,1)S(1)} collective-permute-done((bf16[16,64,128]{2,1,0:T(8,128)(2,1)S(1)}, bf16[16,64,128]{2,1,0:T(8,128)(2,1)S(1)}, u32[]{:S(2)}, u32[]{:S(2)}) %collective-permute-start.15) | collective-permute-done | bytes 262176 | tf_op jit(solution)/shard_map/ppermute | solution.py:25
  163.1 9.1 %collective-permute-done.16 = bf16[16,64,128]{2,1,0:T(8,128)(2,1)S(1)} collective-permute-done((bf16[16,64,128]{2,1,0:T(8,128)(2,1)S(1)}, bf16[16,64,128]{2,1,0:T(8,128)(2,1)S(1)}, u32[]{:S(2)}, u32[]{:S(2)}) %collective-permute-start.16) | collective-permute-done | bytes 262176 | tf_op jit(solution)/shard_map/ppermute | solution.py:25
  173.0 2.2 multiply_convert_fusion
  175.9 1.9 collective-permute-start.18
  177.8 2.8 collective-permute-start.17
  182.8 2.2 fusion.12
  185.8 2.2 fusion.44
  188.7 2.5 fusion.6
  191.2 5.6 %collective-permute-done.20 = bf16[16,64,128]{2,1,0:T(8,128)(2,1)S(1)} collective-permute-done((bf16[16,64,128]{2,1,0:T(8,128)(2,1)S(1)}, bf16[16,64,128]{2,1,0:T(8,128)(2,1)S(1)}, u32[]{:S(2)}, u32[]{:S(2)}) %collective-permute-start.20) | collective-permute-done | bytes 262176 | tf_op jit(solution)/shard_map/ppermute | solution.py:25
  197.6 2.3 convolution_add_fusion.15
  200.0 9.9 %collective-permute-done.21 = bf16[16,64,128]{2,1,0:T(8,128)(2,1)S(1)} collective-permute-done((bf16[16,64,128]{2,1,0:T(8,128)(2,1)S(1)}, bf16[16,64,128]{2,1,0:T(8,128)(2,1)S(1)}, u32[]{:S(2)}, u32[]{:S(2)}) %collective-permute-start.21) | collective-permute-done | bytes 262176 | tf_op jit(solution)/shard_map/ppermute | solution.py:25
  210.7 1.5 convolution_add_fusion.14
  212.2 10.1 %collective-permute-done.22 = bf16[16,64,128]{2,1,0:T(8,128)(2,1)S(1)} collective-permute-done((bf16[16,64,128]{2,1,0:T(8,128)(2,1)S(1)}, bf16[16,64,128]{2,1,0:T(8,128)(2,1)S(1)}, u32[]{:S(2)}, u32[]{:S(2)}) %collective-permute-start.22) | collective-permute-done | bytes 262176 | tf_op jit(solution)/shard_map/ppermute | solution.py:25
  224.6 9.4 %collective-permute-done.23 = bf16[16,64,128]{2,1,0:T(8,128)(2,1)S(1)} collective-permute-done((bf16[16,64,128]{2,1,0:T(8,128)(2,1)S(1)}, bf16[16,64,128]{2,1,0:T(8,128)(2,1)S(1)}, u32[]{:S(2)}, u32[]{:S(2)}) %collective-permute-start.23) | collective-permute-done | bytes 262176 | tf_op jit(solution)/shard_map/ppermute | solution.py:25
  236.2 8.5 %collective-permute-done.24 = bf16[16,64,128]{2,1,0:T(8,128)(2,1)S(1)} collective-permute-done((bf16[16,64,128]{2,1,0:T(8,128)(2,1)S(1)}, bf16[16,64,128]{2,1,0:T(8,128)(2,1)S(1)}, u32[]{:S(2)}, u32[]{:S(2)}) %collective-permute-start.24) | collective-permute-done | bytes 262176 | tf_op jit(solution)/shard_map/ppermute | solution.py:25
  246.9 8.3 %collective-permute-done.25 = bf16[16,64,128]{2,1,0:T(8,128)(2,1)S(1)} collective-permute-done((bf16[16,64,128]{2,1,0:T(8,128)(2,1)S(1)}, bf16[16,64,128]{2,1,0:T(8,128)(2,1)S(1)}, u32[]{:S(2)}, u32[]{:S(2)}) %collective-permute-start.25) | collective-permute-done | bytes 262176 | tf_op jit(solution)/shard_map/ppermute | solution.py:25
  257.5 8.3 %collective-permute-done.26 = bf16[16,64,128]{2,1,0:T(8,128)(2,1)S(1)} collective-permute-done((bf16[16,64,128]{2,1,0:T(8,128)(2,1)S(1)}, bf16[16,64,128]{2,1,0:T(8,128)(2,1)S(1)}, u32[]{:S(2)}, u32[]{:S(2)}) %collective-permute-start.26) | collective-permute-done | bytes 262176 | tf_op jit(solution)/shard_map/ppermute | solution.py:25
  268.0 8.3 %collective-permute-done.27 = bf16[16,64,128]{2,1,0:T(8,128)(2,1)S(1)} collective-permute-done((bf16[16,64,128]{2,1,0:T(8,128)(2,1)S(1)}, bf16[16,64,128]{2,1,0:T(8,128)(2,1)S(1)}, u32[]{:S(2)}, u32[]{:S(2)}) %collective-permute-start.27) | collective-permute-done | bytes 262176 | tf_op jit(solution)/shard_map/ppermute | solution.py:25
  278.7 8.6 %collective-permute-done.28 = bf16[16,64,128]{2,1,0:T(8,128)(2,1)S(1)} collective-permute-done((bf16[16,64,128]{2,1,0:T(8,128)(2,1)S(1)}, bf16[16,64,128]{2,1,0:T(8,128)(2,1)S(1)}, u32[]{:S(2)}, u32[]{:S(2)}) %collective-permute-start.28) | collective-permute-done | bytes 262176 | tf_op jit(solution)/shard_map/ppermute | solution.py:25
  289.6 9.8 %collective-permute-done.29 = bf16[16,64,128]{2,1,0:T(8,128)(2,1)S(1)} collective-permute-done((bf16[16,64,128]{2,1,0:T(8,128)(2,1)S(1)}, bf16[16,64,128]{2,1,0:T(8,128)(2,1)S(1)}, u32[]{:S(2)}, u32[]{:S(2)}) %collective-permute-start.29) | collective-permute-done | bytes 262176 | tf_op jit(solution)/shard_map/ppermute | solution.py:25
  300.2 2.2 convolution_add_fusion.6
  302.4 10.0 %collective-permute-done.30 = bf16[16,64,128]{2,1,0:T(8,128)(2,1)S(1)} collective-permute-done((bf16[16,64,128]{2,1,0:T(8,128)(2,1)S(1)}, bf16[16,64,128]{2,1,0:T(8,128)(2,1)S(1)}, u32[]{:S(2)}, u32[]{:S(2)}) %collective-permute-start.30) | collective-permute-done | bytes 262176 | tf_op jit(solution)/shard_map/ppermute | solution.py:25
  313.3 1.5 convolution_add_fusion.5
  314.8 10.1 %collective-permute-done.31 = bf16[16,64,128]{2,1,0:T(8,128)(2,1)S(1)} collective-permute-done((bf16[16,64,128]{2,1,0:T(8,128)(2,1)S(1)}, bf16[16,64,128]{2,1,0:T(8,128)(2,1)S(1)}, u32[]{:S(2)}, u32[]{:S(2)}) %collective-permute-start.31) | collective-permute-done | bytes 262176 | tf_op jit(solution)/shard_map/ppermute | solution.py:25
  325.8 2.2 convolution_add_fusion.4
  327.9 8.6 %collective-permute-done.32 = bf16[16,64,128]{2,1,0:T(8,128)(2,1)S(1)} collective-permute-done((bf16[16,64,128]{2,1,0:T(8,128)(2,1)S(1)}, bf16[16,64,128]{2,1,0:T(8,128)(2,1)S(1)}, u32[]{:S(2)}, u32[]{:S(2)}) %collective-permute-start.32) | collective-permute-done | bytes 262176 | tf_op jit(solution)/shard_map/ppermute | solution.py:25
  338.9 8.1 %collective-permute-done.33 = bf16[16,64,128]{2,1,0:T(8,128)(2,1)S(1)} collective-permute-done((bf16[16,64,128]{2,1,0:T(8,128)(2,1)S(1)}, bf16[16,64,128]{2,1,0:T(8,128)(2,1)S(1)}, u32[]{:S(2)}, u32[]{:S(2)}) %collective-permute-start.33) | collective-permute-done | bytes 262176 | tf_op jit(solution)/shard_map/ppermute | solution.py:25
  350.4 11.7 %cholesky.149 = f32[128,128]{1,0:T(8,128)S(1)} custom-call(f32[128,128]{1,0:T(8,128)S(1)} %fusion.98), custom_call_target="Cholesky" | custom-call | tf_op jit(solution)/shard_map/jit(cholesky)/cholesky | solution.py:77
  364.6 3.0 collective-permute-done.34
  367.9 11.7 %cholesky.160 = f32[128,128]{1,0:T(8,128)S(1)} custom-call(f32[128,128]{1,0:T(8,128)S(1)} %fusion.97), custom_call_target="Cholesky" | custom-call | tf_op jit(solution)/shard_map/jit(cholesky)/cholesky | solution.py:80
  382.0 4.5 collective-permute-done.35
  386.7 11.7 %cholesky.171 = f32[128,128]{1,0:T(8,128)S(1)} custom-call(f32[128,128]{1,0:T(8,128)S(1)} %fusion.96), custom_call_target="Cholesky" | custom-call | tf_op jit(solution)/shard_map/jit(cholesky)/cholesky | solution.py:80
  401.2 3.0 collective-permute-done.36
  404.5 11.7 %cholesky.182 = f32[128,128]{1,0:T(8,128)S(1)} custom-call(f32[128,128]{1,0:T(8,128)S(1)} %fusion.95), custom_call_target="Cholesky" | custom-call | tf_op jit(solution)/shard_map/jit(cholesky)/cholesky | solution.py:80
  418.6 4.5 collective-permute-done.37
  423.3 11.7 %cholesky.193 = f32[128,128]{1,0:T(8,128)S(1)} custom-call(f32[128,128]{1,0:T(8,128)S(1)} %fusion.94), custom_call_target="Cholesky" | custom-call | tf_op jit(solution)/shard_map/jit(cholesky)/cholesky | solution.py:80
  438.3 11.7 %cholesky.204 = f32[128,128]{1,0:T(8,128)S(1)} custom-call(f32[128,128]{1,0:T(8,128)S(1)} %fusion.93), custom_call_target="Cholesky" | custom-call | tf_op jit(solution)/shard_map/jit(cholesky)/cholesky | solution.py:86
  451.7 4.0 collective-permute-done.39
  456.1 11.7 %cholesky.215 = f32[128,128]{1,0:T(8,128)S(1)} custom-call(f32[128,128]{1,0:T(8,128)S(1)} %fusion.92), custom_call_target="Cholesky" | custom-call | tf_op jit(solution)/shard_map/jit(cholesky)/cholesky | solution.py:86
  469.1 2.6 collective-permute-start.40
  472.0 2.6 collective-permute-done.40
  475.0 11.7 %cholesky.226 = f32[128,128]{1,0:T(8,128)S(1)} custom-call(f32[128,128]{1,0:T(8,128)S(1)} %fusion.91), custom_call_target="Cholesky" | custom-call | tf_op jit(solution)/shard_map/jit(cholesky)/cholesky | solution.py:86
  488.0 4.2 collective-permute-start.41
  492.5 3.8 collective-permute-done.41
  496.7 11.7 %cholesky.237 = f32[128,128]{1,0:T(8,128)S(1)} custom-call(f32[128,128]{1,0:T(8,128)S(1)} %fusion.90), custom_call_target="Cholesky" | custom-call | tf_op jit(solution)/shard_map/jit(cholesky)/cholesky | solution.py:86
  509.7 9.8 %custom-call.5 = f32[1,128,128]{1,2,0:T(8,128)S(1)} custom-call(f32[1,128,128]{2,1,0:T(8,128)S(1)} %get-tuple-element.8), custom_call_target="InvertDiagBlocksLowerTriangular" | custom-call | tf_op jit(solution)/shard_map/triangular_solve | solution.py:90
  (255 shorter events, 96.2 us)
Async XLA Ops:
  1.7 19.2 %collective-permute-start.2 = (bf16[16,64,128]{2,1,0:T(8,128)(2,1)S(1)}, bf16[16,64,128]{2,1,0:T(8,128)(2,1)S(1)}, u32[]{:S(2)}, u32[]{:S(2)}) collective-permute-start(bf16[16,64,128]{2,1,0:T(8,128)(2,1)S(1)} %convert_element_type.22), channel_id=1, source_target_pairs={{0,1},{1,2},{2,3},{3,4},{4,5},{5,6},{6,7},{7,8},{8,9},{9,10},{10,1... | collective-permute-start | bytes 786440 | tf_op jit(solution)/shard_map/ppermute | solution.py:25
  3.3 14.7 %collective-permute-start.1 = (bf16[16,64,128]{2,1,0:T(8,128)(2,1)S(1)}, bf16[16,64,128]{2,1,0:T(8,128)(2,1)S(1)}, u32[]{:S(2)}, u32[]{:S(2)}) collective-permute-start(bf16[16,64,128]{2,1,0:T(8,128)(2,1)S(1)} %convert_element_type.22), channel_id=1, source_target_pairs={{16,0},{32,16},{48,32},{64,48},{80,64},{96,80},{112,96},{128,112},... | collective-permute-start | bytes 786440 | tf_op jit(solution)/shard_map/ppermute | solution.py:17
  5.2 19.3 %collective-permute-start = (bf16[16,64,128]{2,1,0:T(8,128)(2,1)S(1)}, bf16[16,64,128]{2,1,0:T(8,128)(2,1)S(1)}, u32[]{:S(2)}, u32[]{:S(2)}) collective-permute-start(bf16[16,64,128]{2,1,0:T(8,128)(2,1)S(1)} %convert_element_type.22), channel_id=1, source_target_pairs={{0,16},{16,32},{32,48},{48,64},{64,80},{80,96},{96,112},{112,128},... | collective-permute-start | bytes 786440 | tf_op jit(solution)/shard_map/ppermute | solution.py:14
  20.9 12.0 %collective-permute-start.3 = (bf16[16,64,128]{2,1,0:T(8,128)(2,1)S(1)}, bf16[16,64,128]{2,1,0:T(8,128)(2,1)S(1)}, u32[]{:S(2)}, u32[]{:S(2)}) collective-permute-start(bf16[16,64,128]{2,1,0:T(8,128)(2,1)S(1)} %collective-permute-done.2), channel_id=1, source_target_pairs={{0,1},{1,2},{2,3},{3,4},{4,5},{5,6},{6,7},{7,8},{8,9},{9,10},{10,1... | collective-permute-start | bytes 786440 | tf_op jit(solution)/shard_map/ppermute | solution.py:25
  32.9 11.9 %collective-permute-start.4 = (bf16[16,64,128]{2,1,0:T(8,128)(2,1)S(1)}, bf16[16,64,128]{2,1,0:T(8,128)(2,1)S(1)}, u32[]{:S(2)}, u32[]{:S(2)}) collective-permute-start(bf16[16,64,128]{2,1,0:T(8,128)(2,1)S(1)} %collective-permute-done.3), channel_id=1, source_target_pairs={{0,1},{1,2},{2,3},{3,4},{4,5},{5,6},{6,7},{7,8},{8,9},{9,10},{10,1... | collective-permute-start | bytes 786440 | tf_op jit(solution)/shard_map/ppermute | solution.py:25
  44.7 11.0 %collective-permute-start.5 = (bf16[16,64,128]{2,1,0:T(8,128)(2,1)S(1)}, bf16[16,64,128]{2,1,0:T(8,128)(2,1)S(1)}, u32[]{:S(2)}, u32[]{:S(2)}) collective-permute-start(bf16[16,64,128]{2,1,0:T(8,128)(2,1)S(1)} %collective-permute-done.4), channel_id=1, source_target_pairs={{0,1},{1,2},{2,3},{3,4},{4,5},{5,6},{6,7},{7,8},{8,9},{9,10},{10,1... | collective-permute-start | bytes 786440 | tf_op jit(solution)/shard_map/ppermute | solution.py:25
  55.8 10.1 %collective-permute-start.6 = (bf16[16,64,128]{2,1,0:T(8,128)(2,1)S(1)}, bf16[16,64,128]{2,1,0:T(8,128)(2,1)S(1)}, u32[]{:S(2)}, u32[]{:S(2)}) collective-permute-start(bf16[16,64,128]{2,1,0:T(8,128)(2,1)S(1)} %collective-permute-done.5), channel_id=1, source_target_pairs={{0,1},{1,2},{2,3},{3,4},{4,5},{5,6},{6,7},{7,8},{8,9},{9,10},{10,1... | collective-permute-start | bytes 786440 | tf_op jit(solution)/shard_map/ppermute | solution.py:25
  65.9 9.7 %collective-permute-start.7 = (bf16[16,64,128]{2,1,0:T(8,128)(2,1)S(1)}, bf16[16,64,128]{2,1,0:T(8,128)(2,1)S(1)}, u32[]{:S(2)}, u32[]{:S(2)}) collective-permute-start(bf16[16,64,128]{2,1,0:T(8,128)(2,1)S(1)} %collective-permute-done.6), channel_id=1, source_target_pairs={{0,1},{1,2},{2,3},{3,4},{4,5},{5,6},{6,7},{7,8},{8,9},{9,10},{10,1... | collective-permute-start | bytes 786440 | tf_op jit(solution)/shard_map/ppermute | solution.py:25
  75.6 9.8 %collective-permute-start.8 = (bf16[16,64,128]{2,1,0:T(8,128)(2,1)S(1)}, bf16[16,64,128]{2,1,0:T(8,128)(2,1)S(1)}, u32[]{:S(2)}, u32[]{:S(2)}) collective-permute-start(bf16[16,64,128]{2,1,0:T(8,128)(2,1)S(1)} %collective-permute-done.7), channel_id=1, source_target_pairs={{0,1},{1,2},{2,3},{3,4},{4,5},{5,6},{6,7},{7,8},{8,9},{9,10},{10,1... | collective-permute-start | bytes 786440 | tf_op jit(solution)/shard_map/ppermute | solution.py:25
  85.5 9.7 %collective-permute-start.9 = (bf16[16,64,128]{2,1,0:T(8,128)(2,1)S(1)}, bf16[16,64,128]{2,1,0:T(8,128)(2,1)S(1)}, u32[]{:S(2)}, u32[]{:S(2)}) collective-permute-start(bf16[16,64,128]{2,1,0:T(8,128)(2,1)S(1)} %collective-permute-done.8), channel_id=1, source_target_pairs={{0,1},{1,2},{2,3},{3,4},{4,5},{5,6},{6,7},{7,8},{8,9},{9,10},{10,1... | collective-permute-start | bytes 786440 | tf_op jit(solution)/shard_map/ppermute | solution.py:25
  95.2 10.6 %collective-permute-start.10 = (bf16[16,64,128]{2,1,0:T(8,128)(2,1)S(1)}, bf16[16,64,128]{2,1,0:T(8,128)(2,1)S(1)}, u32[]{:S(2)}, u32[]{:S(2)}) collective-permute-start(bf16[16,64,128]{2,1,0:T(8,128)(2,1)S(1)} %collective-permute-done.9), channel_id=1, source_target_pairs={{0,1},{1,2},{2,3},{3,4},{4,5},{5,6},{6,7},{7,8},{8,9},{9,10},{10,1... | collective-permute-start | bytes 786440 | tf_op jit(solution)/shard_map/ppermute | solution.py:25
  105.8 11.8 %collective-permute-start.11 = (bf16[16,64,128]{2,1,0:T(8,128)(2,1)S(1)}, bf16[16,64,128]{2,1,0:T(8,128)(2,1)S(1)}, u32[]{:S(2)}, u32[]{:S(2)}) collective-permute-start(bf16[16,64,128]{2,1,0:T(8,128)(2,1)S(1)} %collective-permute-done.10), channel_id=1, source_target_pairs={{0,1},{1,2},{2,3},{3,4},{4,5},{5,6},{6,7},{7,8},{8,9},{9,10},{10,1... | collective-permute-start | bytes 786440 | tf_op jit(solution)/shard_map/ppermute | solution.py:25
  117.6 12.0 %collective-permute-start.12 = (bf16[16,64,128]{2,1,0:T(8,128)(2,1)S(1)}, bf16[16,64,128]{2,1,0:T(8,128)(2,1)S(1)}, u32[]{:S(2)}, u32[]{:S(2)}) collective-permute-start(bf16[16,64,128]{2,1,0:T(8,128)(2,1)S(1)} %collective-permute-done.11), channel_id=1, source_target_pairs={{0,1},{1,2},{2,3},{3,4},{4,5},{5,6},{6,7},{7,8},{8,9},{9,10},{10,1... | collective-permute-start | bytes 786440 | tf_op jit(solution)/shard_map/ppermute | solution.py:25
  129.6 11.3 %collective-permute-start.13 = (bf16[16,64,128]{2,1,0:T(8,128)(2,1)S(1)}, bf16[16,64,128]{2,1,0:T(8,128)(2,1)S(1)}, u32[]{:S(2)}, u32[]{:S(2)}) collective-permute-start(bf16[16,64,128]{2,1,0:T(8,128)(2,1)S(1)} %collective-permute-done.12), channel_id=1, source_target_pairs={{0,1},{1,2},{2,3},{3,4},{4,5},{5,6},{6,7},{7,8},{8,9},{9,10},{10,1... | collective-permute-start | bytes 786440 | tf_op jit(solution)/shard_map/ppermute | solution.py:25
  130.4 42.6 %copy-start = (f32[1024,128]{1,0:T(8,128)S(1)}, f32[1024,128]{1,0:T(8,128)}, u32[]{:S(2)}) copy-start(f32[1024,128]{1,0:T(8,128)} %param.8) | copy-start | bytes 1572868
  140.9 10.4 %collective-permute-start.14 = (bf16[16,64,128]{2,1,0:T(8,128)(2,1)S(1)}, bf16[16,64,128]{2,1,0:T(8,128)(2,1)S(1)}, u32[]{:S(2)}, u32[]{:S(2)}) collective-permute-start(bf16[16,64,128]{2,1,0:T(8,128)(2,1)S(1)} %collective-permute-done.13), channel_id=1, source_target_pairs={{0,1},{1,2},{2,3},{3,4},{4,5},{5,6},{6,7},{7,8},{8,9},{9,10},{10,1... | collective-permute-start | bytes 786440 | tf_op jit(solution)/shard_map/ppermute | solution.py:25
  151.3 9.7 %collective-permute-start.15 = (bf16[16,64,128]{2,1,0:T(8,128)(2,1)S(1)}, bf16[16,64,128]{2,1,0:T(8,128)(2,1)S(1)}, u32[]{:S(2)}, u32[]{:S(2)}) collective-permute-start(bf16[16,64,128]{2,1,0:T(8,128)(2,1)S(1)} %collective-permute-done.14), channel_id=1, source_target_pairs={{0,1},{1,2},{2,3},{3,4},{4,5},{5,6},{6,7},{7,8},{8,9},{9,10},{10,1... | collective-permute-start | bytes 786440 | tf_op jit(solution)/shard_map/ppermute | solution.py:25
  161.0 11.2 %collective-permute-start.16 = (bf16[16,64,128]{2,1,0:T(8,128)(2,1)S(1)}, bf16[16,64,128]{2,1,0:T(8,128)(2,1)S(1)}, u32[]{:S(2)}, u32[]{:S(2)}) collective-permute-start(bf16[16,64,128]{2,1,0:T(8,128)(2,1)S(1)} %collective-permute-done.15), channel_id=1, source_target_pairs={{0,1},{1,2},{2,3},{3,4},{4,5},{5,6},{6,7},{7,8},{8,9},{9,10},{10,1... | collective-permute-start | bytes 786440 | tf_op jit(solution)/shard_map/ppermute | solution.py:25
  175.1 9.8 %collective-permute-start.19 = (bf16[16,64,128]{2,1,0:T(8,128)(2,1)S(1)}, bf16[16,64,128]{2,1,0:T(8,128)(2,1)S(1)}, u32[]{:S(2)}, u32[]{:S(2)}) collective-permute-start(bf16[16,64,128]{2,1,0:T(8,128)(2,1)S(1)} %get-tuple-element.27), channel_id=1, source_target_pairs={{0,1},{1,2},{2,3},{3,4},{4,5},{5,6},{6,7},{7,8},{8,9},{9,10},{10,1... | collective-permute-start | bytes 786440 | tf_op jit(solution)/shard_map/ppermute | solution.py:25
  175.9 6.1 %collective-permute-start.18 = (bf16[16,64,128]{2,1,0:T(8,128)(2,1)S(1)}, bf16[16,64,128]{2,1,0:T(8,128)(2,1)S(1)}, u32[]{:S(2)}, u32[]{:S(2)}) collective-permute-start(bf16[16,64,128]{2,1,0:T(8,128)(2,1)S(1)} %get-tuple-element.27), channel_id=1, source_target_pairs={{16,0},{32,16},{48,32},{64,48},{80,64},{96,80},{112,96},{128,112},... | collective-permute-start | bytes 786440 | tf_op jit(solution)/shard_map/ppermute | solution.py:17
  177.8 10.1 %collective-permute-start.17 = (bf16[16,64,128]{2,1,0:T(8,128)(2,1)S(1)}, bf16[16,64,128]{2,1,0:T(8,128)(2,1)S(1)}, u32[]{:S(2)}, u32[]{:S(2)}) collective-permute-start(bf16[16,64,128]{2,1,0:T(8,128)(2,1)S(1)} %get-tuple-element.27), channel_id=1, source_target_pairs={{0,16},{16,32},{32,48},{48,64},{64,80},{80,96},{96,112},{112,128},... | collective-permute-start | bytes 786440 | tf_op jit(solution)/shard_map/ppermute | solution.py:14
  185.7 11.1 %collective-permute-start.20 = (bf16[16,64,128]{2,1,0:T(8,128)(2,1)S(1)}, bf16[16,64,128]{2,1,0:T(8,128)(2,1)S(1)}, u32[]{:S(2)}, u32[]{:S(2)}) collective-permute-start(bf16[16,64,128]{2,1,0:T(8,128)(2,1)S(1)} %collective-permute-done.19), channel_id=1, source_target_pairs={{0,1},{1,2},{2,3},{3,4},{4,5},{5,6},{6,7},{7,8},{8,9},{9,10},{10,1... | collective-permute-start | bytes 786440 | tf_op jit(solution)/shard_map/ppermute | solution.py:25
  197.5 12.3 %collective-permute-start.21 = (bf16[16,64,128]{2,1,0:T(8,128)(2,1)S(1)}, bf16[16,64,128]{2,1,0:T(8,128)(2,1)S(1)}, u32[]{:S(2)}, u32[]{:S(2)}) collective-permute-start(bf16[16,64,128]{2,1,0:T(8,128)(2,1)S(1)} %collective-permute-done.20), channel_id=1, source_target_pairs={{0,1},{1,2},{2,3},{3,4},{4,5},{5,6},{6,7},{7,8},{8,9},{9,10},{10,1... | collective-permute-start | bytes 786440 | tf_op jit(solution)/shard_map/ppermute | solution.py:25
  210.6 11.7 %collective-permute-start.22 = (bf16[16,64,128]{2,1,0:T(8,128)(2,1)S(1)}, bf16[16,64,128]{2,1,0:T(8,128)(2,1)S(1)}, u32[]{:S(2)}, u32[]{:S(2)}) collective-permute-start(bf16[16,64,128]{2,1,0:T(8,128)(2,1)S(1)} %collective-permute-done.21), channel_id=1, source_target_pairs={{0,1},{1,2},{2,3},{3,4},{4,5},{5,6},{6,7},{7,8},{8,9},{9,10},{10,1... | collective-permute-start | bytes 786440 | tf_op jit(solution)/shard_map/ppermute | solution.py:25
  223.1 10.9 %collective-permute-start.23 = (bf16[16,64,128]{2,1,0:T(8,128)(2,1)S(1)}, bf16[16,64,128]{2,1,0:T(8,128)(2,1)S(1)}, u32[]{:S(2)}, u32[]{:S(2)}) collective-permute-start(bf16[16,64,128]{2,1,0:T(8,128)(2,1)S(1)} %collective-permute-done.22), channel_id=1, source_target_pairs={{0,1},{1,2},{2,3},{3,4},{4,5},{5,6},{6,7},{7,8},{8,9},{9,10},{10,1... | collective-permute-start | bytes 786440 | tf_op jit(solution)/shard_map/ppermute | solution.py:25
  234.7 10.0 %collective-permute-start.24 = (bf16[16,64,128]{2,1,0:T(8,128)(2,1)S(1)}, bf16[16,64,128]{2,1,0:T(8,128)(2,1)S(1)}, u32[]{:S(2)}, u32[]{:S(2)}) collective-permute-start(bf16[16,64,128]{2,1,0:T(8,128)(2,1)S(1)} %collective-permute-done.23), channel_id=1, source_target_pairs={{0,1},{1,2},{2,3},{3,4},{4,5},{5,6},{6,7},{7,8},{8,9},{9,10},{10,1... | collective-permute-start | bytes 786440 | tf_op jit(solution)/shard_map/ppermute | solution.py:25
  245.5 9.8 %collective-permute-start.25 = (bf16[16,64,128]{2,1,0:T(8,128)(2,1)S(1)}, bf16[16,64,128]{2,1,0:T(8,128)(2,1)S(1)}, u32[]{:S(2)}, u32[]{:S(2)}) collective-permute-start(bf16[16,64,128]{2,1,0:T(8,128)(2,1)S(1)} %collective-permute-done.24), channel_id=1, source_target_pairs={{0,1},{1,2},{2,3},{3,4},{4,5},{5,6},{6,7},{7,8},{8,9},{9,10},{10,1... | collective-permute-start | bytes 786440 | tf_op jit(solution)/shard_map/ppermute | solution.py:25
  256.0 9.8 %collective-permute-start.26 = (bf16[16,64,128]{2,1,0:T(8,128)(2,1)S(1)}, bf16[16,64,128]{2,1,0:T(8,128)(2,1)S(1)}, u32[]{:S(2)}, u32[]{:S(2)}) collective-permute-start(bf16[16,64,128]{2,1,0:T(8,128)(2,1)S(1)} %collective-permute-done.25), channel_id=1, source_target_pairs={{0,1},{1,2},{2,3},{3,4},{4,5},{5,6},{6,7},{7,8},{8,9},{9,10},{10,1... | collective-permute-start | bytes 786440 | tf_op jit(solution)/shard_map/ppermute | solution.py:25
  266.5 9.8 %collective-permute-start.27 = (bf16[16,64,128]{2,1,0:T(8,128)(2,1)S(1)}, bf16[16,64,128]{2,1,0:T(8,128)(2,1)S(1)}, u32[]{:S(2)}, u32[]{:S(2)}) collective-permute-start(bf16[16,64,128]{2,1,0:T(8,128)(2,1)S(1)} %collective-permute-done.26), channel_id=1, source_target_pairs={{0,1},{1,2},{2,3},{3,4},{4,5},{5,6},{6,7},{7,8},{8,9},{9,10},{10,1... | collective-permute-start | bytes 786440 | tf_op jit(solution)/shard_map/ppermute | solution.py:25
  277.0 10.3 %collective-permute-start.28 = (bf16[16,64,128]{2,1,0:T(8,128)(2,1)S(1)}, bf16[16,64,128]{2,1,0:T(8,128)(2,1)S(1)}, u32[]{:S(2)}, u32[]{:S(2)}) collective-permute-start(bf16[16,64,128]{2,1,0:T(8,128)(2,1)S(1)} %collective-permute-done.27), channel_id=1, source_target_pairs={{0,1},{1,2},{2,3},{3,4},{4,5},{5,6},{6,7},{7,8},{8,9},{9,10},{10,1... | collective-permute-start | bytes 786440 | tf_op jit(solution)/shard_map/ppermute | solution.py:25
  288.1 11.2 %collective-permute-start.29 = (bf16[16,64,128]{2,1,0:T(8,128)(2,1)S(1)}, bf16[16,64,128]{2,1,0:T(8,128)(2,1)S(1)}, u32[]{:S(2)}, u32[]{:S(2)}) collective-permute-start(bf16[16,64,128]{2,1,0:T(8,128)(2,1)S(1)} %collective-permute-done.28), channel_id=1, source_target_pairs={{0,1},{1,2},{2,3},{3,4},{4,5},{5,6},{6,7},{7,8},{8,9},{9,10},{10,1... | collective-permute-start | bytes 786440 | tf_op jit(solution)/shard_map/ppermute | solution.py:25
  300.1 12.4 %collective-permute-start.30 = (bf16[16,64,128]{2,1,0:T(8,128)(2,1)S(1)}, bf16[16,64,128]{2,1,0:T(8,128)(2,1)S(1)}, u32[]{:S(2)}, u32[]{:S(2)}) collective-permute-start(bf16[16,64,128]{2,1,0:T(8,128)(2,1)S(1)} %collective-permute-done.29), channel_id=1, source_target_pairs={{0,1},{1,2},{2,3},{3,4},{4,5},{5,6},{6,7},{7,8},{8,9},{9,10},{10,1... | collective-permute-start | bytes 786440 | tf_op jit(solution)/shard_map/ppermute | solution.py:25
  300.2 47.7 %copy-start.1 = (f32[16,64,128]{2,1,0:T(8,128)S(1)}, f32[16,64,128]{2,1,0:T(8,128)}, u32[]{:S(2)}) copy-start(f32[16,64,128]{2,1,0:T(8,128)} %get-tuple-element.28) | copy-start | bytes 1572868
  313.2 11.7 %collective-permute-start.31 = (bf16[16,64,128]{2,1,0:T(8,128)(2,1)S(1)}, bf16[16,64,128]{2,1,0:T(8,128)(2,1)S(1)}, u32[]{:S(2)}, u32[]{:S(2)}) collective-permute-start(bf16[16,64,128]{2,1,0:T(8,128)(2,1)S(1)} %collective-permute-done.30), channel_id=1, source_target_pairs={{0,1},{1,2},{2,3},{3,4},{4,5},{5,6},{6,7},{7,8},{8,9},{9,10},{10,1... | collective-permute-start | bytes 786440 | tf_op jit(solution)/shard_map/ppermute | solution.py:25
  325.7 10.9 %collective-permute-start.32 = (bf16[16,64,128]{2,1,0:T(8,128)(2,1)S(1)}, bf16[16,64,128]{2,1,0:T(8,128)(2,1)S(1)}, u32[]{:S(2)}, u32[]{:S(2)}) collective-permute-start(bf16[16,64,128]{2,1,0:T(8,128)(2,1)S(1)} %collective-permute-done.31), channel_id=1, source_target_pairs={{0,1},{1,2},{2,3},{3,4},{4,5},{5,6},{6,7},{7,8},{8,9},{9,10},{10,1... | collective-permute-start | bytes 786440 | tf_op jit(solution)/shard_map/ppermute | solution.py:25
  337.3 9.8 %collective-permute-start.33 = (bf16[16,64,128]{2,1,0:T(8,128)(2,1)S(1)}, bf16[16,64,128]{2,1,0:T(8,128)(2,1)S(1)}, u32[]{:S(2)}, u32[]{:S(2)}) collective-permute-start(bf16[16,64,128]{2,1,0:T(8,128)(2,1)S(1)} %collective-permute-done.32), channel_id=1, source_target_pairs={{0,1},{1,2},{2,3},{3,4},{4,5},{5,6},{6,7},{7,8},{8,9},{9,10},{10,1... | collective-permute-start | bytes 786440 | tf_op jit(solution)/shard_map/ppermute | solution.py:25
  363.4 4.2 collective-permute-start.34
  381.0 5.5 %collective-permute-start.35 = (bf16[128,128]{1,0:T(8,128)(2,1)S(1)}, bf16[128,128]{1,0:T(8,128)(2,1)S(1)}, u32[]{:S(2)}, u32[]{:S(2)}) collective-permute-start(bf16[128,128]{1,0:T(8,128)(2,1)S(1)} %fusion.117), channel_id=1, source_target_pairs={{0,2},{2,0},{1,3},{3,1},{4,6},{6,4},{5,7},{7,5},{8,10},{10,8},{9,1... | collective-permute-start | bytes 98312 | tf_op jit(solution)/shard_map/ppermute | solution.py:35
  399.8 4.4 collective-permute-start.36
  417.5 5.5 %collective-permute-start.37 = (bf16[128,128]{1,0:T(8,128)(2,1)S(1)}, bf16[128,128]{1,0:T(8,128)(2,1)S(1)}, u32[]{:S(2)}, u32[]{:S(2)}) collective-permute-start(bf16[128,128]{1,0:T(8,128)(2,1)S(1)} %fusion.121), channel_id=1, source_target_pairs={{0,8},{8,0},{1,9},{9,1},{2,10},{10,2},{3,11},{11,3},{4,12},{12,4},... | collective-permute-start | bytes 98312 | tf_op jit(solution)/shard_map/ppermute | solution.py:35
  436.4 1.5 collective-permute-start.38
  451.3 4.4 collective-permute-start.39
  469.1 5.5 %collective-permute-start.40 = (f32[128,128]{1,0:T(8,128)S(1)}, f32[128,128]{1,0:T(8,128)S(1)}, u32[]{:S(2)}, u32[]{:S(2)}) collective-permute-start(f32[128,128]{1,0:T(8,128)S(1)} %select_select_fusion.2), channel_id=1, source_target_pairs={{0,64},{64,0},{16,80},{80,16},{32,96},{96,32},{48,112},{112,48},{1... | collective-permute-start | bytes 196616 | tf_op jit(solution)/shard_map/ppermute | solution.py:35
  488.0 8.3 %collective-permute-start.41 = (f32[128,128]{1,0:T(8,128)S(1)}, f32[128,128]{1,0:T(8,128)S(1)}, u32[]{:S(2)}, u32[]{:S(2)}) collective-permute-start(f32[128,128]{1,0:T(8,128)S(1)} %select_select_fusion.1), channel_id=1, source_target_pairs={{0,128},{128,0},{16,144},{144,16},{32,160},{160,32},{48,176},{176,... | collective-permute-start | bytes 196616 | tf_op jit(solution)/shard_map/ppermute | solution.py:35
where the time goes:
time: 532 us; the launch traced here: 522 us
  waiting for transfers between devices  267 us (50%)
  other arithmetic  129 us (24%)
  matrix products  65.6 us (12%)
  local copies, waits for them, and re-layouts  36.1 us (7%)
  starting transfers between devices  21.8 us (4%)
    ppermute x30, waiting for transfers between devices, shifted(): return lax.ppermute(value, axis, pairs)  241 us
    another operation x24, other arithmetic, on_device(): jnp.linalg.cholesky(jnp.dot(lower, lower.T, precision=precise) + jnp.dot(...  99.1 us
    dot_general x36, matrix products, couple_source(): jnp.einsum('rik,rkn->rin', coupling, picked, preferred_element_type=jnp.f...  57 us
    gather x36, local copies, waits for them, and re-layouts, couple_source(): piece[columns]  26.9 us
    ppermute x8, waiting for transfers between devices, from_partner(): return lax.ppermute(block, axis, route)  26.3 us
    another operation x3, other arithmetic, on_device(): lower = jnp.linalg.cholesky(local_gram)  12.4 us
  transfers between devices with their start and end apart: 42, of which 36 were waited for; matrix products, arithmetic and copies ran while one was open for 16% of the time, Pallas kernels for 0%

commit v1 on v0

v1 whole, which is shorter than its diff:
```python
import jax
import jax.numpy as jnp
from jax import lax
from jax.sharding import PartitionSpec as P

precise = lax.Precision.HIGHEST


def neighbours(block):
    count = lax.axis_size("group")
    forward = [(i, i + 1) for i in range(count - 1)]
    backward = [(i + 1, i) for i in range(count - 1)]
    below = lax.ppermute(block, "group", forward)
    above = lax.ppermute(block, "group", backward)
    return below, above


def couple_all(hamiltonian, block_columns, rounded):
    shard_blocks, nsrc, block_size, width = hamiltonian.shape
    per_source = block_columns.shape[2]
    states = rounded.shape[2]
    gathered = lax.all_gather(rounded, "blk", axis=0, tiled=True)
    below, above = neighbours(rounded)
    table = jnp.concatenate([gathered, below, above], axis=0)
    offsets = (jnp.arange(nsrc, dtype=jnp.int32) * shard_blocks)[None, :, None]
    index = block_columns + offsets
    picked = table[index.reshape(-1)].reshape(shard_blocks, nsrc, per_source * block_size, states)
    return jnp.einsum(
        "rsik,rskn->rin", hamiltonian, picked, preferred_element_type=jnp.float32
    )


def on_device(hamiltonian, block_columns, potential, trial_slab):
    shard_blocks = hamiltonian.shape[0]
    block_size = hamiltonian.shape[2]
    states = trial_slab.shape[1]
    start_slab = trial_slab.reshape(shard_blocks, block_size, states)
    weights = potential.reshape(shard_blocks, block_size, 1)
    coupled_start = couple_all(hamiltonian, block_columns, start_slab.astype(jnp.bfloat16))
    filtered_once = 0.5 * (coupled_start + weights * start_slab)
    coupled_next = couple_all(hamiltonian, block_columns, filtered_once.astype(jnp.bfloat16))
    filtered = coupled_next + weights * filtered_once - start_slab
    flat = filtered.reshape(shard_blocks * block_size, states)
    rows_total = flat.shape[0] * lax.axis_size("group") * lax.axis_size("blk")
    local_gram = jnp.dot(flat.T, flat, precision=precise)
    gram = lax.psum(local_gram, ("group", "blk")) / rows_total
    lower = jnp.linalg.cholesky(gram)
    ortho_slab = lax.linalg.triangular_solve(
        lower, flat, left_side=False, lower=True, transpose_a=True
    )
    return (ortho_slab, jnp.transpose(lower))


def solution(mesh):
    placed = (
        P(("group", "blk"), None, None, None),
        P(("group", "blk"), None, None),
        P(("group", "blk")),
        P(("group", "blk"), None),
    )
    return jax.shard_map(
        on_device,
        mesh=mesh,
        in_specs=placed,
        out_specs=(P(("group", "blk"), None), P()),
        check_vma=False,
    )
```

time: 532 us -> 494 us (0.929)
  the two profiles are of different devices: /device:TPU:32 before, /device:TPU:1 now
where the time goes in v1:
time: 494 us
  waiting for transfers between devices  342 us (69%)
  local copies, waits for them, and re-layouts  60.2 us (12%)
  other arithmetic  35.5 us (7%)
  matrix products  29.3 us (6%)
  between operations  13.9 us (3%)
  starting transfers between devices  13 us (3%)
    psum x1, waiting for transfers between devices, on_device(): gram = lax.psum(local_gram, ('group', 'blk')) / rows_total  238 us
    all_gather x2, waiting for transfers between devices, couple_all(): gathered = lax.all_gather(rounded, 'blk', axis=0, tiled=True)  98.7 us
    gather x2, local copies, waits for them, and re-layouts, couple_all(): table[index.reshape(-1)]  58.3 us
    dot_general x2, matrix products, couple_all(): jnp.einsum('rsik,rskn->rin', hamiltonian, picked, preferred_element_type=...  26.3 us
    another operation x3, other arithmetic, on_device(): lower = jnp.linalg.cholesky(gram)  12.4 us
  transfers between devices with their start and end apart: 7, of which 7 were waited for; matrix products, arithmetic and copies ran while one was open for 0% of the time, Pallas kernels for 0%

profile of v1, /device:TPU:1, one launch (start us, length us, event | category | flops | bytes accessed | tf_op | source)
XLA Modules:
  0.0 493.7 jit_solution(8105677238921476546)
XLA Ops:
  7.2 0.0 all-gather.3.cloned.1.call-start
  7.2 1.8 convert_element_type.6
  9.0 0.0 all-gather.3.cloned.1.call-update
  9.0 0.0 all-gather.5.cloned.1.call-start
  9.1 5.1 %collective-permute-start.1 = (bf16[16,64,128]{2,1,0:T(8,128)(2,1)}, bf16[16,64,128]{2,1,0:T(8,128)(2,1)S(1)}, u32[]{:S(2)}, u32[]{:S(2)}) collective-permute-start(bf16[16,64,128]{2,1,0:T(8,128)(2,1)} %convert_element_type.6), channel_id=1, source_target_pairs={{16,0},{32,16},{48,32},{64,48},{80,64},{96,80},{112,96},{128,112},... | collective-permute-start | bytes 786440 | tf_op jit(solution)/shard_map/ppermute | solution.py:14
  14.2 1.9 collective-permute-start
  16.2 0.8 broadcast_add_fusion
  16.9 0.8 mul.37
  17.7 0.2 copy.13
  17.9 0.1 reshape.64
  18.1 0.2 collective-permute-done.1
  18.3 1.5 collective-permute-done
  19.8 51.6 %all-gather.3.cloned.1.call-done = bf16[256,64,128]{2,1,0:T(8,128)(2,1)} async-done(((bf16[16,64,128]{2,1,0:T(8,128)(2,1)}), bf16[256,64,128]{2,1,0:T(8,128)(2,1)}) %all-gather.3.cloned.1.call-update) | async-done | bytes 4194320 | tf_op jit(solution)/shard_map/all_gather | solution.py:22
  71.4 4.2 pad_maximum_fusion
  75.5 0.0 copy-start
  75.5 29.1 %gather_fusion = bf16[1152,64,128]{2,1,0:T(8,128)(2,1)} fusion(bf16[288,64,128]{2,1,0:T(8,128)(2,1)} %pad_maximum_fusion, s32[2048]{0:T(1024)S(1)} %pad_clamp_fusion), kind=kCustom, calls=%fused_computation | custom fusion | bytes 37753344 | tf_op jit(solution)/shard_map/gather | solution.py:27
  104.6 0.0 copy-done
  104.6 13.5 %multiply_convert_fusion = (bf16[16,64,128]{2,1,0:T(8,128)(2,1)}, f32[16,64,128]{2,1,0:T(8,128)S(1)}) fusion(f32[16,64,128]{2,1,0:T(8,128)S(1)} %bitcast.44, f32[16,64]{1,0:T(8,128)S(1)} %mul.37, bf16[16,18,64,256]{3,2,1,0:T(8,128)(2,1)} %param.4, bf16[16,18,256,128]{3,2,1,0:T(8,128)(2,1)} %bitcast.41), kind=kOutput, calls=%fused_computation.10 | convolution fusion | flops 1208483840 | bytes 29626368 | tf_op jit(solution)/shard_map/rsik,rskn->rin/dot_general | solution.py:28
  118.2 0.0 all-gather.5.cloned.1.call-update
  118.2 0.0 all-reduce.2.cloned.1.call-start
  118.2 2.6 collective-permute-start.3
  120.8 3.3 collective-permute-start.2
  124.1 2.1 collective-permute-done.3
  126.2 1.3 collective-permute-done.2
  127.5 47.1 %all-gather.5.cloned.1.call-done = bf16[256,64,128]{2,1,0:T(8,128)(2,1)} async-done(((bf16[16,64,128]{2,1,0:T(8,128)(2,1)}), bf16[256,64,128]{2,1,0:T(8,128)(2,1)}) %all-gather.5.cloned.1.call-update) | async-done | bytes 4194320 | tf_op jit(solution)/shard_map/all_gather | solution.py:22
  174.6 4.2 pad_maximum_fusion.1
  178.8 29.2 %gather_fusion.1 = bf16[1152,64,128]{2,1,0:T(8,128)(2,1)} fusion(bf16[288,64,128]{2,1,0:T(8,128)(2,1)} %pad_maximum_fusion.1, s32[2048]{0:T(1024)S(1)} %pad_clamp_fusion), kind=kCustom, calls=%fused_computation.1 | custom fusion | bytes 37753344 | tf_op jit(solution)/shard_map/gather | solution.py:27
  208.0 12.8 %fusion.2 = f32[16,64,128]{2,1,0:T(8,128)S(1)} fusion(f32[16,64,128]{2,1,0:T(8,128)S(1)} %bitcast.45, bf16[16,18,64,256]{3,2,1,0:T(8,128)(2,1)} %param.4, bf16[16,18,256,128]{3,2,1,0:T(8,128)(2,1)} %bitcast.40, f32[16,64,128]{2,1,0:T(8,128)S(1)} %get-tuple-element.11, f32[16,64]{1,0:T(8,128)S(1)} %broadcast_multiply_fusion.1), kind=kOutput, calls=%fused_computation.8 | convolution fusion | flops 1208352768 | bytes 29888512 | tf_op jit(solution)/shard_map/rsik,rskn->rin/dot_general | solution.py:28
  220.8 1.6 convolution_bitcast_fusion.2
  222.5 0.0 all-reduce.2.cloned.1.call-update
  222.5 237.9 %all-reduce.2.cloned.1.call-done = f32[128,128]{0,1:T(8,128)} async-done(((f32[128,128]{0,1:T(8,128)}), f32[128,128]{0,1:T(8,128)}) %all-reduce.2.cloned.1.call-update) | async-done | bytes 65552 | tf_op jit(solution)/shard_map/psum | solution.py:46
  460.4 0.8 broadcast_multiply_fusion
  461.3 0.1 copy.15
  461.4 0.9 fusion.5
  462.2 11.7 %cholesky.16 = f32[128,128]{1,0:T(8,128)S(1)} custom-call(f32[128,128]{1,0:T(8,128)S(1)} %fusion.5), custom_call_target="Cholesky" | custom-call | tf_op jit(solution)/shard_map/jit(cholesky)/cholesky | solution.py:47
  474.0 0.6 compare_reduce_fusion
  474.6 0.7 fusion.6
  475.3 0.7 copy.16
  476.0 9.8 %custom-call.6 = f32[1,128,128]{1,2,0:T(8,128)S(1)} custom-call(f32[1,128,128]{2,1,0:T(8,128)S(1)} %get-tuple-element.9), custom_call_target="InvertDiagBlocksLowerTriangular" | custom-call | tf_op jit(solution)/shard_map/triangular_solve | solution.py:48
  485.8 1.4 fusion.3
  (5 shorter events, 0.1 us)
Async XLA Ops:
  7.2 64.2 %all-gather.3.cloned.1.call-start = ((), (), s32[]{:S(2)}) async-start(), calls=%async_computation | async-start | bytes 4456448 | tf_op jit(solution)/shard_map/all_gather | solution.py:22
  9.0 165.6 %all-gather.5.cloned.1.call-start = ((), (), s32[]{:S(2)}) async-start(), calls=%async_computation.1 | async-start | bytes 4456448 | tf_op jit(solution)/shard_map/all_gather | solution.py:22
  9.1 9.2 %collective-permute-start.1 = (bf16[16,64,128]{2,1,0:T(8,128)(2,1)}, bf16[16,64,128]{2,1,0:T(8,128)(2,1)S(1)}, u32[]{:S(2)}, u32[]{:S(2)}) collective-permute-start(bf16[16,64,128]{2,1,0:T(8,128)(2,1)} %convert_element_type.6), channel_id=1, source_target_pairs={{16,0},{32,16},{48,32},{64,48},{80,64},{96,80},{112,96},{128,112},... | collective-permute-start | bytes 786440 | tf_op jit(solution)/shard_map/ppermute | solution.py:14
  14.2 5.5 %collective-permute-start = (bf16[16,64,128]{2,1,0:T(8,128)(2,1)}, bf16[16,64,128]{2,1,0:T(8,128)(2,1)S(1)}, u32[]{:S(2)}, u32[]{:S(2)}) collective-permute-start(bf16[16,64,128]{2,1,0:T(8,128)(2,1)} %convert_element_type.6), channel_id=1, source_target_pairs={{0,16},{16,32},{32,48},{48,64},{64,80},{80,96},{96,112},{112,128},... | collective-permute-start | bytes 786440 | tf_op jit(solution)/shard_map/ppermute | solution.py:13
  75.5 29.1 %copy-start = (f32[1024,128]{1,0:T(8,128)S(1)}, f32[1024,128]{1,0:T(8,128)}, u32[]{:S(2)}) copy-start(f32[1024,128]{1,0:T(8,128)} %param.7) | copy-start | bytes 1572868
  118.2 342.3 %all-reduce.2.cloned.1.call-start = ((), (), s32[]{:S(2)}) async-start(), calls=%async_computation.2 | async-start | bytes 131072 | tf_op jit(solution)/shard_map/psum | solution.py:46
  118.2 8.0 %collective-permute-start.3 = (bf16[16,64,128]{2,1,0:T(8,128)(2,1)}, bf16[16,64,128]{2,1,0:T(8,128)(2,1)S(1)}, u32[]{:S(2)}, u32[]{:S(2)}) collective-permute-start(bf16[16,64,128]{2,1,0:T(8,128)(2,1)} %get-tuple-element.10), channel_id=1, source_target_pairs={{16,0},{32,16},{48,32},{64,48},{80,64},{96,80},{112,96},{128,112},... | collective-permute-start | bytes 786440 | tf_op jit(solution)/shard_map/ppermute | solution.py:14
  120.8 6.7 %collective-permute-start.2 = (bf16[16,64,128]{2,1,0:T(8,128)(2,1)}, bf16[16,64,128]{2,1,0:T(8,128)(2,1)S(1)}, u32[]{:S(2)}, u32[]{:S(2)}) collective-permute-start(bf16[16,64,128]{2,1,0:T(8,128)(2,1)} %get-tuple-element.10), channel_id=1, source_target_pairs={{0,16},{16,32},{32,48},{48,64},{64,80},{80,96},{96,112},{112,128},... | collective-permute-start | bytes 786440 | tf_op jit(solution)/shard_map/ppermute | solution.py:13
Sparse Core Ops, SparseCore 0:
  11.0 60.3 all-gather.2
  118.3 56.2 all-gather.4
  222.6 237.7 all-reduce.1

commit v2 on v1

--- a/solution.py
+++ b/solution.py
@@ -13,6 +13,23 @@
     below = lax.ppermute(block, "group", forward)
     above = lax.ppermute(block, "group", backward)
     return below, above
+
+
+def from_partner(block, axis, bit):
+    count = lax.axis_size(axis)
+    route = []
+    for low in range(count):
+        high = low | 1 << bit
+        if high != low and high < count:
+            route += [(low, high), (high, low)]
+    return lax.ppermute(block, axis, route)
+
+
+def summed_over_mesh(value):
+    for axis in ("blk", "group"):
+        for bit in range(lax.axis_size(axis).bit_length() - 1):
+            value = value + from_partner(value, axis, bit)
+    return value
 
 
 def couple_all(hamiltonian, block_columns, rounded):
@@ -43,7 +60,7 @@
     flat = filtered.reshape(shard_blocks * block_size, states)
     rows_total = flat.shape[0] * lax.axis_size("group") * lax.axis_size("blk")
     local_gram = jnp.dot(flat.T, flat, precision=precise)
-    gram = lax.psum(local_gram, ("group", "blk")) / rows_total
+    gram = summed_over_mesh(local_gram) / rows_total
     lower = jnp.linalg.cholesky(gram)
     ortho_slab = lax.linalg.triangular_solve(
         lower, flat, left_side=False, lower=True, transpose_a=True

time: 494 us -> 295 us (0.60)
  waiting for transfers between devices: 342 us -> 118 us
  starting transfers between devices: 13 us -> 36.6 us
    psum x1 -> x0, waiting for transfers between devices: 238 us -> none  [on_device(): gram = lax.psum(local_gram, ('group', 'blk')) / rows_total]
    ppermute x0 -> x8, starting transfers between devices: none -> 23.6 us  [from_partner(): return lax.ppermute(block, axis, route)]
    ppermute x0 -> x8, waiting for transfers between devices: none -> 14 us  [from_partner(): return lax.ppermute(block, axis, route)]
  transfers between devices with their start and end apart: 7 -> 14, of which waited for: 7 -> 14; matrix products, arithmetic and copies ran while one was open for 0% -> 1% of each run, Pallas kernels for 0% -> 0%
where the time goes in v2:
time: 295 us; the launch traced here: 291 us
  waiting for transfers between devices  118 us (40%)
  local copies, waits for them, and re-layouts  60 us (20%)
  starting transfers between devices  36.6 us (12%)
  other arithmetic  33.8 us (11%)
  matrix products  28.7 us (10%)
  between operations  14.2 us (5%)
    all_gather x2, waiting for transfers between devices, couple_all(): gathered = lax.all_gather(rounded, 'blk', axis=0, tiled=True)  98.8 us
    gather x2, local copies, waits for them, and re-layouts, couple_all(): table[index.reshape(-1)]  58.1 us
    dot_general x2, matrix products, couple_all(): jnp.einsum('rsik,rskn->rin', hamiltonian, picked, preferred_element_type=...  26.3 us
    ppermute x8, starting transfers between devices, from_partner(): return lax.ppermute(block, axis, route)  23.6 us
    ppermute x8, waiting for transfers between devices, from_partner(): return lax.ppermute(block, axis, route)  14 us
    another operation x3, other arithmetic, on_device(): lower = jnp.linalg.cholesky(gram)  12.4 us
    another operation x1, other arithmetic, on_device(): lax.linalg.triangular_solve(lower, flat, left_side=False, lower=True, tra...  9.81 us
    concatenate x2, other arithmetic, couple_all(): table = jnp.concatenate([gathered, below, above], axis=0)  8.25 us
  transfers between devices with their start and end apart: 14, of which 14 were waited for; matrix products, arithmetic and copies ran while one was open for 1% of the time, Pallas kernels for 0%

profile of v2, /device:TPU:1, one launch (start us, length us, event | category | flops | bytes accessed | tf_op | source)
XLA Modules:
  0.0 291.2 jit_solution(2760195185760826905)
XLA Ops:
  7.2 0.0 all-gather.3.cloned.1.call-start
  7.2 1.8 convert_element_type.6
  9.0 0.0 all-gather.3.cloned.1.call-update
  9.0 0.0 all-gather.5.cloned.1.call-start
  9.1 5.1 %collective-permute-start.1 = (bf16[16,64,128]{2,1,0:T(8,128)(2,1)}, bf16[16,64,128]{2,1,0:T(8,128)(2,1)S(1)}, u32[]{:S(2)}, u32[]{:S(2)}) collective-permute-start(bf16[16,64,128]{2,1,0:T(8,128)(2,1)} %convert_element_type.6), channel_id=1, source_target_pairs={{16,0},{32,16},{48,32},{64,48},{80,64},{96,80},{112,96},{128,112},... | collective-permute-start | bytes 786440 | tf_op jit(solution)/shard_map/ppermute | solution.py:14
  14.2 1.9 collective-permute-start
  16.2 0.8 broadcast_add_fusion
  16.9 0.8 mul.37
  17.7 0.2 copy.15
  17.9 0.1 reshape.64
  18.1 0.2 collective-permute-done.1
  18.3 1.5 collective-permute-done
  19.8 51.6 %all-gather.3.cloned.1.call-done = bf16[256,64,128]{2,1,0:T(8,128)(2,1)} async-done(((bf16[16,64,128]{2,1,0:T(8,128)(2,1)}), bf16[256,64,128]{2,1,0:T(8,128)(2,1)}) %all-gather.3.cloned.1.call-update) | async-done | bytes 4194320 | tf_op jit(solution)/shard_map/all_gather | solution.py:39
  71.4 4.1 %pad_maximum_fusion = bf16[288,64,128]{2,1,0:T(8,128)(2,1)} fusion(bf16[16,64,128]{2,1,0:T(8,128)(2,1)S(1)} %collective-permute-done.1, bf16[16,64,128]{2,1,0:T(8,128)(2,1)S(1)} %collective-permute-done, bf16[256,64,128]{2,1,0:T(8,128)(2,1)} %all-gather.3.cloned.1.call-done), kind=kLoop, calls=%fused_computation.2 | loop fusion | flops 4718592 | bytes 9437184 | tf_op jit(solution)/shard_map/concatenate | solution.py:41
  75.5 0.0 copy-start
  75.5 29.1 %gather_fusion = bf16[1152,64,128]{2,1,0:T(8,128)(2,1)} fusion(bf16[288,64,128]{2,1,0:T(8,128)(2,1)} %pad_maximum_fusion, s32[2048]{0:T(1024)S(1)} %pad_clamp_fusion), kind=kCustom, calls=%fused_computation | custom fusion | bytes 37753344 | tf_op jit(solution)/shard_map/gather | solution.py:44
  104.6 0.0 copy-done
  104.6 13.5 %multiply_convert_fusion = (bf16[16,64,128]{2,1,0:T(8,128)(2,1)}, f32[16,64,128]{2,1,0:T(8,128)S(1)}) fusion(f32[16,64,128]{2,1,0:T(8,128)S(1)} %bitcast.46, f32[16,64]{1,0:T(8,128)S(1)} %mul.37, bf16[16,18,64,256]{3,2,1,0:T(8,128)(2,1)} %param.4, bf16[16,18,256,128]{3,2,1,0:T(8,128)(2,1)} %bitcast.43), kind=kOutput, calls=%fused_computation.10 | convolution fusion | flops 1208483840 | bytes 29626368 | tf_op jit(solution)/shard_map/rsik,rskn->rin/dot_general | solution.py:45
  118.1 0.0 all-gather.5.cloned.1.call-update
  118.1 2.6 collective-permute-start.3
  120.7 3.3 %collective-permute-start.2 = (bf16[16,64,128]{2,1,0:T(8,128)(2,1)}, bf16[16,64,128]{2,1,0:T(8,128)(2,1)S(1)}, u32[]{:S(2)}, u32[]{:S(2)}) collective-permute-start(bf16[16,64,128]{2,1,0:T(8,128)(2,1)} %get-tuple-element.10), channel_id=1, source_target_pairs={{0,16},{16,32},{32,48},{48,64},{64,80},{80,96},{96,112},{112,128},... | collective-permute-start | bytes 786440 | tf_op jit(solution)/shard_map/ppermute | solution.py:13
  124.0 2.1 collective-permute-done.3
  126.2 1.3 collective-permute-done.2
  127.4 47.2 %all-gather.5.cloned.1.call-done = bf16[256,64,128]{2,1,0:T(8,128)(2,1)} async-done(((bf16[16,64,128]{2,1,0:T(8,128)(2,1)}), bf16[256,64,128]{2,1,0:T(8,128)(2,1)}) %all-gather.5.cloned.1.call-update) | async-done | bytes 4194320 | tf_op jit(solution)/shard_map/all_gather | solution.py:39
  174.6 4.1 %pad_maximum_fusion.1 = bf16[288,64,128]{2,1,0:T(8,128)(2,1)} fusion(bf16[16,64,128]{2,1,0:T(8,128)(2,1)S(1)} %collective-permute-done.3, bf16[16,64,128]{2,1,0:T(8,128)(2,1)S(1)} %collective-permute-done.2, bf16[256,64,128]{2,1,0:T(8,128)(2,1)} %all-gather.5.cloned.1.call-done), kind=kLoop, calls=%fused_computation.3 | loop fusion | flops 4718592 | bytes 9437184 | tf_op jit(solution)/shard_map/concatenate | solution.py:41
  178.7 29.0 %gather_fusion.1 = bf16[1152,64,128]{2,1,0:T(8,128)(2,1)} fusion(bf16[288,64,128]{2,1,0:T(8,128)(2,1)} %pad_maximum_fusion.1, s32[2048]{0:T(1024)S(1)} %pad_clamp_fusion), kind=kCustom, calls=%fused_computation.1 | custom fusion | bytes 37753344 | tf_op jit(solution)/shard_map/gather | solution.py:44
  207.7 12.8 %fusion.2 = f32[16,64,128]{2,1,0:T(8,128)S(1)} fusion(f32[16,64,128]{2,1,0:T(8,128)S(1)} %bitcast.47, bf16[16,18,64,256]{3,2,1,0:T(8,128)(2,1)} %param.4, bf16[16,18,256,128]{3,2,1,0:T(8,128)(2,1)} %bitcast.42, f32[16,64,128]{2,1,0:T(8,128)S(1)} %get-tuple-element.11, f32[16,64]{1,0:T(8,128)S(1)} %broadcast_multiply_fusion), kind=kOutput, calls=%fused_computation.8 | convolution fusion | flops 1208352768 | bytes 29888512 | tf_op jit(solution)/shard_map/rsik,rskn->rin/dot_general | solution.py:45
  220.6 1.0 convolution_bitcast_fusion.2
  221.6 1.3 collective-permute-start.4
  222.8 1.9 collective-permute-done.4
  224.8 3.0 %collective-permute-start.5 = (f32[128,128]{0,1:T(8,128)S(1)}, f32[128,128]{0,1:T(8,128)S(1)}, u32[]{:S(2)}, u32[]{:S(2)}) collective-permute-start(f32[128,128]{0,1:T(8,128)S(1)} %add.69), channel_id=1, source_target_pairs={{0,2},{2,0},{1,3},{3,1},{4,6},{6,4},{5,7},{7,5},{8,10},{10,8},{9,1... | collective-permute-start | bytes 196616 | tf_op jit(solution)/shard_map/ppermute | solution.py:25
  227.8 1.9 collective-permute-done.5
  229.7 1.2 collective-permute-start.6
  231.0 2.0 collective-permute-done.6
  232.9 2.8 collective-permute-start.7
  235.7 1.9 collective-permute-done.7
  237.7 5.4 %collective-permute-start.8 = (f32[128,128]{0,1:T(8,128)S(1)}, f32[128,128]{0,1:T(8,128)S(1)}, u32[]{:S(2)}, u32[]{:S(2)}) collective-permute-start(f32[128,128]{0,1:T(8,128)S(1)} %add.72), channel_id=1, source_target_pairs={{0,16},{16,0},{32,48},{48,32},{64,80},{80,64},{96,112},{112,96},{1... | collective-permute-start | bytes 196616 | tf_op jit(solution)/shard_map/ppermute | solution.py:25
  243.0 0.9 collective-permute-done.8
  243.9 1.4 collective-permute-start.9
  245.3 1.8 collective-permute-done.9
  247.2 2.4 collective-permute-start.10
  249.5 1.7 collective-permute-done.10
  251.3 6.2 %collective-permute-start.11 = (f32[128,128]{0,1:T(8,128)S(1)}, f32[128,128]{0,1:T(8,128)S(1)}, u32[]{:S(2)}, u32[]{:S(2)}) collective-permute-start(f32[128,128]{0,1:T(8,128)S(1)} %add.75), channel_id=1, source_target_pairs={{0,128},{128,0},{16,144},{144,16},{32,160},{160,32},{48,176},{176,... | collective-permute-start | bytes 196616 | tf_op jit(solution)/shard_map/ppermute | solution.py:25
  257.5 1.8 collective-permute-done.11
  259.3 0.1 copy.18
  259.4 11.7 %cholesky.16 = f32[128,128]{1,0:T(8,128)S(1)} custom-call(f32[128,128]{1,0:T(8,128)S(1)} %fusion.5), custom_call_target="Cholesky" | custom-call | tf_op jit(solution)/shard_map/jit(cholesky)/cholesky | solution.py:64
  271.2 0.6 compare_reduce_fusion
  271.8 0.7 fusion.6
  272.5 0.7 copy.19
  273.2 9.8 %custom-call.6 = f32[1,128,128]{1,2,0:T(8,128)S(1)} custom-call(f32[1,128,128]{2,1,0:T(8,128)S(1)} %get-tuple-element.9), custom_call_target="InvertDiagBlocksLowerTriangular" | custom-call | tf_op jit(solution)/shard_map/triangular_solve | solution.py:65
  283.0 1.4 fusion.3
  (14 shorter events, 0.2 us)
Async XLA Ops:
  7.2 64.2 %all-gather.3.cloned.1.call-start = ((), (), s32[]{:S(2)}) async-start(), calls=%async_computation | async-start | bytes 4456448 | tf_op jit(solution)/shard_map/all_gather | solution.py:39
  9.0 165.6 %all-gather.5.cloned.1.call-start = ((), (), s32[]{:S(2)}) async-start(), calls=%async_computation.1 | async-start | bytes 4456448 | tf_op jit(solution)/shard_map/all_gather | solution.py:39
  9.1 9.2 %collective-permute-start.1 = (bf16[16,64,128]{2,1,0:T(8,128)(2,1)}, bf16[16,64,128]{2,1,0:T(8,128)(2,1)S(1)}, u32[]{:S(2)}, u32[]{:S(2)}) collective-permute-start(bf16[16,64,128]{2,1,0:T(8,128)(2,1)} %convert_element_type.6), channel_id=1, source_target_pairs={{16,0},{32,16},{48,32},{64,48},{80,64},{96,80},{112,96},{128,112},... | collective-permute-start | bytes 786440 | tf_op jit(solution)/shard_map/ppermute | solution.py:14
  14.2 5.5 %collective-permute-start = (bf16[16,64,128]{2,1,0:T(8,128)(2,1)}, bf16[16,64,128]{2,1,0:T(8,128)(2,1)S(1)}, u32[]{:S(2)}, u32[]{:S(2)}) collective-permute-start(bf16[16,64,128]{2,1,0:T(8,128)(2,1)} %convert_element_type.6), channel_id=1, source_target_pairs={{0,16},{16,32},{32,48},{48,64},{64,80},{80,96},{96,112},{112,128},... | collective-permute-start | bytes 786440 | tf_op jit(solution)/shard_map/ppermute | solution.py:13
  75.5 29.1 %copy-start = (f32[1024,128]{1,0:T(8,128)S(1)}, f32[1024,128]{1,0:T(8,128)}, u32[]{:S(2)}) copy-start(f32[1024,128]{1,0:T(8,128)} %param.7) | copy-start | bytes 1572868
  118.1 8.0 %collective-permute-start.3 = (bf16[16,64,128]{2,1,0:T(8,128)(2,1)}, bf16[16,64,128]{2,1,0:T(8,128)(2,1)S(1)}, u32[]{:S(2)}, u32[]{:S(2)}) collective-permute-start(bf16[16,64,128]{2,1,0:T(8,128)(2,1)} %get-tuple-element.10), channel_id=1, source_target_pairs={{16,0},{32,16},{48,32},{64,48},{80,64},{96,80},{112,96},{128,112},... | collective-permute-start | bytes 786440 | tf_op jit(solution)/shard_map/ppermute | solution.py:14
  120.7 6.7 %collective-permute-start.2 = (bf16[16,64,128]{2,1,0:T(8,128)(2,1)}, bf16[16,64,128]{2,1,0:T(8,128)(2,1)S(1)}, u32[]{:S(2)}, u32[]{:S(2)}) collective-permute-start(bf16[16,64,128]{2,1,0:T(8,128)(2,1)} %get-tuple-element.10), channel_id=1, source_target_pairs={{0,16},{16,32},{32,48},{48,64},{64,80},{80,96},{96,112},{112,128},... | collective-permute-start | bytes 786440 | tf_op jit(solution)/shard_map/ppermute | solution.py:13
  221.6 3.2 %collective-permute-start.4 = (f32[128,128]{0,1:T(8,128)S(1)}, f32[128,128]{0,1:T(8,128)S(1)}, u32[]{:S(2)}, u32[]{:S(2)}) collective-permute-start(f32[128,128]{0,1:T(8,128)S(1)} %convolution_bitcast_fusion.2), channel_id=1, source_target_pairs={{0,1},{1,0},{2,3},{3,2},{4,5},{5,4},{6,7},{7,6},{8,9},{9,8},{10,11... | collective-permute-start | bytes 196616 | tf_op jit(solution)/shard_map/ppermute | solution.py:25
  224.8 4.9 %collective-permute-start.5 = (f32[128,128]{0,1:T(8,128)S(1)}, f32[128,128]{0,1:T(8,128)S(1)}, u32[]{:S(2)}, u32[]{:S(2)}) collective-permute-start(f32[128,128]{0,1:T(8,128)S(1)} %add.69), channel_id=1, source_target_pairs={{0,2},{2,0},{1,3},{3,1},{4,6},{6,4},{5,7},{7,5},{8,10},{10,8},{9,1... | collective-permute-start | bytes 196616 | tf_op jit(solution)/shard_map/ppermute | solution.py:25
  229.7 3.2 %collective-permute-start.6 = (f32[128,128]{0,1:T(8,128)S(1)}, f32[128,128]{0,1:T(8,128)S(1)}, u32[]{:S(2)}, u32[]{:S(2)}) collective-permute-start(f32[128,128]{0,1:T(8,128)S(1)} %add.70), channel_id=1, source_target_pairs={{0,4},{4,0},{1,5},{5,1},{2,6},{6,2},{3,7},{7,3},{8,12},{12,8},{9,1... | collective-permute-start | bytes 196616 | tf_op jit(solution)/shard_map/ppermute | solution.py:25
  232.9 4.7 %collective-permute-start.7 = (f32[128,128]{0,1:T(8,128)S(1)}, f32[128,128]{0,1:T(8,128)S(1)}, u32[]{:S(2)}, u32[]{:S(2)}) collective-permute-start(f32[128,128]{0,1:T(8,128)S(1)} %add.71), channel_id=1, source_target_pairs={{0,8},{8,0},{1,9},{9,1},{2,10},{10,2},{3,11},{11,3},{4,12},{12,4},... | collective-permute-start | bytes 196616 | tf_op jit(solution)/shard_map/ppermute | solution.py:25
  237.7 6.3 %collective-permute-start.8 = (f32[128,128]{0,1:T(8,128)S(1)}, f32[128,128]{0,1:T(8,128)S(1)}, u32[]{:S(2)}, u32[]{:S(2)}) collective-permute-start(f32[128,128]{0,1:T(8,128)S(1)} %add.72), channel_id=1, source_target_pairs={{0,16},{16,0},{32,48},{48,32},{64,80},{80,64},{96,112},{112,96},{1... | collective-permute-start | bytes 196616 | tf_op jit(solution)/shard_map/ppermute | solution.py:25
  243.9 3.2 %collective-permute-start.9 = (f32[128,128]{0,1:T(8,128)S(1)}, f32[128,128]{0,1:T(8,128)S(1)}, u32[]{:S(2)}, u32[]{:S(2)}) collective-permute-start(f32[128,128]{0,1:T(8,128)S(1)} %add.73), channel_id=1, source_target_pairs={{0,32},{32,0},{16,48},{48,16},{64,96},{96,64},{80,112},{112,80},{1... | collective-permute-start | bytes 196616 | tf_op jit(solution)/shard_map/ppermute | solution.py:25
  247.2 4.1 %collective-permute-start.10 = (f32[128,128]{0,1:T(8,128)S(1)}, f32[128,128]{0,1:T(8,128)S(1)}, u32[]{:S(2)}, u32[]{:S(2)}) collective-permute-start(f32[128,128]{0,1:T(8,128)S(1)} %add.74), channel_id=1, source_target_pairs={{0,64},{64,0},{16,80},{80,16},{32,96},{96,32},{48,112},{112,48},{1... | collective-permute-start | bytes 196616 | tf_op jit(solution)/shard_map/ppermute | solution.py:25
  251.3 8.0 %collective-permute-start.11 = (f32[128,128]{0,1:T(8,128)S(1)}, f32[128,128]{0,1:T(8,128)S(1)}, u32[]{:S(2)}, u32[]{:S(2)}) collective-permute-start(f32[128,128]{0,1:T(8,128)S(1)} %add.75), channel_id=1, source_target_pairs={{0,128},{128,0},{16,144},{144,16},{32,160},{160,32},{48,176},{176,... | collective-permute-start | bytes 196616 | tf_op jit(solution)/shard_map/ppermute | solution.py:25
Sparse Core Ops, SparseCore 0:
  11.0 60.3 all-gather.2
  118.3 56.2 all-gather.4

commit v3 on v2

v3 whole, which is shorter than its diff:
```python
import functools

import jax
import jax.numpy as jnp
from jax import lax
from jax.experimental import pallas as pl
from jax.experimental.pallas import tpu as pltpu
from jax.sharding import PartitionSpec as P

precise = lax.Precision.HIGHEST
MESH = pl.DeviceIdType.MESH


def hops(t):
    ring = (0, 1, 2, 1)
    return ring[t & 3] + ring[t >> 2]


def coupling_kernel(
    cycle, groups, index_ref, own_ref, ham_hbm, out_ref, *scratch
):
    peers = cycle - 1
    held = scratch[: peers + 2]
    ham_buf, ham_sem, send_sem, recv_sem = scratch[peers + 2 :]
    shard_blocks, nsrc, block_size, width = ham_hbm.shape
    per_source = width // block_size
    me = lax.axis_index("blk")
    grp = lax.axis_index("group")
    has_below = grp > 0
    has_above = grp < groups - 1

    def remote(slot, device, dest_slot):
        return pltpu.make_async_remote_copy(
            src_ref=own_ref,
            dst_ref=held[dest_slot],
            send_sem=send_sem.at[slot],
            recv_sem=recv_sem.at[dest_slot],
            device_id=device,
            device_id_type=MESH,
        )

    barrier = pltpu.get_barrier_semaphore()
    for t in range(1, cycle):
        pl.semaphore_signal(barrier, inc=1, device_id=(grp, me ^ t), device_id_type=MESH)

    @pl.when(has_below)
    def _():
        pl.semaphore_signal(barrier, inc=1, device_id=(grp - 1, me), device_id_type=MESH)

    @pl.when(has_above)
    def _():
        pl.semaphore_signal(barrier, inc=1, device_id=(grp + 1, me), device_id_type=MESH)

    expected = peers + has_below.astype(jnp.int32) + has_above.astype(jnp.int32)
    pl.semaphore_wait(barrier, expected)

    @pl.when(has_above)
    def _():
        remote(peers, (grp + 1, me), peers).start()

    @pl.when(has_below)
    def _():
        remote(peers + 1, (grp - 1, me), peers + 1).start()

    order = sorted(range(1, cycle), key=hops)
    for t in order:
        remote(t - 1, (grp, me ^ t), t - 1).start()

    steps = [("own", 0), ("below", nsrc - 2), ("above", nsrc - 1)] + [("peer", t) for t in order]

    def source_of(kind, t):
        if kind == "own":
            return me
        if kind == "peer":
            return me ^ t
        return t

    def ham_copy(step, slot):
        kind, t = steps[step]
        return pltpu.make_async_copy(
            ham_hbm.at[:, source_of(kind, t)], ham_buf.at[slot], ham_sem.at[slot]
        )

    out_ref[...] = jnp.zeros_like(out_ref)
    ham_copy(0, 0).start()

    for step, (kind, t) in enumerate(steps):
        slot = step % 2
        if kind == "own":
            data = own_ref
        elif kind == "peer":
            data = held[t - 1]
        elif kind == "below":
            data = held[peers]
        else:
            data = held[peers + 1]
        source = source_of(kind, t)

        def work(data=data, source=source, slot=slot, step=step, kind=kind, t=t):
            if kind == "peer":
                remote(t - 1, (grp, me ^ t), t - 1).wait_recv()
            elif kind == "below":
                remote(peers, (grp, me), peers).wait_recv()
            elif kind == "above":
                remote(peers + 1, (grp, me), peers + 1).wait_recv()

            def row(r, carry):
                base = (r * nsrc + source) * per_source
                blocks = [data[index_ref[base + j]] for j in range(per_source)]
                picked = jnp.concatenate(blocks, axis=0)
                out_ref[r] += jnp.dot(
                    ham_buf[slot, r], picked, preferred_element_type=jnp.float32
                )
                return carry

            lax.fori_loop(0, shard_blocks, row, 0)

        ham_copy(step, slot).wait()
        if step + 1 < len(steps):
            ham_copy(step + 1, 1 - slot).start()
        if kind == "below":
            pl.when(has_below)(work)
        elif kind == "above":
            pl.when(has_above)(work)
        else:
            work()

    for t in order:
        remote(t - 1, (grp, me ^ t), t - 1).wait_send()

    @pl.when(has_above)
    def _():
        remote(peers, (grp + 1, me), peers).wait_send()

    @pl.when(has_below)
    def _():
        remote(peers + 1, (grp - 1, me), peers + 1).wait_send()


def couple_all(hamiltonian, index, rounded):
    shard_blocks, nsrc, block_size, width = hamiltonian.shape
    states = rounded.shape[2]
    cycle = lax.axis_size("blk")
    groups = lax.axis_size("group")
    slab = pltpu.VMEM(rounded.shape, rounded.dtype)
    flops = 2 * shard_blocks * nsrc * block_size * width * states
    return pl.pallas_call(
        functools.partial(coupling_kernel, cycle, groups),
        out_shape=jax.ShapeDtypeStruct((shard_blocks, block_size, states), jnp.float32),
        in_specs=[
            pl.BlockSpec(memory_space=pltpu.SMEM),
            pl.BlockSpec(memory_space=pltpu.VMEM),
            pl.BlockSpec(memory_space=pl.ANY),
        ],
        out_specs=pl.BlockSpec(memory_space=pltpu.VMEM),
        scratch_shapes=[slab] * (cycle + 1)
        + [
            pltpu.VMEM((2, shard_blocks, block_size, width), hamiltonian.dtype),
            pltpu.SemaphoreType.DMA((2,)),
            pltpu.SemaphoreType.DMA((cycle + 1,)),
            pltpu.SemaphoreType.DMA((cycle + 1,)),
        ],
        compiler_params=pltpu.CompilerParams(
            collective_id=0, has_side_effects=True, vmem_limit_bytes=48 * 1024 * 1024
        ),
        cost_estimate=pl.CostEstimate(
            flops=flops, transcendentals=0, bytes_accessed=hamiltonian.size * 2
        ),
    )(index, rounded, hamiltonian)


def from_partner(block, axis, bit):
    count = lax.axis_size(axis)
    route = []
    for low in range(count):
        high = low | 1 << bit
        if high != low and high < count:
            route += [(low, high), (high, low)]
    return lax.ppermute(block, axis, route)


def summed_over_mesh(value):
    for axis in ("blk", "group"):
        for bit in range(lax.axis_size(axis).bit_length() - 1):
            value = value + from_partner(value, axis, bit)
    return value


def on_device(hamiltonian, block_columns, potential, trial_slab):
    shard_blocks = hamiltonian.shape[0]
    block_size = hamiltonian.shape[2]
    states = trial_slab.shape[1]
    index = block_columns.reshape(-1)
    start_slab = trial_slab.reshape(shard_blocks, block_size, states)
    weights = potential.reshape(shard_blocks, block_size, 1)
    coupled_start = couple_all(hamiltonian, index, start_slab.astype(jnp.bfloat16))
    filtered_once = 0.5 * (coupled_start + weights * start_slab)
    coupled_next = couple_all(hamiltonian, index, filtered_once.astype(jnp.bfloat16))
    filtered = coupled_next + weights * filtered_once - start_slab
    flat = filtered.reshape(shard_blocks * block_size, states)
    rows_total = flat.shape[0] * lax.axis_size("group") * lax.axis_size("blk")
    local_gram = jnp.dot(flat.T, flat, precision=precise)
    gram = summed_over_mesh(local_gram) / rows_total
    lower = jnp.linalg.cholesky(gram)
    ortho_slab = lax.linalg.triangular_solve(
        lower, flat, left_side=False, lower=True, transpose_a=True
    )
    return (ortho_slab, jnp.transpose(lower))


def solution(mesh):
    placed = (
        P(("group", "blk"), None, None, None),
        P(("group", "blk"), None, None),
        P(("group", "blk")),
        P(("group", "blk"), None),
    )
    return jax.shard_map(
        on_device,
        mesh=mesh,
        in_specs=placed,
        out_specs=(P(("group", "blk"), None), P()),
        check_vma=False,
    )
```

time: 295 us -> 217 us (0.74)
  Pallas kernels: 0 us -> 137 us
  waiting for transfers between devices: 118 us -> 16.6 us
  local copies, waits for them, and re-layouts: 60 us -> 2.67 us
  matrix products: 28.7 us -> 2.36 us
  between operations: 14.2 us -> 0.77 us
  other arithmetic: 33.8 us -> 24.6 us
  starting transfers between devices: 36.6 us -> 29.8 us
    pallas_call x0 -> x2, Pallas kernels: none -> 137 us  [couple_all(): pl.pallas_call(functools.partial(coupling_kernel, cycle, groups), out_sha...]
    all_gather x2 -> x0, waiting for transfers between devices: 98.8 us -> none  [couple_all(): gathered = lax.all_gather(rounded, 'blk', axis=0, tiled=True)]
    gather x2 -> x0, local copies, waits for them, and re-layouts: 58.1 us -> none  [couple_all(): table[index.reshape(-1)]]
    dot_general x2 -> x0, matrix products: 26.3 us -> none  [couple_all(): jnp.einsum('rsik,rskn->rin', hamiltonian, picked, preferred_element_type=...]
    ppermute x4 -> x0, starting transfers between devices: 12.9 us -> none  [the longest x2 7.73 us: neighbours(): above = lax.ppermute(block, 'group', backward)]
    concatenate x2 -> x0, other arithmetic: 8.25 us -> none  [couple_all(): table = jnp.concatenate([gathered, below, above], axis=0)]
    ppermute x8, starting transfers between devices: 23.6 us -> 29.8 us  [from_partner(): return lax.ppermute(block, axis, route)]
    ppermute x4 -> x0, waiting for transfers between devices: 5.1 us -> none  [the longest x2 2.79 us: neighbours(): below = lax.ppermute(block, 'group', forward)]
  transfers between devices with their start and end apart: 14 -> 8, of which waited for: 14 -> 8; matrix products, arithmetic and copies ran while one was open for 1% -> 0% of each run, Pallas kernels for 0% -> 0%
where the time goes in v3:
time: 217 us; the launch traced here: 214 us
  Pallas kernels  137 us (63%)
  starting transfers between devices  29.8 us (14%)
  other arithmetic  24.6 us (11%)
  waiting for transfers between devices  16.6 us (8%)
  local copies, waits for them, and re-layouts  2.67 us (1%)
  matrix products  2.36 us (1%)
    pallas_call x2, Pallas kernels, couple_all(): pl.pallas_call(functools.partial(coupling_kernel, cycle, groups), out_sha...  137 us
    ppermute x8, starting transfers between devices, from_partner(): return lax.ppermute(block, axis, route)  29.8 us
    ppermute x8, waiting for transfers between devices, from_partner(): return lax.ppermute(block, axis, route)  16.6 us
    another operation x3, other arithmetic, on_device(): lower = jnp.linalg.cholesky(gram)  12.4 us
    another operation x1, other arithmetic, on_device(): lax.linalg.triangular_solve(lower, flat, left_side=False, lower=True, tra...  9.81 us
  transfers between devices with their start and end apart: 8, of which 8 were waited for; matrix products, arithmetic and copies ran while one was open for 0% of the time, Pallas kernels for 0%

profile of v3, /device:TPU:1, one launch (start us, length us, event | category | flops | bytes accessed | tf_op | source)
XLA Modules:
  0.0 213.7 jit_solution(17476302876132560788)
XLA Ops:
  0.6 0.0 copy-start
  0.6 1.1 convert_element_type.6.own_ref
  1.8 1.0 copy.10
  2.8 0.1 reshape.24.index_ref
  2.9 0.8 mul.28
  3.7 70.1 %shard_map.59 = f32[16,64,128]{2,1,0:T(8,128)S(1)} custom-call(s32[1152]{0:T(1024)S(1)} %reshape.24.index_ref, bf16[16,64,128]{2,1,0:T(8,128)(2,1)S(1)} %convert_element_type.6.own_ref, bf16[16,18,64,256]{3,2,1,0:T(8,128)(2,1)} %ham_hbm.3), custom_call_target="tpu_custom_call" | custom-call | flops 1207959552 | bytes 9437184 | tf_op jit(solution)/shard_map/pallas_call | solution.py:147
  73.8 0.0 copy-done
  73.8 0.2 multiply_convert_fusion.own_ref
  74.0 66.7 %shard_map.60 = f32[16,64,128]{2,1,0:T(8,128)S(1)} custom-call(s32[1152]{0:T(1024)S(1)} %reshape.24.index_ref, bf16[16,64,128]{2,1,0:T(8,128)(2,1)S(1)} %multiply_convert_fusion.own_ref, bf16[16,18,64,256]{3,2,1,0:T(8,128)(2,1)} %ham_hbm.3), custom_call_target="tpu_custom_call" | custom-call | flops 1207959552 | bytes 9437184 | tf_op jit(solution)/shard_map/pallas_call | solution.py:147
  140.7 0.3 add_subtract_fusion
  141.0 1.0 convolution_bitcast_fusion
  142.0 0.1 collective-permute-start
  142.1 3.1 %collective-permute-done = f32[128,128]{0,1:T(8,128)S(1)} collective-permute-done((f32[128,128]{0,1:T(8,128)S(1)}, f32[128,128]{0,1:T(8,128)S(1)}, u32[]{:S(2)}, u32[]{:S(2)}) %collective-permute-start) | collective-permute-done | bytes 65568 | tf_op jit(solution)/shard_map/ppermute | solution.py:179
  145.3 3.2 %collective-permute-start.1 = (f32[128,128]{0,1:T(8,128)S(1)}, f32[128,128]{0,1:T(8,128)S(1)}, u32[]{:S(2)}, u32[]{:S(2)}) collective-permute-start(f32[128,128]{0,1:T(8,128)S(1)} %add.43), channel_id=1, source_target_pairs={{0,2},{2,0},{1,3},{3,1},{4,6},{6,4},{5,7},{7,5},{8,10},{10,8},{9,1... | collective-permute-start | bytes 196616 | tf_op jit(solution)/shard_map/ppermute | solution.py:179
  148.5 1.9 collective-permute-done.1
  150.3 0.1 collective-permute-start.2
  150.4 3.1 %collective-permute-done.2 = f32[128,128]{0,1:T(8,128)S(1)} collective-permute-done((f32[128,128]{0,1:T(8,128)S(1)}, f32[128,128]{0,1:T(8,128)S(1)}, u32[]{:S(2)}, u32[]{:S(2)}) %collective-permute-start.2) | collective-permute-done | bytes 65568 | tf_op jit(solution)/shard_map/ppermute | solution.py:179
  153.6 8.0 %collective-permute-start.3 = (f32[128,128]{0,1:T(8,128)S(1)}, f32[128,128]{0,1:T(8,128)S(1)}, u32[]{:S(2)}, u32[]{:S(2)}) collective-permute-start(f32[128,128]{0,1:T(8,128)S(1)} %add.45), channel_id=1, source_target_pairs={{0,8},{8,0},{1,9},{9,1},{2,10},{10,2},{3,11},{11,3},{4,12},{12,4},... | collective-permute-start | bytes 196616 | tf_op jit(solution)/shard_map/ppermute | solution.py:179
  161.5 2.0 collective-permute-done.3
  163.6 5.1 %collective-permute-start.4 = (f32[128,128]{0,1:T(8,128)S(1)}, f32[128,128]{0,1:T(8,128)S(1)}, u32[]{:S(2)}, u32[]{:S(2)}) collective-permute-start(f32[128,128]{0,1:T(8,128)S(1)} %add.46), channel_id=1, source_target_pairs={{0,16},{16,0},{32,48},{48,32},{64,80},{80,64},{96,112},{112,96},{1... | collective-permute-start | bytes 196616 | tf_op jit(solution)/shard_map/ppermute | solution.py:179
  168.7 0.9 collective-permute-done.4
  169.6 0.9 collective-permute-start.5
  170.5 2.3 %collective-permute-done.5 = f32[128,128]{0,1:T(8,128)S(1)} collective-permute-done((f32[128,128]{0,1:T(8,128)S(1)}, f32[128,128]{0,1:T(8,128)S(1)}, u32[]{:S(2)}, u32[]{:S(2)}) %collective-permute-start.5) | collective-permute-done | bytes 65568 | tf_op jit(solution)/shard_map/ppermute | solution.py:179
  172.8 5.7 %collective-permute-start.6 = (f32[128,128]{0,1:T(8,128)S(1)}, f32[128,128]{0,1:T(8,128)S(1)}, u32[]{:S(2)}, u32[]{:S(2)}) collective-permute-start(f32[128,128]{0,1:T(8,128)S(1)} %add.48), channel_id=1, source_target_pairs={{0,64},{64,0},{16,80},{80,16},{32,96},{96,32},{48,112},{112,48},{1... | collective-permute-start | bytes 196616 | tf_op jit(solution)/shard_map/ppermute | solution.py:179
  178.5 1.7 collective-permute-done.6
  180.2 6.8 %collective-permute-start.7 = (f32[128,128]{0,1:T(8,128)S(1)}, f32[128,128]{0,1:T(8,128)S(1)}, u32[]{:S(2)}, u32[]{:S(2)}) collective-permute-start(f32[128,128]{0,1:T(8,128)S(1)} %add.49), channel_id=1, source_target_pairs={{0,128},{128,0},{16,144},{144,16},{32,160},{160,32},{48,176},{176,... | collective-permute-start | bytes 196616 | tf_op jit(solution)/shard_map/ppermute | solution.py:179
  186.9 1.7 collective-permute-done.7
  188.6 0.1 copy.13
  188.7 11.7 %cholesky.16 = f32[128,128]{1,0:T(8,128)S(1)} custom-call(f32[128,128]{1,0:T(8,128)S(1)} %fusion.2), custom_call_target="Cholesky" | custom-call | tf_op jit(solution)/shard_map/jit(cholesky)/cholesky | solution.py:204
  200.5 0.6 compare_reduce_fusion
  201.1 0.7 fusion.3
  201.8 9.8 %custom-call.6 = f32[1,128,128]{1,2,0:T(8,128)S(1)} custom-call(f32[1,128,128]{2,1,0:T(8,128)S(1)} %get-tuple-element.7), custom_call_target="InvertDiagBlocksLowerTriangular" | custom-call | tf_op jit(solution)/shard_map/triangular_solve | solution.py:205
  211.6 0.7 copy.14
  212.3 1.4 fusion
  (11 shorter events, 0.1 us)
Async XLA Ops:
  0.6 73.2 %copy-start = (f32[1024,128]{1,0:T(8,128)S(1)}, f32[1024,128]{1,0:T(8,128)}, u32[]{:S(2)}) copy-start(f32[1024,128]{1,0:T(8,128)} %param.7) | copy-start | bytes 1572868
  142.0 3.2 %collective-permute-start = (f32[128,128]{0,1:T(8,128)S(1)}, f32[128,128]{0,1:T(8,128)S(1)}, u32[]{:S(2)}, u32[]{:S(2)}) collective-permute-start(f32[128,128]{0,1:T(8,128)S(1)} %convolution_bitcast_fusion), channel_id=1, source_target_pairs={{0,1},{1,0},{2,3},{3,2},{4,5},{5,4},{6,7},{7,6},{8,9},{9,8},{10,11... | collective-permute-start | bytes 196616 | tf_op jit(solution)/shard_map/ppermute | solution.py:179
  145.3 5.1 %collective-permute-start.1 = (f32[128,128]{0,1:T(8,128)S(1)}, f32[128,128]{0,1:T(8,128)S(1)}, u32[]{:S(2)}, u32[]{:S(2)}) collective-permute-start(f32[128,128]{0,1:T(8,128)S(1)} %add.43), channel_id=1, source_target_pairs={{0,2},{2,0},{1,3},{3,1},{4,6},{6,4},{5,7},{7,5},{8,10},{10,8},{9,1... | collective-permute-start | bytes 196616 | tf_op jit(solution)/shard_map/ppermute | solution.py:179
  150.3 3.2 %collective-permute-start.2 = (f32[128,128]{0,1:T(8,128)S(1)}, f32[128,128]{0,1:T(8,128)S(1)}, u32[]{:S(2)}, u32[]{:S(2)}) collective-permute-start(f32[128,128]{0,1:T(8,128)S(1)} %add.44), channel_id=1, source_target_pairs={{0,4},{4,0},{1,5},{5,1},{2,6},{6,2},{3,7},{7,3},{8,12},{12,8},{9,1... | collective-permute-start | bytes 196616 | tf_op jit(solution)/shard_map/ppermute | solution.py:179
  153.6 10.0 %collective-permute-start.3 = (f32[128,128]{0,1:T(8,128)S(1)}, f32[128,128]{0,1:T(8,128)S(1)}, u32[]{:S(2)}, u32[]{:S(2)}) collective-permute-start(f32[128,128]{0,1:T(8,128)S(1)} %add.45), channel_id=1, source_target_pairs={{0,8},{8,0},{1,9},{9,1},{2,10},{10,2},{3,11},{11,3},{4,12},{12,4},... | collective-permute-start | bytes 196616 | tf_op jit(solution)/shard_map/ppermute | solution.py:179
  163.6 6.0 %collective-permute-start.4 = (f32[128,128]{0,1:T(8,128)S(1)}, f32[128,128]{0,1:T(8,128)S(1)}, u32[]{:S(2)}, u32[]{:S(2)}) collective-permute-start(f32[128,128]{0,1:T(8,128)S(1)} %add.46), channel_id=1, source_target_pairs={{0,16},{16,0},{32,48},{48,32},{64,80},{80,64},{96,112},{112,96},{1... | collective-permute-start | bytes 196616 | tf_op jit(solution)/shard_map/ppermute | solution.py:179
  169.6 3.2 %collective-permute-start.5 = (f32[128,128]{0,1:T(8,128)S(1)}, f32[128,128]{0,1:T(8,128)S(1)}, u32[]{:S(2)}, u32[]{:S(2)}) collective-permute-start(f32[128,128]{0,1:T(8,128)S(1)} %add.47), channel_id=1, source_target_pairs={{0,32},{32,0},{16,48},{48,16},{64,96},{96,64},{80,112},{112,80},{1... | collective-permute-start | bytes 196616 | tf_op jit(solution)/shard_map/ppermute | solution.py:179
  172.8 7.4 %collective-permute-start.6 = (f32[128,128]{0,1:T(8,128)S(1)}, f32[128,128]{0,1:T(8,128)S(1)}, u32[]{:S(2)}, u32[]{:S(2)}) collective-permute-start(f32[128,128]{0,1:T(8,128)S(1)} %add.48), channel_id=1, source_target_pairs={{0,64},{64,0},{16,80},{80,16},{32,96},{96,32},{48,112},{112,48},{1... | collective-permute-start | bytes 196616 | tf_op jit(solution)/shard_map/ppermute | solution.py:179
  180.2 8.4 %collective-permute-start.7 = (f32[128,128]{0,1:T(8,128)S(1)}, f32[128,128]{0,1:T(8,128)S(1)}, u32[]{:S(2)}, u32[]{:S(2)}) collective-permute-start(f32[128,128]{0,1:T(8,128)S(1)} %add.49), channel_id=1, source_target_pairs={{0,128},{128,0},{16,144},{144,16},{32,160},{160,32},{48,176},{176,... | collective-permute-start | bytes 196616 | tf_op jit(solution)/shard_map/ppermute | solution.py:179

commit v4 on v3

--- a/solution.py
+++ b/solution.py
@@ -169,21 +169,51 @@
     )(index, rounded, hamiltonian)
 
 
-def from_partner(block, axis, bit):
-    count = lax.axis_size(axis)
-    route = []
-    for low in range(count):
-        high = low | 1 << bit
-        if high != low and high < count:
-            route += [(low, high), (high, low)]
-    return lax.ppermute(block, axis, route)
+def gram_kernel(stages, gram_ref, out_ref, arrived, send_sem, recv_sem):
+    place = {"group": lax.axis_index("group"), "blk": lax.axis_index("blk")}
+
+    def partner(axis, mask):
+        other = dict(place)
+        other[axis] = place[axis] ^ mask
+        return (other["group"], other["blk"])
+
+    barrier = pltpu.get_barrier_semaphore()
+    for axis, mask in stages:
+        pl.semaphore_signal(barrier, inc=1, device_id=partner(axis, mask), device_id_type=MESH)
+    pl.semaphore_wait(barrier, len(stages))
+    out_ref[...] = gram_ref[...]
+    for k, (axis, mask) in enumerate(stages):
+        copy = pltpu.make_async_remote_copy(
+            src_ref=out_ref,
+            dst_ref=arrived.at[k],
+            send_sem=send_sem.at[k],
+            recv_sem=recv_sem.at[k],
+            device_id=partner(axis, mask),
+            device_id_type=MESH,
+        )
+        copy.start()
+        copy.wait_send()
+        copy.wait_recv()
+        out_ref[...] = out_ref[...] + arrived[k]
 
 
 def summed_over_mesh(value):
-    for axis in ("blk", "group"):
-        for bit in range(lax.axis_size(axis).bit_length() - 1):
-            value = value + from_partner(value, axis, bit)
-    return value
+    stages = []
+    for axis, masks in (("blk", (1, 3, 4, 12)), ("group", (1, 2, 4, 8))):
+        size = lax.axis_size(axis)
+        stages += [(axis, m) for m in masks if m < size]
+    return pl.pallas_call(
+        functools.partial(gram_kernel, stages),
+        out_shape=jax.ShapeDtypeStruct(value.shape, value.dtype),
+        in_specs=[pl.BlockSpec(memory_space=pltpu.VMEM)],
+        out_specs=pl.BlockSpec(memory_space=pltpu.VMEM),
+        scratch_shapes=[
+            pltpu.VMEM((len(stages),) + value.shape, value.dtype),
+            pltpu.SemaphoreType.DMA((len(stages),)),
+            pltpu.SemaphoreType.DMA((len(stages),)),
+        ],
+        compiler_params=pltpu.CompilerParams(collective_id=1, has_side_effects=True),
+    )(value)
 
 
 def on_device(hamiltonian, block_columns, potential, trial_slab):

time: 217 us -> 214 us (0.986)
  Pallas kernels: 137 us -> 181 us
  starting transfers between devices: 29.8 us -> 0 us
  waiting for transfers between devices: 16.6 us -> 0 us
    pallas_call x0 -> x1, Pallas kernels: none -> 44 us  [summed_over_mesh(): pl.pallas_call(functools.partial(gram_kernel, stages), out_shape=jax.Shap...]
    ppermute x8 -> x0, starting transfers between devices: 29.8 us -> none  [from_partner(): return lax.ppermute(block, axis, route)]
    ppermute x8 -> x0, waiting for transfers between devices: 16.6 us -> none  [from_partner(): return lax.ppermute(block, axis, route)]
  transfers between devices with their start and end apart: 8 -> 0, of which waited for: 8 -> 0; matrix products, arithmetic and copies ran while one was open for 0% -> 0% of each run, Pallas kernels for 0% -> 0%
where the time goes in v4:
time: 214 us; the launch traced here: 212 us
  Pallas kernels  181 us (85%)
  other arithmetic  24.6 us (11%)
  matrix products  3.01 us (1%)
  local copies, waits for them, and re-layouts  2.92 us (1%)
    pallas_call x2, Pallas kernels, couple_all(): pl.pallas_call(functools.partial(coupling_kernel, cycle, groups), out_sha...  137 us
    pallas_call x1, Pallas kernels, summed_over_mesh(): pl.pallas_call(functools.partial(gram_kernel, stages), out_shape=jax.Shap...  44 us
    another operation x3, other arithmetic, on_device(): lower = jnp.linalg.cholesky(gram)  12.4 us
    another operation x1, other arithmetic, on_device(): lax.linalg.triangular_solve(lower, flat, left_side=False, lower=True, tra...  9.81 us

profile of v4, /device:TPU:1, one launch (start us, length us, event | category | flops | bytes accessed | tf_op | source)
XLA Modules:
  0.0 212.2 jit_solution(11703059370742265826)
XLA Ops:
  0.6 0.0 copy-start
  0.6 0.0 copy-start.1
  0.6 1.1 convert_element_type.6.own_ref
  1.8 1.0 copy.9
  2.8 0.1 reshape.24.index_ref
  2.9 70.3 %shard_map.59 = f32[16,64,128]{2,1,0:T(8,128)S(1)} custom-call(s32[1152]{0:T(1024)S(1)} %reshape.24.index_ref, bf16[16,64,128]{2,1,0:T(8,128)(2,1)S(1)} %convert_element_type.6.own_ref, bf16[16,18,64,256]{3,2,1,0:T(8,128)(2,1)} %ham_hbm.3), custom_call_target="tpu_custom_call" | custom-call | flops 1207959552 | bytes 9437184 | tf_op jit(solution)/shard_map/pallas_call | solution.py:147
  73.2 0.0 copy-done.1
  73.2 0.1 mul.28
  73.3 0.0 copy-done
  73.3 0.2 multiply_convert_fusion.own_ref
  73.5 66.7 %shard_map.60 = f32[16,64,128]{2,1,0:T(8,128)S(1)} custom-call(s32[1152]{0:T(1024)S(1)} %reshape.24.index_ref, bf16[16,64,128]{2,1,0:T(8,128)(2,1)S(1)} %multiply_convert_fusion.own_ref, bf16[16,18,64,256]{3,2,1,0:T(8,128)(2,1)} %ham_hbm.3), custom_call_target="tpu_custom_call" | custom-call | flops 1207959552 | bytes 9437184 | tf_op jit(solution)/shard_map/pallas_call | solution.py:147
  140.2 0.3 add_subtract_fusion
  140.5 1.6 convolution_bitcast_fusion.gram_ref
  142.1 44.0 %shard_map.61 = f32[128,128]{1,0:T(8,128)} custom-call(f32[128,128]{1,0:T(8,128)} %convolution_bitcast_fusion.gram_ref), custom_call_target="tpu_custom_call" | custom-call | tf_op jit(solution)/shard_map/pallas_call | solution.py:205
  186.2 0.9 copy.10
  187.1 0.1 copy.11
  187.3 11.7 %cholesky.16 = f32[128,128]{1,0:T(8,128)S(1)} custom-call(f32[128,128]{1,0:T(8,128)S(1)} %fusion.2), custom_call_target="Cholesky" | custom-call | tf_op jit(solution)/shard_map/jit(cholesky)/cholesky | solution.py:234
  199.0 0.6 compare_reduce_fusion
  199.6 0.7 fusion.3
  200.3 9.8 %custom-call.6 = f32[1,128,128]{1,2,0:T(8,128)S(1)} custom-call(f32[1,128,128]{2,1,0:T(8,128)S(1)} %get-tuple-element.7), custom_call_target="InvertDiagBlocksLowerTriangular" | custom-call | tf_op jit(solution)/shard_map/triangular_solve | solution.py:235
  210.1 1.4 fusion
  211.5 0.7 copy.12
  (4 shorter events, 0.1 us)
Async XLA Ops:
  0.6 72.6 %copy-start = (f32[1024,128]{1,0:T(8,128)S(1)}, f32[1024,128]{1,0:T(8,128)}, u32[]{:S(2)}) copy-start(f32[1024,128]{1,0:T(8,128)} %param.7) | copy-start | bytes 1572868
  0.6 72.6 %copy-start.1 = (f32[1024]{0:T(1024)S(1)}, f32[1024]{0:T(1024)}, u32[]{:S(2)}) copy-start(f32[1024]{0:T(1024)} %param.6) | copy-start | bytes 12292

commit v5 on v4

--- a/solution.py
+++ b/solution.py
@@ -11,36 +11,56 @@
 MESH = pl.DeviceIdType.MESH
 
 
-def hops(t):
-    ring = (0, 1, 2, 1)
-    return ring[t & 3] + ring[t >> 2]
-
-
-def coupling_kernel(
-    cycle, groups, index_ref, own_ref, ham_hbm, out_ref, *scratch
-):
-    peers = cycle - 1
-    held = scratch[: peers + 2]
-    ham_buf, ham_sem, send_sem, recv_sem = scratch[peers + 2 :]
+RING = 4
+DIRECT = (1, 3, 4, 12, 2, 8)
+
+
+def relayed_slots():
+    both = [(ty << 2) | tx for ty in (1, 3, 2) for tx in (1, 3, 2)]
+    return both
+
+
+def coupling_kernel(groups, index_ref, own_ref, ham_hbm, out_ref, *scratch):
+    cycle = RING * RING
+    held = scratch[: cycle + 1]
+    ham_buf, ham_sem, send_sem, recv_full, recv_a, recv_b, recv_side = scratch[cycle + 1 :]
     shard_blocks, nsrc, block_size, width = ham_hbm.shape
     per_source = width // block_size
+    half = shard_blocks // 2
     me = lax.axis_index("blk")
     grp = lax.axis_index("group")
     has_below = grp > 0
     has_above = grp < groups - 1
-
-    def remote(slot, device, dest_slot):
+    below_buf, above_buf = held[cycle - 1], held[cycle]
+
+    def buf(t):
+        return held[t - 1]
+
+    def copy_to(src, dst, send_index, recv, device):
         return pltpu.make_async_remote_copy(
-            src_ref=own_ref,
-            dst_ref=held[dest_slot],
-            send_sem=send_sem.at[slot],
-            recv_sem=recv_sem.at[dest_slot],
+            src_ref=src,
+            dst_ref=dst,
+            send_sem=send_sem.at[send_index],
+            recv_sem=recv,
             device_id=device,
             device_id_type=MESH,
         )
 
+    def direct(k, t):
+        return copy_to(own_ref, buf(t), k, recv_full.at[k], (grp, me ^ t))
+
+    def relay(k, slot, peer_t, lower):
+        part = pl.ds(0, half) if lower else pl.ds(half, half)
+        dest = slot | peer_t
+        recv = recv_a if lower else recv_b
+        return copy_to(buf(slot).at[part], buf(dest).at[part], 8 + k, recv.at[dest], (grp, me ^ peer_t))
+
+    def side(k, device):
+        dst = below_buf if k == 0 else above_buf
+        return copy_to(own_ref, dst, 6 + k, recv_side.at[k], device)
+
     barrier = pltpu.get_barrier_semaphore()
-    for t in range(1, cycle):
+    for t in DIRECT:
         pl.semaphore_signal(barrier, inc=1, device_id=(grp, me ^ t), device_id_type=MESH)
 
     @pl.when(has_below)
@@ -51,27 +71,35 @@
     def _():
         pl.semaphore_signal(barrier, inc=1, device_id=(grp + 1, me), device_id_type=MESH)
 
-    expected = peers + has_below.astype(jnp.int32) + has_above.astype(jnp.int32)
+    expected = len(DIRECT) + has_below.astype(jnp.int32) + has_above.astype(jnp.int32)
     pl.semaphore_wait(barrier, expected)
 
     @pl.when(has_above)
     def _():
-        remote(peers, (grp + 1, me), peers).start()
+        side(0, (grp + 1, me)).start()
 
     @pl.when(has_below)
     def _():
-        remote(peers + 1, (grp - 1, me), peers + 1).start()
-
-    order = sorted(range(1, cycle), key=hops)
-    for t in order:
-        remote(t - 1, (grp, me ^ t), t - 1).start()
-
-    steps = [("own", 0), ("below", nsrc - 2), ("above", nsrc - 1)] + [("peer", t) for t in order]
+        side(1, (grp - 1, me)).start()
+
+    for k, t in enumerate(DIRECT):
+        direct(k, t).start()
+
+    relays = []
+    for k, t in enumerate(DIRECT):
+        onward = (4, 12, 8) if t < RING else (1, 3, 2)
+        relays.append([(len(relays) * 3 + i, t, p, t < RING) for i, p in enumerate(onward)])
+
+    steps = [("own", 0), ("below", nsrc - 2), ("above", nsrc - 1)]
+    steps += [("direct", k) for k in range(len(DIRECT))]
+    steps += [("relayed", t) for t in relayed_slots()]
 
     def source_of(kind, t):
         if kind == "own":
             return me
-        if kind == "peer":
+        if kind == "direct":
+            return me ^ DIRECT[t]
+        if kind == "relayed":
             return me ^ t
         return t
 
@@ -88,21 +116,28 @@
         slot = step % 2
         if kind == "own":
             data = own_ref
-        elif kind == "peer":
-            data = held[t - 1]
+        elif kind == "direct":
+            data = buf(DIRECT[t])
+        elif kind == "relayed":
+            data = buf(t)
         elif kind == "below":
-            data = held[peers]
+            data = below_buf
         else:
-            data = held[peers + 1]
+            data = above_buf
         source = source_of(kind, t)
 
-        def work(data=data, source=source, slot=slot, step=step, kind=kind, t=t):
-            if kind == "peer":
-                remote(t - 1, (grp, me ^ t), t - 1).wait_recv()
+        def work(data=data, source=source, slot=slot, kind=kind, t=t):
+            if kind == "direct":
+                direct(t, DIRECT[t]).wait_recv()
+                for k, slot_t, peer_t, lower in relays[t]:
+                    relay(k, slot_t, peer_t, lower).start()
+            elif kind == "relayed":
+                copy_to(own_ref.at[pl.ds(0, half)], buf(t).at[pl.ds(0, half)], 0, recv_a.at[t], (grp, me)).wait_recv()
+                copy_to(own_ref.at[pl.ds(half, half)], buf(t).at[pl.ds(half, half)], 0, recv_b.at[t], (grp, me)).wait_recv()
             elif kind == "below":
-                remote(peers, (grp, me), peers).wait_recv()
+                side(0, (grp, me)).wait_recv()
             elif kind == "above":
-                remote(peers + 1, (grp, me), peers + 1).wait_recv()
+                side(1, (grp, me)).wait_recv()
 
             def row(r, carry):
                 base = (r * nsrc + source) * per_source
@@ -125,27 +160,31 @@
         else:
             work()
 
-    for t in order:
-        remote(t - 1, (grp, me ^ t), t - 1).wait_send()
+    for k, t in enumerate(DIRECT):
+        direct(k, t).wait_send()
+    for group_of in relays:
+        for k, slot_t, peer_t, lower in group_of:
+            relay(k, slot_t, peer_t, lower).wait_send()
 
     @pl.when(has_above)
     def _():
-        remote(peers, (grp + 1, me), peers).wait_send()
+        side(0, (grp + 1, me)).wait_send()
 
     @pl.when(has_below)
     def _():
-        remote(peers + 1, (grp - 1, me), peers + 1).wait_send()
+        side(1, (grp - 1, me)).wait_send()
 
 
 def couple_all(hamiltonian, index, rounded):
     shard_blocks, nsrc, block_size, width = hamiltonian.shape
     states = rounded.shape[2]
     cycle = lax.axis_size("blk")
+    assert cycle == RING * RING
     groups = lax.axis_size("group")
     slab = pltpu.VMEM(rounded.shape, rounded.dtype)
     flops = 2 * shard_blocks * nsrc * block_size * width * states
     return pl.pallas_call(
-        functools.partial(coupling_kernel, cycle, groups),
+        functools.partial(coupling_kernel, groups),
         out_shape=jax.ShapeDtypeStruct((shard_blocks, block_size, states), jnp.float32),
         in_specs=[
             pl.BlockSpec(memory_space=pltpu.SMEM),
@@ -157,8 +196,11 @@
         + [
             pltpu.VMEM((2, shard_blocks, block_size, width), hamiltonian.dtype),
             pltpu.SemaphoreType.DMA((2,)),
-            pltpu.SemaphoreType.DMA((cycle + 1,)),
-            pltpu.SemaphoreType.DMA((cycle + 1,)),
+            pltpu.SemaphoreType.DMA((8 + 18,)),
+            pltpu.SemaphoreType.DMA((len(DIRECT),)),
+            pltpu.SemaphoreType.DMA((cycle,)),
+            pltpu.SemaphoreType.DMA((cycle,)),
+            pltpu.SemaphoreType.DMA((2,)),
         ],
         compiler_params=pltpu.CompilerParams(
             collective_id=0, has_side_effects=True, vmem_limit_bytes=48 * 1024 * 1024

time: 214 us -> 164 us (0.77)
  Pallas kernels: 181 us -> 132 us
    pallas_call x2, Pallas kernels: 137 us -> 97.4 us  [couple_all(): pl.pallas_call(functools.partial(coupling_kernel, groups), out_shape=jax....]
    pallas_call x1, Pallas kernels: 44 us -> 34.7 us  [summed_over_mesh(): pl.pallas_call(functools.partial(gram_kernel, stages), out_shape=jax.Shap...]
where the time goes in v5:
time: 164 us; the launch traced here: 163 us
  Pallas kernels  132 us (80%)
  other arithmetic  24.6 us (15%)
  matrix products  3 us (2%)
  local copies, waits for them, and re-layouts  2.92 us (2%)
    pallas_call x2, Pallas kernels, couple_all(): pl.pallas_call(functools.partial(coupling_kernel, groups), out_shape=jax....  97.4 us
    pallas_call x1, Pallas kernels, summed_over_mesh(): pl.pallas_call(functools.partial(gram_kernel, stages), out_shape=jax.Shap...  34.7 us
    another operation x3, other arithmetic, on_device(): lower = jnp.linalg.cholesky(gram)  12.4 us
    another operation x1, other arithmetic, on_device(): lax.linalg.triangular_solve(lower, flat, left_side=False, lower=True, tra...  9.81 us

profile of v5, /device:TPU:1, one launch (start us, length us, event | category | flops | bytes accessed | tf_op | source)
XLA Modules:
  0.0 163.3 jit_solution(3804848323417934442)
XLA Ops:
  0.6 0.0 copy-start
  0.6 0.0 copy-start.1
  0.6 1.1 convert_element_type.6.own_ref
  1.8 1.0 copy.9
  2.8 0.1 reshape.24.index_ref
  2.9 48.8 %shard_map.59 = f32[16,64,128]{2,1,0:T(8,128)S(1)} custom-call(s32[1152]{0:T(1024)S(1)} %reshape.24.index_ref, bf16[16,64,128]{2,1,0:T(8,128)(2,1)S(1)} %convert_element_type.6.own_ref, bf16[16,18,64,256]{3,2,1,0:T(8,128)(2,1)} %ham_hbm.3), custom_call_target="tpu_custom_call" | custom-call | flops 1207959552 | bytes 9437184 | tf_op jit(solution)/shard_map/pallas_call | solution.py:186
  51.7 0.0 copy-done.1
  51.7 0.1 mul.28
  51.7 0.0 copy-done
  51.7 0.2 multiply_convert_fusion.own_ref
  52.0 48.7 %shard_map.60 = f32[16,64,128]{2,1,0:T(8,128)S(1)} custom-call(s32[1152]{0:T(1024)S(1)} %reshape.24.index_ref, bf16[16,64,128]{2,1,0:T(8,128)(2,1)S(1)} %multiply_convert_fusion.own_ref, bf16[16,18,64,256]{3,2,1,0:T(8,128)(2,1)} %ham_hbm.3), custom_call_target="tpu_custom_call" | custom-call | flops 1207959552 | bytes 9437184 | tf_op jit(solution)/shard_map/pallas_call | solution.py:186
  100.6 0.3 add_subtract_fusion
  101.0 1.6 %convolution_bitcast_fusion.gram_ref = f32[128,128]{1,0:T(8,128)} fusion(f32[16,64,128]{2,1,0:T(8,128)S(1)} %add_subtract_fusion), kind=kOutput, calls=%fused_computation | convolution fusion | flops 201326592 | bytes 589824 | tf_op jit(solution)/shard_map/dot_general | solution.py:274
  102.6 34.7 %shard_map.61 = f32[128,128]{1,0:T(8,128)} custom-call(f32[128,128]{1,0:T(8,128)} %convolution_bitcast_fusion.gram_ref), custom_call_target="tpu_custom_call" | custom-call | tf_op jit(solution)/shard_map/pallas_call | solution.py:247
  137.3 0.9 copy.10
  138.3 0.1 copy.11
  138.4 11.7 %cholesky.16 = f32[128,128]{1,0:T(8,128)S(1)} custom-call(f32[128,128]{1,0:T(8,128)S(1)} %fusion.2), custom_call_target="Cholesky" | custom-call | tf_op jit(solution)/shard_map/jit(cholesky)/cholesky | solution.py:276
  150.1 0.6 compare_reduce_fusion
  150.8 0.7 fusion.3
  151.4 9.8 %custom-call.6 = f32[1,128,128]{1,2,0:T(8,128)S(1)} custom-call(f32[1,128,128]{2,1,0:T(8,128)S(1)} %get-tuple-element.7), custom_call_target="InvertDiagBlocksLowerTriangular" | custom-call | tf_op jit(solution)/shard_map/triangular_solve | solution.py:277
  161.3 1.4 fusion
  162.6 0.7 copy.12
  (4 shorter events, 0.1 us)
Async XLA Ops:
  0.6 51.1 %copy-start = (f32[1024,128]{1,0:T(8,128)S(1)}, f32[1024,128]{1,0:T(8,128)}, u32[]{:S(2)}) copy-start(f32[1024,128]{1,0:T(8,128)} %param.7) | copy-start | bytes 1572868
  0.6 51.0 %copy-start.1 = (f32[1024]{0:T(1024)S(1)}, f32[1024]{0:T(1024)}, u32[]{:S(2)}) copy-start(f32[1024]{0:T(1024)} %param.6) | copy-start | bytes 12292

commit v6 on v5

--- a/solution.py
+++ b/solution.py
@@ -148,7 +148,7 @@
                 )
                 return carry
 
-            lax.fori_loop(0, shard_blocks, row, 0)
+            lax.fori_loop(0, shard_blocks, row, 0, unroll=True)
 
         ham_copy(step, slot).wait()
         if step + 1 < len(steps):

time: 164 us -> 146 us (0.89); the launches traced: 163 us -> 144 us
  Pallas kernels: 132 us -> 112 us
    pallas_call x2, Pallas kernels: 97.4 us -> 75.3 us  [couple_all(): pl.pallas_call(functools.partial(coupling_kernel, groups), out_shape=jax....]
    pallas_call x1, Pallas kernels: 34.7 us -> 37 us  [summed_over_mesh(): pl.pallas_call(functools.partial(gram_kernel, stages), out_shape=jax.Shap...]
where the time goes in v6:
time: 146 us; the launch traced here: 144 us
  Pallas kernels  112 us (77%)
  other arithmetic  24.6 us (17%)
  matrix products  3 us (2%)
  local copies, waits for them, and re-layouts  2.92 us (2%)
    pallas_call x2, Pallas kernels, couple_all(): pl.pallas_call(functools.partial(coupling_kernel, groups), out_shape=jax....  75.3 us
    pallas_call x1, Pallas kernels, summed_over_mesh(): pl.pallas_call(functools.partial(gram_kernel, stages), out_shape=jax.Shap...  37 us
    another operation x3, other arithmetic, on_device(): lower = jnp.linalg.cholesky(gram)  12.4 us
    another operation x1, other arithmetic, on_device(): lax.linalg.triangular_solve(lower, flat, left_side=False, lower=True, tra...  9.81 us

profile of v6, /device:TPU:1, one launch (start us, length us, event | category | flops | bytes accessed | tf_op | source)
XLA Modules:
  0.0 143.5 jit_solution(17982137707035801884)
XLA Ops:
  0.6 0.0 copy-start
  0.6 0.0 copy-start.1
  0.6 1.1 convert_element_type.6.own_ref
  1.8 1.0 copy.9
  2.8 0.1 reshape.24.index_ref
  2.9 38.1 %shard_map.59 = f32[16,64,128]{2,1,0:T(8,128)S(1)} custom-call(s32[1152]{0:T(1024)S(1)} %reshape.24.index_ref, bf16[16,64,128]{2,1,0:T(8,128)(2,1)S(1)} %convert_element_type.6.own_ref, bf16[16,18,64,256]{3,2,1,0:T(8,128)(2,1)} %ham_hbm.3), custom_call_target="tpu_custom_call" | custom-call | flops 1207959552 | bytes 9437184 | tf_op jit(solution)/shard_map/pallas_call | solution.py:186
  41.0 0.0 copy-done.1
  41.0 0.1 mul.28
  41.1 0.0 copy-done
  41.1 0.2 multiply_convert_fusion.own_ref
  41.3 37.2 %shard_map.60 = f32[16,64,128]{2,1,0:T(8,128)S(1)} custom-call(s32[1152]{0:T(1024)S(1)} %reshape.24.index_ref, bf16[16,64,128]{2,1,0:T(8,128)(2,1)S(1)} %multiply_convert_fusion.own_ref, bf16[16,18,64,256]{3,2,1,0:T(8,128)(2,1)} %ham_hbm.3), custom_call_target="tpu_custom_call" | custom-call | flops 1207959552 | bytes 9437184 | tf_op jit(solution)/shard_map/pallas_call | solution.py:186
  78.5 0.3 add_subtract_fusion
  78.9 1.6 %convolution_bitcast_fusion.gram_ref = f32[128,128]{1,0:T(8,128)} fusion(f32[16,64,128]{2,1,0:T(8,128)S(1)} %add_subtract_fusion), kind=kOutput, calls=%fused_computation | convolution fusion | flops 201326592 | bytes 589824 | tf_op jit(solution)/shard_map/dot_general | solution.py:274
  80.5 37.0 %shard_map.61 = f32[128,128]{1,0:T(8,128)} custom-call(f32[128,128]{1,0:T(8,128)} %convolution_bitcast_fusion.gram_ref), custom_call_target="tpu_custom_call" | custom-call | tf_op jit(solution)/shard_map/pallas_call | solution.py:247
  117.5 0.9 copy.10
  118.5 0.1 copy.11
  118.6 11.7 %cholesky.16 = f32[128,128]{1,0:T(8,128)S(1)} custom-call(f32[128,128]{1,0:T(8,128)S(1)} %fusion.2), custom_call_target="Cholesky" | custom-call | tf_op jit(solution)/shard_map/jit(cholesky)/cholesky | solution.py:276
  130.3 0.6 compare_reduce_fusion
  131.0 0.7 fusion.3
  131.6 9.8 %custom-call.6 = f32[1,128,128]{1,2,0:T(8,128)S(1)} custom-call(f32[1,128,128]{2,1,0:T(8,128)S(1)} %get-tuple-element.7), custom_call_target="InvertDiagBlocksLowerTriangular" | custom-call | tf_op jit(solution)/shard_map/triangular_solve | solution.py:277
  141.5 1.4 fusion
  142.8 0.7 copy.12
  (4 shorter events, 0.1 us)
Async XLA Ops:
  0.6 40.4 %copy-start = (f32[1024,128]{1,0:T(8,128)S(1)}, f32[1024,128]{1,0:T(8,128)}, u32[]{:S(2)}) copy-start(f32[1024,128]{1,0:T(8,128)} %param.7) | copy-start | bytes 1572868
  0.6 40.3 %copy-start.1 = (f32[1024]{0:T(1024)S(1)}, f32[1024]{0:T(1024)}, u32[]{:S(2)}) copy-start(f32[1024]{0:T(1024)} %param.6) | copy-start | bytes 12292

commit v7 on v6

--- a/solution.py
+++ b/solution.py
@@ -213,46 +213,75 @@
 
 def gram_kernel(stages, gram_ref, out_ref, arrived, send_sem, recv_sem):
     place = {"group": lax.axis_index("group"), "blk": lax.axis_index("blk")}
-
-    def partner(axis, mask):
+    members = 4
+
+    def field(axis, shift):
+        return (place[axis] >> shift) % members
+
+    def peer(axis, shift, position):
         other = dict(place)
-        other[axis] = place[axis] ^ mask
+        other[axis] = place[axis] + (position - field(axis, shift)) * (1 << shift)
         return (other["group"], other["blk"])
 
     barrier = pltpu.get_barrier_semaphore()
-    for axis, mask in stages:
-        pl.semaphore_signal(barrier, inc=1, device_id=partner(axis, mask), device_id_type=MESH)
-    pl.semaphore_wait(barrier, len(stages))
+    for axis, shift in stages:
+        for m in range(1, members):
+            pl.semaphore_signal(
+                barrier, inc=1, device_id=peer(axis, shift, field(axis, shift) ^ m), device_id_type=MESH
+            )
+    pl.semaphore_wait(barrier, len(stages) * (members - 1))
     out_ref[...] = gram_ref[...]
-    for k, (axis, mask) in enumerate(stages):
-        copy = pltpu.make_async_remote_copy(
-            src_ref=out_ref,
-            dst_ref=arrived.at[k],
-            send_sem=send_sem.at[k],
-            recv_sem=recv_sem.at[k],
-            device_id=partner(axis, mask),
-            device_id_type=MESH,
-        )
-        copy.start()
-        copy.wait_send()
-        copy.wait_recv()
-        out_ref[...] = out_ref[...] + arrived[k]
+    for k, (axis, shift) in enumerate(stages):
+        mine = field(axis, shift)
+
+        def exchange(position, m):
+            return pltpu.make_async_remote_copy(
+                src_ref=out_ref,
+                dst_ref=arrived.at[k, mine],
+                send_sem=send_sem.at[k, m],
+                recv_sem=recv_sem.at[k, mine],
+                device_id=peer(axis, shift, position),
+                device_id_type=MESH,
+            )
+
+        def incoming(position):
+            return pltpu.make_async_remote_copy(
+                src_ref=out_ref,
+                dst_ref=arrived.at[k, position],
+                send_sem=send_sem.at[k, 0],
+                recv_sem=recv_sem.at[k, position],
+                device_id=peer(axis, shift, position),
+                device_id_type=MESH,
+            )
+
+        for m in range(1, members):
+            exchange(mine ^ m, m).start()
+        arrived[k, mine] = out_ref[...]
+        for m in range(1, members):
+            exchange(mine ^ m, m).wait_send()
+        for m in range(1, members):
+            incoming(mine ^ m).wait_recv()
+        total = arrived[k, 0]
+        for position in range(1, members):
+            total = total + arrived[k, position]
+        out_ref[...] = total
 
 
 def summed_over_mesh(value):
     stages = []
-    for axis, masks in (("blk", (1, 3, 4, 12)), ("group", (1, 2, 4, 8))):
+    for axis in ("blk", "group"):
         size = lax.axis_size(axis)
-        stages += [(axis, m) for m in masks if m < size]
+        assert size == 16
+        stages += [(axis, 0), (axis, 2)]
     return pl.pallas_call(
         functools.partial(gram_kernel, stages),
         out_shape=jax.ShapeDtypeStruct(value.shape, value.dtype),
         in_specs=[pl.BlockSpec(memory_space=pltpu.VMEM)],
         out_specs=pl.BlockSpec(memory_space=pltpu.VMEM),
         scratch_shapes=[
-            pltpu.VMEM((len(stages),) + value.shape, value.dtype),
-            pltpu.SemaphoreType.DMA((len(stages),)),
-            pltpu.SemaphoreType.DMA((len(stages),)),
+            pltpu.VMEM((len(stages), 4) + value.shape, value.dtype),
+            pltpu.SemaphoreType.DMA((len(stages), 4)),
+            pltpu.SemaphoreType.DMA((len(stages), 4)),
         ],
         compiler_params=pltpu.CompilerParams(collective_id=1, has_side_effects=True),
     )(value)

time: 146 us -> 141 us (0.966)
  Pallas kernels: 112 us -> 108 us
    pallas_call x1, Pallas kernels: 37 us -> 32.6 us  [summed_over_mesh(): pl.pallas_call(functools.partial(gram_kernel, stages), out_shape=jax.Shap...]
where the time goes in v7:
time: 141 us; the launch traced here: 139 us
  Pallas kernels  108 us (77%)
  other arithmetic  24.6 us (17%)
  matrix products  3.01 us (2%)
  local copies, waits for them, and re-layouts  2.92 us (2%)
    pallas_call x2, Pallas kernels, couple_all(): pl.pallas_call(functools.partial(coupling_kernel, groups), out_shape=jax....  75.3 us
    pallas_call x1, Pallas kernels, summed_over_mesh(): pl.pallas_call(functools.partial(gram_kernel, stages), out_shape=jax.Shap...  32.6 us
    another operation x3, other arithmetic, on_device(): lower = jnp.linalg.cholesky(gram)  12.4 us
    another operation x1, other arithmetic, on_device(): lax.linalg.triangular_solve(lower, flat, left_side=False, lower=True, tra...  9.81 us

profile of v7, /device:TPU:1, one launch (start us, length us, event | category | flops | bytes accessed | tf_op | source)
XLA Modules:
  0.0 139.1 jit_solution(2958109066676166811)
XLA Ops:
  0.6 0.0 copy-start
  0.6 0.0 copy-start.1
  0.6 1.1 convert_element_type.6.own_ref
  1.8 1.0 copy.9
  2.8 0.1 reshape.24.index_ref
  2.9 38.1 %shard_map.59 = f32[16,64,128]{2,1,0:T(8,128)S(1)} custom-call(s32[1152]{0:T(1024)S(1)} %reshape.24.index_ref, bf16[16,64,128]{2,1,0:T(8,128)(2,1)S(1)} %convert_element_type.6.own_ref, bf16[16,18,64,256]{3,2,1,0:T(8,128)(2,1)} %ham_hbm.3), custom_call_target="tpu_custom_call" | custom-call | flops 1207959552 | bytes 9437184 | tf_op jit(solution)/shard_map/pallas_call | solution.py:186
  41.0 0.0 copy-done.1
  41.0 0.1 mul.28
  41.1 0.0 copy-done
  41.1 0.2 multiply_convert_fusion.own_ref
  41.3 37.2 %shard_map.60 = f32[16,64,128]{2,1,0:T(8,128)S(1)} custom-call(s32[1152]{0:T(1024)S(1)} %reshape.24.index_ref, bf16[16,64,128]{2,1,0:T(8,128)(2,1)S(1)} %multiply_convert_fusion.own_ref, bf16[16,18,64,256]{3,2,1,0:T(8,128)(2,1)} %ham_hbm.3), custom_call_target="tpu_custom_call" | custom-call | flops 1207959552 | bytes 9437184 | tf_op jit(solution)/shard_map/pallas_call | solution.py:186
  78.5 0.3 add_subtract_fusion
  78.9 1.6 %convolution_bitcast_fusion.gram_ref = f32[128,128]{1,0:T(8,128)} fusion(f32[16,64,128]{2,1,0:T(8,128)S(1)} %add_subtract_fusion), kind=kOutput, calls=%fused_computation | convolution fusion | flops 201326592 | bytes 589824 | tf_op jit(solution)/shard_map/dot_general | solution.py:303
  80.5 32.6 %shard_map.61 = f32[128,128]{1,0:T(8,128)} custom-call(f32[128,128]{1,0:T(8,128)} %convolution_bitcast_fusion.gram_ref), custom_call_target="tpu_custom_call" | custom-call | tf_op jit(solution)/shard_map/pallas_call | solution.py:276
  113.1 0.9 copy.10
  114.0 0.1 copy.11
  114.2 11.7 %cholesky.16 = f32[128,128]{1,0:T(8,128)S(1)} custom-call(f32[128,128]{1,0:T(8,128)S(1)} %fusion.2), custom_call_target="Cholesky" | custom-call | tf_op jit(solution)/shard_map/jit(cholesky)/cholesky | solution.py:305
  125.9 0.6 compare_reduce_fusion
  126.6 0.7 fusion.3
  127.2 9.8 %custom-call.6 = f32[1,128,128]{1,2,0:T(8,128)S(1)} custom-call(f32[1,128,128]{2,1,0:T(8,128)S(1)} %get-tuple-element.7), custom_call_target="InvertDiagBlocksLowerTriangular" | custom-call | tf_op jit(solution)/shard_map/triangular_solve | solution.py:306
  137.0 1.4 fusion
  138.4 0.7 copy.12
  (4 shorter events, 0.1 us)
Async XLA Ops:
  0.6 40.4 %copy-start = (f32[1024,128]{1,0:T(8,128)S(1)}, f32[1024,128]{1,0:T(8,128)}, u32[]{:S(2)}) copy-start(f32[1024,128]{1,0:T(8,128)} %param.7) | copy-start | bytes 1572868
  0.6 40.3 %copy-start.1 = (f32[1024]{0:T(1024)S(1)}, f32[1024]{0:T(1024)}, u32[]{:S(2)}) copy-start(f32[1024]{0:T(1024)} %param.6) | copy-start | bytes 12292

commit v8 on v7

--- a/solution.py
+++ b/solution.py
@@ -12,56 +12,115 @@
 
 
 RING = 4
-DIRECT = (1, 3, 4, 12, 2, 8)
-
-
-def relayed_slots():
-    both = [(ty << 2) | tx for ty in (1, 3, 2) for tx in (1, 3, 2)]
-    return both
+QUARTERS = 4
+NEIGHBOURS = (1, 3, 4, 12)
+
+
+def forwards(t, q):
+    tx, ty = t & 3, t >> 2
+    out = []
+    if q < 2:
+        if t == 0:
+            out += [1, 3]
+        if ty == 0 and tx == 1 and q == 0:
+            out.append(3)
+        if ty == 0 and tx == 3 and q == 1:
+            out.append(1)
+        if ty == 0:
+            out += [4, 12]
+        if ty == 1 and q == 0:
+            out.append(12)
+        if ty == 3 and q == 1:
+            out.append(4)
+    else:
+        if t == 0:
+            out += [4, 12]
+        if tx == 0 and ty == 1 and q == 2:
+            out.append(12)
+        if tx == 0 and ty == 3 and q == 3:
+            out.append(4)
+        if tx == 0:
+            out += [1, 3]
+        if tx == 1 and q == 2:
+            out.append(3)
+        if tx == 3 and q == 3:
+            out.append(1)
+    return out
+
+
+def schedule():
+    level = {(0, q): 0 for q in range(QUARTERS)}
+    sends = []
+    frontier = [(0, q) for q in range(QUARTERS)]
+    while frontier:
+        nxt = []
+        for t, q in frontier:
+            for d in forwards(t, q):
+                dest = (t ^ d, q)
+                assert dest not in level
+                level[dest] = level[(t, q)] + 1
+                sends.append((t, q, d))
+                nxt.append(dest)
+        frontier = nxt
+    assert len(level) == RING * RING * QUARTERS
+    return level, sends
 
 
 def coupling_kernel(groups, index_ref, own_ref, ham_hbm, out_ref, *scratch):
     cycle = RING * RING
     held = scratch[: cycle + 1]
-    ham_buf, ham_sem, send_sem, recv_full, recv_a, recv_b, recv_side = scratch[cycle + 1 :]
+    ham_buf, ham_sem, send_sem, recv_sem, side_send, side_recv = scratch[cycle + 1 :]
     shard_blocks, nsrc, block_size, width = ham_hbm.shape
     per_source = width // block_size
-    half = shard_blocks // 2
+    part = shard_blocks // QUARTERS
     me = lax.axis_index("blk")
     grp = lax.axis_index("group")
     has_below = grp > 0
     has_above = grp < groups - 1
     below_buf, above_buf = held[cycle - 1], held[cycle]
+    level, sends = schedule()
+    send_index = {item: k for k, item in enumerate(sends)}
 
     def buf(t):
-        return held[t - 1]
-
-    def copy_to(src, dst, send_index, recv, device):
+        return own_ref if t == 0 else held[t - 1]
+
+    def quarter(ref, q):
+        return ref.at[pl.ds(q * part, part)]
+
+    def link(t, q, d):
         return pltpu.make_async_remote_copy(
-            src_ref=src,
+            src_ref=quarter(buf(t), q),
+            dst_ref=quarter(buf(t ^ d), q),
+            send_sem=send_sem.at[send_index[(t, q, d)]],
+            recv_sem=recv_sem.at[t ^ d, q],
+            device_id=(grp, me ^ d),
+            device_id_type=MESH,
+        )
+
+    def arrival(t, q):
+        return pltpu.make_async_remote_copy(
+            src_ref=quarter(own_ref, q),
+            dst_ref=quarter(buf(t), q),
+            send_sem=side_send.at[0],
+            recv_sem=recv_sem.at[t, q],
+            device_id=(grp, me),
+            device_id_type=MESH,
+        )
+
+    def side(k, device):
+        dst = below_buf if k == 0 else above_buf
+        return pltpu.make_async_remote_copy(
+            src_ref=own_ref,
             dst_ref=dst,
-            send_sem=send_sem.at[send_index],
-            recv_sem=recv,
+            send_sem=side_send.at[k],
+            recv_sem=side_recv.at[k],
             device_id=device,
             device_id_type=MESH,
         )
 
-    def direct(k, t):
-        return copy_to(own_ref, buf(t), k, recv_full.at[k], (grp, me ^ t))
-
-    def relay(k, slot, peer_t, lower):
-        part = pl.ds(0, half) if lower else pl.ds(half, half)
-        dest = slot | peer_t
-        recv = recv_a if lower else recv_b
-        return copy_to(buf(slot).at[part], buf(dest).at[part], 8 + k, recv.at[dest], (grp, me ^ peer_t))
-
-    def side(k, device):
-        dst = below_buf if k == 0 else above_buf
-        return copy_to(own_ref, dst, 6 + k, recv_side.at[k], device)
-
     barrier = pltpu.get_barrier_semaphore()
-    for t in DIRECT:
-        pl.semaphore_signal(barrier, inc=1, device_id=(grp, me ^ t), device_id_type=MESH)
+    for d in NEIGHBOURS:
+        pl.semaphore_signal(barrier, inc=1, device_id=(grp, me ^ d), device_id_type=MESH)
 
     @pl.when(has_below)
     def _():
@@ -71,9 +130,13 @@
     def _():
         pl.semaphore_signal(barrier, inc=1, device_id=(grp + 1, me), device_id_type=MESH)
 
-    expected = len(DIRECT) + has_below.astype(jnp.int32) + has_above.astype(jnp.int32)
+    expected = len(NEIGHBOURS) + has_below.astype(jnp.int32) + has_above.astype(jnp.int32)
     pl.semaphore_wait(barrier, expected)
 
+    for t, q, d in sends:
+        if t == 0:
+            link(t, q, d).start()
+
     @pl.when(has_above)
     def _():
         side(0, (grp + 1, me)).start()
@@ -82,29 +145,24 @@
     def _():
         side(1, (grp - 1, me)).start()
 
-    for k, t in enumerate(DIRECT):
-        direct(k, t).start()
-
-    relays = []
-    for k, t in enumerate(DIRECT):
-        onward = (4, 12, 8) if t < RING else (1, 3, 2)
-        relays.append([(len(relays) * 3 + i, t, p, t < RING) for i, p in enumerate(onward)])
-
+    top = max(level.values())
     steps = [("own", 0), ("below", nsrc - 2), ("above", nsrc - 1)]
-    steps += [("direct", k) for k in range(len(DIRECT))]
-    steps += [("relayed", t) for t in relayed_slots()]
+    for lv in range(1, top + 1):
+        ready = [t for t in range(1, cycle) if max(level[(t, q)] for q in range(QUARTERS)) == lv]
+        steps.append(("arrive", lv))
+        steps += [("slot", t) for t in ready]
+
+    compute_steps = [s for s in steps if s[0] != "arrive"]
 
     def source_of(kind, t):
         if kind == "own":
             return me
-        if kind == "direct":
-            return me ^ DIRECT[t]
-        if kind == "relayed":
+        if kind == "slot":
             return me ^ t
         return t
 
-    def ham_copy(step, slot):
-        kind, t = steps[step]
+    def ham_copy(i, slot):
+        kind, t = compute_steps[i]
         return pltpu.make_async_copy(
             ham_hbm.at[:, source_of(kind, t)], ham_buf.at[slot], ham_sem.at[slot]
         )
@@ -112,13 +170,19 @@
     out_ref[...] = jnp.zeros_like(out_ref)
     ham_copy(0, 0).start()
 
-    for step, (kind, t) in enumerate(steps):
-        slot = step % 2
+    i = 0
+    for kind, t in steps:
+        if kind == "arrive":
+            for (slot_t, q), v in sorted(level.items()):
+                if v == t:
+                    arrival(slot_t, q).wait_recv()
+                    for d in forwards(slot_t, q):
+                        link(slot_t, q, d).start()
+            continue
+        slot = i % 2
         if kind == "own":
             data = own_ref
-        elif kind == "direct":
-            data = buf(DIRECT[t])
-        elif kind == "relayed":
+        elif kind == "slot":
             data = buf(t)
         elif kind == "below":
             data = below_buf
@@ -126,15 +190,8 @@
             data = above_buf
         source = source_of(kind, t)
 
-        def work(data=data, source=source, slot=slot, kind=kind, t=t):
-            if kind == "direct":
-                direct(t, DIRECT[t]).wait_recv()
-                for k, slot_t, peer_t, lower in relays[t]:
-                    relay(k, slot_t, peer_t, lower).start()
-            elif kind == "relayed":
-                copy_to(own_ref.at[pl.ds(0, half)], buf(t).at[pl.ds(0, half)], 0, recv_a.at[t], (grp, me)).wait_recv()
-                copy_to(own_ref.at[pl.ds(half, half)], buf(t).at[pl.ds(half, half)], 0, recv_b.at[t], (grp, me)).wait_recv()
-            elif kind == "below":
+        def work(data=data, source=source, slot=slot, kind=kind):
+            if kind == "below":
                 side(0, (grp, me)).wait_recv()
             elif kind == "above":
                 side(1, (grp, me)).wait_recv()
@@ -150,21 +207,19 @@
 
             lax.fori_loop(0, shard_blocks, row, 0, unroll=True)
 
-        ham_copy(step, slot).wait()
-        if step + 1 < len(steps):
-            ham_copy(step + 1, 1 - slot).start()
+        ham_copy(i, slot).wait()
+        if i + 1 < len(compute_steps):
+            ham_copy(i + 1, 1 - slot).start()
         if kind == "below":
             pl.when(has_below)(work)
         elif kind == "above":
             pl.when(has_above)(work)
         else:
             work()
-
-    for k, t in enumerate(DIRECT):
-        direct(k, t).wait_send()
-    for group_of in relays:
-        for k, slot_t, peer_t, lower in group_of:
-            relay(k, slot_t, peer_t, lower).wait_send()
+        i += 1
+
+    for t, q, d in sends:
+        link(t, q, d).wait_send()
 
     @pl.when(has_above)
     def _():
@@ -196,10 +251,9 @@
         + [
             pltpu.VMEM((2, shard_blocks, block_size, width), hamiltonian.dtype),
             pltpu.SemaphoreType.DMA((2,)),
-            pltpu.SemaphoreType.DMA((8 + 18,)),
-            pltpu.SemaphoreType.DMA((len(DIRECT),)),
-            pltpu.SemaphoreType.DMA((cycle,)),
-            pltpu.SemaphoreType.DMA((cycle,)),
+            pltpu.SemaphoreType.DMA((len(schedule()[1]),)),
+            pltpu.SemaphoreType.DMA((cycle, QUARTERS)),
+            pltpu.SemaphoreType.DMA((2,)),
             pltpu.SemaphoreType.DMA((2,)),
         ],
         compiler_params=pltpu.CompilerParams(

time: 141 us -> 132 us (0.936)
  Pallas kernels: 108 us -> 99.4 us
    pallas_call x2, Pallas kernels: 75.3 us -> 68 us  [couple_all(): pl.pallas_call(functools.partial(coupling_kernel, groups), out_shape=jax....]
where the time goes in v8:
time: 132 us; the launch traced here: 131 us
  Pallas kernels  99.4 us (75%)
  other arithmetic  24.6 us (19%)
  matrix products  3.01 us (2%)
  local copies, waits for them, and re-layouts  2.92 us (2%)
    pallas_call x2, Pallas kernels, couple_all(): pl.pallas_call(functools.partial(coupling_kernel, groups), out_shape=jax....  68 us
    pallas_call x1, Pallas kernels, summed_over_mesh(): pl.pallas_call(functools.partial(gram_kernel, stages), out_shape=jax.Shap...  31.4 us
    another operation x3, other arithmetic, on_device(): lower = jnp.linalg.cholesky(gram)  12.4 us
    another operation x1, other arithmetic, on_device(): lax.linalg.triangular_solve(lower, flat, left_side=False, lower=True, tra...  9.81 us

profile of v8, /device:TPU:1, one launch (start us, length us, event | category | flops | bytes accessed | tf_op | source)
XLA Modules:
  0.0 130.7 jit_solution(9472158016051812377)
XLA Ops:
  0.6 0.0 copy-start
  0.6 0.0 copy-start.1
  0.6 1.1 convert_element_type.6.own_ref
  1.8 1.0 copy.9
  2.8 0.1 reshape.24.index_ref
  2.9 35.0 %shard_map.59 = f32[16,64,128]{2,1,0:T(8,128)S(1)} custom-call(s32[1152]{0:T(1024)S(1)} %reshape.24.index_ref, bf16[16,64,128]{2,1,0:T(8,128)(2,1)S(1)} %convert_element_type.6.own_ref, bf16[16,18,64,256]{3,2,1,0:T(8,128)(2,1)} %ham_hbm.3), custom_call_target="tpu_custom_call" | custom-call | flops 1207959552 | bytes 9437184 | tf_op jit(solution)/shard_map/pallas_call | solution.py:241
  37.9 0.0 copy-done.1
  37.9 0.1 mul.28
  38.0 0.0 copy-done
  38.0 0.2 multiply_convert_fusion.own_ref
  38.2 33.0 %shard_map.60 = f32[16,64,128]{2,1,0:T(8,128)S(1)} custom-call(s32[1152]{0:T(1024)S(1)} %reshape.24.index_ref, bf16[16,64,128]{2,1,0:T(8,128)(2,1)S(1)} %multiply_convert_fusion.own_ref, bf16[16,18,64,256]{3,2,1,0:T(8,128)(2,1)} %ham_hbm.3), custom_call_target="tpu_custom_call" | custom-call | flops 1207959552 | bytes 9437184 | tf_op jit(solution)/shard_map/pallas_call | solution.py:241
  71.3 0.3 add_subtract_fusion
  71.6 1.6 %convolution_bitcast_fusion.gram_ref = f32[128,128]{1,0:T(8,128)} fusion(f32[16,64,128]{2,1,0:T(8,128)S(1)} %add_subtract_fusion), kind=kOutput, calls=%fused_computation | convolution fusion | flops 201326592 | bytes 589824 | tf_op jit(solution)/shard_map/dot_general | solution.py:357
  73.2 31.4 %shard_map.61 = f32[128,128]{1,0:T(8,128)} custom-call(f32[128,128]{1,0:T(8,128)} %convolution_bitcast_fusion.gram_ref), custom_call_target="tpu_custom_call" | custom-call | tf_op jit(solution)/shard_map/pallas_call | solution.py:330
  104.6 0.9 copy.10
  105.6 0.1 copy.11
  105.7 11.7 %cholesky.16 = f32[128,128]{1,0:T(8,128)S(1)} custom-call(f32[128,128]{1,0:T(8,128)S(1)} %fusion.2), custom_call_target="Cholesky" | custom-call | tf_op jit(solution)/shard_map/jit(cholesky)/cholesky | solution.py:359
  117.5 0.6 compare_reduce_fusion
  118.1 0.7 fusion.3
  118.8 9.8 %custom-call.6 = f32[1,128,128]{1,2,0:T(8,128)S(1)} custom-call(f32[1,128,128]{2,1,0:T(8,128)S(1)} %get-tuple-element.7), custom_call_target="InvertDiagBlocksLowerTriangular" | custom-call | tf_op jit(solution)/shard_map/triangular_solve | solution.py:360
  128.6 1.4 %fusion = f32[1024,128]{1,0:T(8,128)} fusion(f32[1024,128]{1,0:T(8,128)S(1)} %bitcast.18, f32[1,128,128]{1,2,0:T(8,128)S(1)} %custom-call.6), kind=kOutput, calls=%fused_computation.4 | convolution fusion | flops 201326592 | bytes 1114112 | tf_op jit(solution)/shard_map/triangular_solve | solution.py:360
  129.9 0.7 copy.12
  (4 shorter events, 0.1 us)
Async XLA Ops:
  0.6 37.4 %copy-start = (f32[1024,128]{1,0:T(8,128)S(1)}, f32[1024,128]{1,0:T(8,128)}, u32[]{:S(2)}) copy-start(f32[1024,128]{1,0:T(8,128)} %param.7) | copy-start | bytes 1572868
  0.6 37.3 %copy-start.1 = (f32[1024]{0:T(1024)S(1)}, f32[1024]{0:T(1024)}, u32[]{:S(2)}) copy-start(f32[1024]{0:T(1024)} %param.6) | copy-start | bytes 12292

commit v9 on v8

--- a/solution.py
+++ b/solution.py
@@ -197,8 +197,7 @@
                 side(1, (grp, me)).wait_recv()
 
             def row(r, carry):
-                base = (r * nsrc + source) * per_source
-                blocks = [data[index_ref[base + j]] for j in range(per_source)]
+                blocks = [data[index_ref[(r * per_source + j) * nsrc + source]] for j in range(per_source)]
                 picked = jnp.concatenate(blocks, axis=0)
                 out_ref[r] += jnp.dot(
                     ham_buf[slot, r], picked, preferred_element_type=jnp.float32
@@ -345,7 +344,7 @@
     shard_blocks = hamiltonian.shape[0]
     block_size = hamiltonian.shape[2]
     states = trial_slab.shape[1]
-    index = block_columns.reshape(-1)
+    index = jnp.transpose(block_columns, (0, 2, 1)).reshape(-1)
     start_slab = trial_slab.reshape(shard_blocks, block_size, states)
     weights = potential.reshape(shard_blocks, block_size, 1)
     coupled_start = couple_all(hamiltonian, index, start_slab.astype(jnp.bfloat16))
@@ -354,9 +353,9 @@
     filtered = coupled_next + weights * filtered_once - start_slab
     flat = filtered.reshape(shard_blocks * block_size, states)
     rows_total = flat.shape[0] * lax.axis_size("group") * lax.axis_size("blk")
-    local_gram = jnp.dot(flat.T, flat, precision=precise)
-    gram = summed_over_mesh(local_gram) / rows_total
-    lower = jnp.linalg.cholesky(gram)
+    local_gram = jnp.dot(flat.T, flat, precision=precise) * (1.0 / rows_total)
+    gram = summed_over_mesh(local_gram)
+    lower = lax.linalg.cholesky(gram, symmetrize_input=False)
     ortho_slab = lax.linalg.triangular_solve(
         lower, flat, left_side=False, lower=True, transpose_a=True
     )

time: 132 us -> 132 us (level)
  no operation moved by 1% of the time
where the time goes in v9:
time: 132 us; the launch traced here: 130 us
  Pallas kernels  99.4 us (75%)
  other arithmetic  25.4 us (19%)
  matrix products  3.01 us (2%)
  local copies, waits for them, and re-layouts  1.7 us (1%)
    pallas_call x2, Pallas kernels, couple_all(): pl.pallas_call(functools.partial(coupling_kernel, groups), out_shape=jax....  68 us
    pallas_call x1, Pallas kernels, summed_over_mesh(): pl.pallas_call(functools.partial(gram_kernel, stages), out_shape=jax.Shap...  31.4 us
    another operation x3, other arithmetic, on_device(): lower = lax.linalg.cholesky(gram, symmetrize_input=False)  13.2 us
    another operation x1, other arithmetic, on_device(): lax.linalg.triangular_solve(lower, flat, left_side=False, lower=True, tra...  9.81 us

profile of v9, /device:TPU:1, one launch (start us, length us, event | category | flops | bytes accessed | tf_op | source)
XLA Modules:
  0.0 130.2 jit_solution(14237286479778484812)
XLA Ops:
  0.6 0.0 copy-start
  0.6 0.0 copy-start.1
  0.6 1.1 convert_element_type.6.own_ref
  1.8 0.9 reshape.23.index_ref
  2.7 35.0 %shard_map.59 = f32[16,64,128]{2,1,0:T(8,128)S(1)} custom-call(s32[1152]{0:T(1024)S(1)} %reshape.23.index_ref, bf16[16,64,128]{2,1,0:T(8,128)(2,1)S(1)} %convert_element_type.6.own_ref, bf16[16,18,64,256]{3,2,1,0:T(8,128)(2,1)} %ham_hbm.3), custom_call_target="tpu_custom_call" | custom-call | flops 1207959552 | bytes 9437184 | tf_op jit(solution)/shard_map/pallas_call | solution.py:240
  37.7 0.0 copy-done.1
  37.7 0.1 mul.34
  37.8 0.0 copy-done
  37.8 0.2 multiply_convert_fusion.own_ref
  38.0 33.1 %shard_map.60 = f32[16,64,128]{2,1,0:T(8,128)S(1)} custom-call(s32[1152]{0:T(1024)S(1)} %reshape.23.index_ref, bf16[16,64,128]{2,1,0:T(8,128)(2,1)S(1)} %multiply_convert_fusion.own_ref, bf16[16,18,64,256]{3,2,1,0:T(8,128)(2,1)} %ham_hbm.3), custom_call_target="tpu_custom_call" | custom-call | flops 1207959552 | bytes 9437184 | tf_op jit(solution)/shard_map/pallas_call | solution.py:240
  71.1 0.3 add_subtract_fusion
  71.4 1.6 %fusion.gram_ref = f32[128,128]{1,0:T(8,128)} fusion(f32[16,64,128]{2,1,0:T(8,128)S(1)} %add_subtract_fusion), kind=kOutput, calls=%fused_computation.1 | convolution fusion | flops 201342976 | bytes 589824 | tf_op jit(solution)/shard_map/dot_general | solution.py:356
  73.0 31.4 %shard_map.61 = f32[128,128]{1,0:T(8,128)} custom-call(f32[128,128]{1,0:T(8,128)} %fusion.gram_ref), custom_call_target="tpu_custom_call" | custom-call | tf_op jit(solution)/shard_map/pallas_call | solution.py:329
  104.4 12.5 %cholesky.16 = f32[128,128]{1,0:T(8,128)S(1)} custom-call(f32[128,128]{1,0:T(8,128)} %shard_map.61), custom_call_target="Cholesky" | custom-call | tf_op jit(solution)/shard_map/cholesky | solution.py:358
  117.0 0.6 compare_reduce_fusion
  117.7 0.7 fusion.3
  118.3 9.8 %custom-call.5 = f32[1,128,128]{1,2,0:T(8,128)S(1)} custom-call(f32[1,128,128]{2,1,0:T(8,128)S(1)} %get-tuple-element.5), custom_call_target="InvertDiagBlocksLowerTriangular" | custom-call | tf_op jit(solution)/shard_map/triangular_solve | solution.py:359
  128.1 1.4 %fusion.1 = f32[1024,128]{1,0:T(8,128)} fusion(f32[1024,128]{1,0:T(8,128)S(1)} %bitcast.17, f32[1,128,128]{1,2,0:T(8,128)S(1)} %custom-call.5), kind=kOutput, calls=%fused_computation.5 | convolution fusion | flops 201326592 | bytes 1114112 | tf_op jit(solution)/shard_map/triangular_solve | solution.py:359
  129.5 0.7 copy.6
  (2 shorter events, 0.0 us)
Async XLA Ops:
  0.6 37.1 %copy-start = (f32[1024,128]{1,0:T(8,128)S(1)}, f32[1024,128]{1,0:T(8,128)}, u32[]{:S(2)}) copy-start(f32[1024,128]{1,0:T(8,128)} %param.7) | copy-start | bytes 1572868
  0.6 37.1 %copy-start.1 = (f32[1024]{0:T(1024)S(1)}, f32[1024]{0:T(1024)}, u32[]{:S(2)}) copy-start(f32[1024]{0:T(1024)} %param.6) | copy-start | bytes 12292

commit v10 on v9

--- a/solution.py
+++ b/solution.py
@@ -66,10 +66,10 @@
     return level, sends
 
 
-def coupling_kernel(groups, index_ref, own_ref, ham_hbm, out_ref, *scratch):
+def coupling_kernel(groups, index_ref, start_ref, scaled_ref, ham_hbm, once_ref, next_ref, *scratch):
     cycle = RING * RING
-    held = scratch[: cycle + 1]
-    ham_buf, ham_sem, send_sem, recv_sem, side_send, side_recv = scratch[cycle + 1 :]
+    held_sets = (scratch[: cycle + 1], scratch[cycle + 1 : 2 * cycle + 2])
+    rounded, ham_buf, ham_sem, send_sem, recv_sem, side_send, side_recv = scratch[2 * cycle + 2 :]
     shard_blocks, nsrc, block_size, width = ham_hbm.shape
     per_source = width // block_size
     part = shard_blocks // QUARTERS
@@ -77,43 +77,44 @@
     grp = lax.axis_index("group")
     has_below = grp > 0
     has_above = grp < groups - 1
-    below_buf, above_buf = held[cycle - 1], held[cycle]
     level, sends = schedule()
     send_index = {item: k for k, item in enumerate(sends)}
-
-    def buf(t):
-        return own_ref if t == 0 else held[t - 1]
+    owns = (start_ref, rounded)
+    outs = (once_ref, next_ref)
+
+    def buf(p, t):
+        return owns[p] if t == 0 else held_sets[p][t - 1]
 
     def quarter(ref, q):
         return ref.at[pl.ds(q * part, part)]
 
-    def link(t, q, d):
+    def link(p, t, q, d):
         return pltpu.make_async_remote_copy(
-            src_ref=quarter(buf(t), q),
-            dst_ref=quarter(buf(t ^ d), q),
-            send_sem=send_sem.at[send_index[(t, q, d)]],
-            recv_sem=recv_sem.at[t ^ d, q],
+            src_ref=quarter(buf(p, t), q),
+            dst_ref=quarter(buf(p, t ^ d), q),
+            send_sem=send_sem.at[p, send_index[(t, q, d)]],
+            recv_sem=recv_sem.at[p, t ^ d, q],
             device_id=(grp, me ^ d),
             device_id_type=MESH,
         )
 
-    def arrival(t, q):
+    def arrival(p, t, q):
         return pltpu.make_async_remote_copy(
-            src_ref=quarter(own_ref, q),
-            dst_ref=quarter(buf(t), q),
-            send_sem=side_send.at[0],
-            recv_sem=recv_sem.at[t, q],
+            src_ref=quarter(owns[p], q),
+            dst_ref=quarter(buf(p, t), q),
+            send_sem=side_send.at[p, 0],
+            recv_sem=recv_sem.at[p, t, q],
             device_id=(grp, me),
             device_id_type=MESH,
         )
 
-    def side(k, device):
-        dst = below_buf if k == 0 else above_buf
+    def side(p, k, device):
+        dst = held_sets[p][cycle - 1 + k]
         return pltpu.make_async_remote_copy(
-            src_ref=own_ref,
+            src_ref=owns[p],
             dst_ref=dst,
-            send_sem=side_send.at[k],
-            recv_sem=side_recv.at[k],
+            send_sem=side_send.at[p, k],
+            recv_sem=side_recv.at[p, k],
             device_id=device,
             device_id_type=MESH,
         )
@@ -133,26 +134,30 @@
     expected = len(NEIGHBOURS) + has_below.astype(jnp.int32) + has_above.astype(jnp.int32)
     pl.semaphore_wait(barrier, expected)
 
-    for t, q, d in sends:
-        if t == 0:
-            link(t, q, d).start()
-
-    @pl.when(has_above)
-    def _():
-        side(0, (grp + 1, me)).start()
-
-    @pl.when(has_below)
-    def _():
-        side(1, (grp - 1, me)).start()
+    def send_own(p):
+        for t, q, d in sends:
+            if t == 0:
+                link(p, t, q, d).start()
+
+        @pl.when(has_above)
+        def _():
+            side(p, 0, (grp + 1, me)).start()
+
+        @pl.when(has_below)
+        def _():
+            side(p, 1, (grp - 1, me)).start()
 
     top = max(level.values())
-    steps = [("own", 0), ("below", nsrc - 2), ("above", nsrc - 1)]
-    for lv in range(1, top + 1):
-        ready = [t for t in range(1, cycle) if max(level[(t, q)] for q in range(QUARTERS)) == lv]
-        steps.append(("arrive", lv))
-        steps += [("slot", t) for t in ready]
-
-    compute_steps = [s for s in steps if s[0] != "arrive"]
+    steps = []
+    for p in range(2):
+        steps += [(p, "send", 0), (p, "own", 0), (p, "below", nsrc - 2), (p, "above", nsrc - 1)]
+        for lv in range(1, top + 1):
+            ready = [t for t in range(1, cycle) if max(level[(t, q)] for q in range(QUARTERS)) == lv]
+            steps.append((p, "arrive", lv))
+            steps += [(p, "slot", t) for t in ready]
+        steps.append((p, "finish", 0))
+
+    compute_steps = [x for x in steps if x[1] in ("own", "below", "above", "slot")]
 
     def source_of(kind, t):
         if kind == "own":
@@ -162,39 +167,49 @@
         return t
 
     def ham_copy(i, slot):
-        kind, t = compute_steps[i]
+        p, kind, t = compute_steps[i]
         return pltpu.make_async_copy(
             ham_hbm.at[:, source_of(kind, t)], ham_buf.at[slot], ham_sem.at[slot]
         )
 
-    out_ref[...] = jnp.zeros_like(out_ref)
+    once_ref[...] = jnp.zeros_like(once_ref)
+    next_ref[...] = jnp.zeros_like(next_ref)
     ham_copy(0, 0).start()
 
     i = 0
-    for kind, t in steps:
+    for p, kind, t in steps:
+        if kind == "send":
+            send_own(p)
+            continue
         if kind == "arrive":
             for (slot_t, q), v in sorted(level.items()):
                 if v == t:
-                    arrival(slot_t, q).wait_recv()
+                    arrival(p, slot_t, q).wait_recv()
                     for d in forwards(slot_t, q):
-                        link(slot_t, q, d).start()
+                        link(p, slot_t, q, d).start()
+            continue
+        if kind == "finish":
+            if p == 0:
+                once_ref[...] = 0.5 * (once_ref[...] + scaled_ref[...])
+                rounded[...] = once_ref[...].astype(rounded.dtype)
             continue
         slot = i % 2
         if kind == "own":
-            data = own_ref
+            data = owns[p]
         elif kind == "slot":
-            data = buf(t)
+            data = buf(p, t)
         elif kind == "below":
-            data = below_buf
+            data = held_sets[p][cycle - 1]
         else:
-            data = above_buf
+            data = held_sets[p][cycle]
         source = source_of(kind, t)
-
-        def work(data=data, source=source, slot=slot, kind=kind):
+        out_ref = outs[p]
+
+        def work(data=data, source=source, slot=slot, kind=kind, p=p, out_ref=out_ref):
             if kind == "below":
-                side(0, (grp, me)).wait_recv()
+                side(p, 0, (grp, me)).wait_recv()
             elif kind == "above":
-                side(1, (grp, me)).wait_recv()
+                side(p, 1, (grp, me)).wait_recv()
 
             def row(r, carry):
                 blocks = [data[index_ref[(r * per_source + j) * nsrc + source]] for j in range(per_source)]
@@ -217,51 +232,51 @@
             work()
         i += 1
 
-    for t, q, d in sends:
-        link(t, q, d).wait_send()
-
-    @pl.when(has_above)
-    def _():
-        side(0, (grp + 1, me)).wait_send()
-
-    @pl.when(has_below)
-    def _():
-        side(1, (grp - 1, me)).wait_send()
-
-
-def couple_all(hamiltonian, index, rounded):
+    for p in range(2):
+        for t, q, d in sends:
+            link(p, t, q, d).wait_send()
+
+        @pl.when(has_above)
+        def _():
+            side(p, 0, (grp + 1, me)).wait_send()
+
+        @pl.when(has_below)
+        def _():
+            side(p, 1, (grp - 1, me)).wait_send()
+
+
+def couple_both(hamiltonian, index, start_round, scaled):
     shard_blocks, nsrc, block_size, width = hamiltonian.shape
-    states = rounded.shape[2]
+    states = start_round.shape[2]
     cycle = lax.axis_size("blk")
     assert cycle == RING * RING
     groups = lax.axis_size("group")
-    slab = pltpu.VMEM(rounded.shape, rounded.dtype)
-    flops = 2 * shard_blocks * nsrc * block_size * width * states
+    slab = pltpu.VMEM(start_round.shape, start_round.dtype)
+    flops = 4 * shard_blocks * nsrc * block_size * width * states
+    result = jax.ShapeDtypeStruct((shard_blocks, block_size, states), jnp.float32)
+    vmem = pl.BlockSpec(memory_space=pltpu.VMEM)
     return pl.pallas_call(
         functools.partial(coupling_kernel, groups),
-        out_shape=jax.ShapeDtypeStruct((shard_blocks, block_size, states), jnp.float32),
-        in_specs=[
-            pl.BlockSpec(memory_space=pltpu.SMEM),
-            pl.BlockSpec(memory_space=pltpu.VMEM),
-            pl.BlockSpec(memory_space=pl.ANY),
-        ],
-        out_specs=pl.BlockSpec(memory_space=pltpu.VMEM),
-        scratch_shapes=[slab] * (cycle + 1)
+        out_shape=(result, result),
+        in_specs=[pl.BlockSpec(memory_space=pltpu.SMEM), vmem, vmem, pl.BlockSpec(memory_space=pl.ANY)],
+        out_specs=(vmem, vmem),
+        scratch_shapes=[slab] * (2 * cycle + 2)
         + [
+            slab,
             pltpu.VMEM((2, shard_blocks, block_size, width), hamiltonian.dtype),
             pltpu.SemaphoreType.DMA((2,)),
-            pltpu.SemaphoreType.DMA((len(schedule()[1]),)),
-            pltpu.SemaphoreType.DMA((cycle, QUARTERS)),
-            pltpu.SemaphoreType.DMA((2,)),
-            pltpu.SemaphoreType.DMA((2,)),
+            pltpu.SemaphoreType.DMA((2, len(schedule()[1]))),
+            pltpu.SemaphoreType.DMA((2, cycle, QUARTERS)),
+            pltpu.SemaphoreType.DMA((2, 2)),
+            pltpu.SemaphoreType.DMA((2, 2)),
         ],
         compiler_params=pltpu.CompilerParams(
             collective_id=0, has_side_effects=True, vmem_limit_bytes=48 * 1024 * 1024
         ),
         cost_estimate=pl.CostEstimate(
-            flops=flops, transcendentals=0, bytes_accessed=hamiltonian.size * 2
+            flops=flops, transcendentals=0, bytes_accessed=hamiltonian.size * 4
         ),
-    )(index, rounded, hamiltonian)
+    )(index, start_round, scaled, hamiltonian)
 
 
 def gram_kernel(stages, gram_ref, out_ref, arrived, send_sem, recv_sem):
@@ -347,9 +362,9 @@
     index = jnp.transpose(block_columns, (0, 2, 1)).reshape(-1)
     start_slab = trial_slab.reshape(shard_blocks, block_size, states)
     weights = potential.reshape(shard_blocks, block_size, 1)
-    coupled_start = couple_all(hamiltonian, index, start_slab.astype(jnp.bfloat16))
-    filtered_once = 0.5 * (coupled_start + weights * start_slab)
-    coupled_next = couple_all(hamiltonian, index, filtered_once.astype(jnp.bfloat16))
+    filtered_once, coupled_next = couple_both(
+        hamiltonian, index, start_slab.astype(jnp.bfloat16), weights * start_slab
+    )
     filtered = coupled_next + weights * filtered_once - start_slab
     flat = filtered.reshape(shard_blocks * block_size, states)
     rows_total = flat.shape[0] * lax.axis_size("group") * lax.axis_size("blk")

time: 132 us -> 131 us (level)
  Pallas kernels: 99.4 us -> 96.8 us
    pallas_call x2 -> x1, Pallas kernels: 68 us -> 65.2 us  [couple_both(): pl.pallas_call(functools.partial(coupling_kernel, groups), out_shape=(res...]
where the time goes in v10:
time: 131 us; the launch traced here: 129 us
  Pallas kernels  96.8 us (74%)
  other arithmetic  26.2 us (20%)
  matrix products  3.01 us (2%)
  local copies, waits for them, and re-layouts  2.44 us (2%)
    pallas_call x1, Pallas kernels, couple_both(): pl.pallas_call(functools.partial(coupling_kernel, groups), out_shape=(res...  65.2 us
    pallas_call x1, Pallas kernels, summed_over_mesh(): pl.pallas_call(functools.partial(gram_kernel, stages), out_shape=jax.Shap...  31.6 us
    another operation x3, other arithmetic, on_device(): lower = lax.linalg.cholesky(gram, symmetrize_input=False)  13.2 us
    another operation x1, other arithmetic, on_device(): lax.linalg.triangular_solve(lower, flat, left_side=False, lower=True, tra...  9.81 us

profile of v10, /device:TPU:1, one launch (start us, length us, event | category | flops | bytes accessed | tf_op | source)
XLA Modules:
  0.0 129.2 jit_solution(4452507478337811464)
XLA Ops:
  0.6 0.0 copy-start
  0.6 0.8 mul.22
  1.5 0.9 reshape.23.index_ref
  2.4 1.1 convert_element_type.3.start_ref
  3.4 1.2 broadcast_multiply_fusion.scaled_ref
  4.7 65.2 %shard_map.59 = (f32[16,64,128]{2,1,0:T(8,128)S(1)}, f32[16,64,128]{2,1,0:T(8,128)S(1)}) custom-call(s32[1152]{0:T(1024)S(1)} %reshape.23.index_ref, bf16[16,64,128]{2,1,0:T(8,128)(2,1)S(1)} %convert_element_type.3.start_ref, f32[16,64,128]{2,1,0:T(8,128)S(1)} %broadcast_multiply_fusion.scaled_ref, bf16[16,18,64,256]{3,2,1,0:T(8,128)(2,1)} %ham_hbm.1), custom_call_target="tpu_custom_call" | custom-call | flops 2415919104 | bytes 18874368 | tf_op jit(solution)/shard_map/pallas_call | solution.py:258
  69.9 0.0 copy-done
  69.9 0.2 add_subtract_fusion
  70.1 1.6 %fusion.gram_ref = f32[128,128]{1,0:T(8,128)} fusion(f32[16,64,128]{2,1,0:T(8,128)S(1)} %add_subtract_fusion), kind=kOutput, calls=%fused_computation.1 | convolution fusion | flops 201342976 | bytes 589824 | tf_op jit(solution)/shard_map/dot_general | solution.py:371
  71.8 31.6 %shard_map.60 = f32[128,128]{1,0:T(8,128)} custom-call(f32[128,128]{1,0:T(8,128)} %fusion.gram_ref), custom_call_target="tpu_custom_call" | custom-call | tf_op jit(solution)/shard_map/pallas_call | solution.py:344
  103.4 12.5 %cholesky.16 = f32[128,128]{1,0:T(8,128)S(1)} custom-call(f32[128,128]{1,0:T(8,128)} %shard_map.60), custom_call_target="Cholesky" | custom-call | tf_op jit(solution)/shard_map/cholesky | solution.py:373
  115.9 0.6 compare_reduce_fusion
  116.6 0.7 fusion.3
  117.3 0.7 copy.6
  118.0 9.8 %custom-call.5 = f32[1,128,128]{1,2,0:T(8,128)S(1)} custom-call(f32[1,128,128]{2,1,0:T(8,128)S(1)} %get-tuple-element.9), custom_call_target="InvertDiagBlocksLowerTriangular" | custom-call | tf_op jit(solution)/shard_map/triangular_solve | solution.py:374
  127.8 1.4 %fusion.1 = f32[1024,128]{1,0:T(8,128)} fusion(f32[1024,128]{1,0:T(8,128)S(1)} %bitcast.17, f32[1,128,128]{1,2,0:T(8,128)S(1)} %custom-call.5), kind=kOutput, calls=%fused_computation.4 | convolution fusion | flops 201326592 | bytes 1114112 | tf_op jit(solution)/shard_map/triangular_solve | solution.py:374
  (1 shorter events, 0.0 us)
Async XLA Ops:
  0.6 69.3 %copy-start = (f32[1024,128]{1,0:T(8,128)S(1)}, f32[1024,128]{1,0:T(8,128)}, u32[]{:S(2)}) copy-start(f32[1024,128]{1,0:T(8,128)} %param.7) | copy-start | bytes 1572868

commit v11 on v10

--- a/solution.py
+++ b/solution.py
@@ -66,10 +66,10 @@
     return level, sends
 
 
-def coupling_kernel(groups, index_ref, start_ref, scaled_ref, ham_hbm, once_ref, next_ref, *scratch):
+def coupling_kernel(groups, index_ref, trial_ref, weight_ref, ham_hbm, once_ref, next_ref, *scratch):
     cycle = RING * RING
     held_sets = (scratch[: cycle + 1], scratch[cycle + 1 : 2 * cycle + 2])
-    rounded, ham_buf, ham_sem, send_sem, recv_sem, side_send, side_recv = scratch[2 * cycle + 2 :]
+    start_ref, rounded, ham_buf, ham_sem, send_sem, recv_sem, side_send, side_recv = scratch[2 * cycle + 2 :]
     shard_blocks, nsrc, block_size, width = ham_hbm.shape
     per_source = width // block_size
     part = shard_blocks // QUARTERS
@@ -119,6 +119,7 @@
             device_id_type=MESH,
         )
 
+    start_ref[...] = trial_ref[...].astype(start_ref.dtype)
     barrier = pltpu.get_barrier_semaphore()
     for d in NEIGHBOURS:
         pl.semaphore_signal(barrier, inc=1, device_id=(grp, me ^ d), device_id_type=MESH)
@@ -190,7 +191,7 @@
             continue
         if kind == "finish":
             if p == 0:
-                once_ref[...] = 0.5 * (once_ref[...] + scaled_ref[...])
+                once_ref[...] = 0.5 * (once_ref[...] + weight_ref[...] * trial_ref[...])
                 rounded[...] = once_ref[...].astype(rounded.dtype)
             continue
         slot = i % 2
@@ -245,13 +246,13 @@
             side(p, 1, (grp - 1, me)).wait_send()
 
 
-def couple_both(hamiltonian, index, start_round, scaled):
+def couple_both(hamiltonian, index, trial, weights):
     shard_blocks, nsrc, block_size, width = hamiltonian.shape
-    states = start_round.shape[2]
+    states = trial.shape[2]
     cycle = lax.axis_size("blk")
     assert cycle == RING * RING
     groups = lax.axis_size("group")
-    slab = pltpu.VMEM(start_round.shape, start_round.dtype)
+    slab = pltpu.VMEM(trial.shape, jnp.bfloat16)
     flops = 4 * shard_blocks * nsrc * block_size * width * states
     result = jax.ShapeDtypeStruct((shard_blocks, block_size, states), jnp.float32)
     vmem = pl.BlockSpec(memory_space=pltpu.VMEM)
@@ -262,6 +263,7 @@
         out_specs=(vmem, vmem),
         scratch_shapes=[slab] * (2 * cycle + 2)
         + [
+            slab,
             slab,
             pltpu.VMEM((2, shard_blocks, block_size, width), hamiltonian.dtype),
             pltpu.SemaphoreType.DMA((2,)),
@@ -276,7 +278,7 @@
         cost_estimate=pl.CostEstimate(
             flops=flops, transcendentals=0, bytes_accessed=hamiltonian.size * 4
         ),
-    )(index, start_round, scaled, hamiltonian)
+    )(index, trial, weights, hamiltonian)
 
 
 def gram_kernel(stages, gram_ref, out_ref, arrived, send_sem, recv_sem):
@@ -362,9 +364,7 @@
     index = jnp.transpose(block_columns, (0, 2, 1)).reshape(-1)
     start_slab = trial_slab.reshape(shard_blocks, block_size, states)
     weights = potential.reshape(shard_blocks, block_size, 1)
-    filtered_once, coupled_next = couple_both(
-        hamiltonian, index, start_slab.astype(jnp.bfloat16), weights * start_slab
-    )
+    filtered_once, coupled_next = couple_both(hamiltonian, index, start_slab, weights)
     filtered = coupled_next + weights * filtered_once - start_slab
     flat = filtered.reshape(shard_blocks * block_size, states)
     rows_total = flat.shape[0] * lax.axis_size("group") * lax.axis_size("blk")

time: 131 us -> 130 us (level)
  other arithmetic: 26.2 us -> 23.9 us
  local copies, waits for them, and re-layouts: 2.44 us -> 3.83 us
where the time goes in v11:
time: 130 us; the launch traced here: 128 us
  Pallas kernels  96.7 us (74%)
  other arithmetic  23.9 us (18%)
  local copies, waits for them, and re-layouts  3.83 us (3%)
  matrix products  3.01 us (2%)
    pallas_call x1, Pallas kernels, couple_both(): pl.pallas_call(functools.partial(coupling_kernel, groups), out_shape=(res...  65.3 us
    pallas_call x1, Pallas kernels, summed_over_mesh(): pl.pallas_call(functools.partial(gram_kernel, stages), out_shape=jax.Shap...  31.4 us
    another operation x3, other arithmetic, on_device(): lower = lax.linalg.cholesky(gram, symmetrize_input=False)  13.2 us
    another operation x1, other arithmetic, on_device(): lax.linalg.triangular_solve(lower, flat, left_side=False, lower=True, tra...  9.81 us

profile of v11, /device:TPU:1, one launch (start us, length us, event | category | flops | bytes accessed | tf_op | source)
XLA Modules:
  0.0 128.2 jit_solution(4914829520668883879)
XLA Ops:
  0.6 0.0 copy-start.1
  0.6 0.0 copy-start.2
  0.7 1.1 reshape.30.weight_ref
  1.7 0.9 reshape.25.index_ref
  2.6 0.0 copy-start
  2.7 1.0 copy-done
  3.7 65.3 %shard_map.59 = (f32[16,64,128]{2,1,0:T(8,128)S(1)}, f32[16,64,128]{2,1,0:T(8,128)S(1)}) custom-call(s32[1152]{0:T(1024)S(1)} %reshape.25.index_ref, f32[16,64,128]{2,1,0:T(8,128)S(1)} %bitcast.17, f32[16,64,1]{2,1,0:T(8,128)S(1)} %reshape.30.weight_ref, bf16[16,18,64,256]{3,2,1,0:T(8,128)(2,1)} %ham_hbm.1), custom_call_target="tpu_custom_call" | custom-call | flops 2415919104 | bytes 18874368 | tf_op jit(solution)/shard_map/pallas_call | solution.py:259
  69.0 0.0 copy-done.2
  69.0 0.1 mul.16
  69.0 0.0 copy-done.1
  69.1 0.2 add_subtract_fusion
  69.3 1.6 %fusion.gram_ref = f32[128,128]{1,0:T(8,128)} fusion(f32[16,64,128]{2,1,0:T(8,128)S(1)} %add_subtract_fusion), kind=kOutput, calls=%fused_computation.1 | convolution fusion | flops 201342976 | bytes 589824 | tf_op jit(solution)/shard_map/dot_general | solution.py:371
  70.9 31.4 %shard_map.60 = f32[128,128]{1,0:T(8,128)} custom-call(f32[128,128]{1,0:T(8,128)} %fusion.gram_ref), custom_call_target="tpu_custom_call" | custom-call | tf_op jit(solution)/shard_map/pallas_call | solution.py:346
  102.3 12.5 %cholesky.16 = f32[128,128]{1,0:T(8,128)S(1)} custom-call(f32[128,128]{1,0:T(8,128)} %shard_map.60), custom_call_target="Cholesky" | custom-call | tf_op jit(solution)/shard_map/cholesky | solution.py:373
  114.9 0.6 compare_reduce_fusion
  115.6 0.7 fusion.3
  116.2 9.8 %custom-call.5 = f32[1,128,128]{1,2,0:T(8,128)S(1)} custom-call(f32[1,128,128]{2,1,0:T(8,128)S(1)} %get-tuple-element.11), custom_call_target="InvertDiagBlocksLowerTriangular" | custom-call | tf_op jit(solution)/shard_map/triangular_solve | solution.py:374
  126.1 1.4 %fusion.1 = f32[1024,128]{1,0:T(8,128)} fusion(f32[1024,128]{1,0:T(8,128)S(1)} %bitcast.19, f32[1,128,128]{1,2,0:T(8,128)S(1)} %custom-call.5), kind=kOutput, calls=%fused_computation.3 | convolution fusion | flops 201326592 | bytes 1114112 | tf_op jit(solution)/shard_map/triangular_solve | solution.py:374
  127.4 0.7 copy.8
  (1 shorter events, 0.0 us)
Async XLA Ops:
  0.6 68.4 %copy-start.1 = (f32[1024,128]{1,0:T(8,128)S(1)}, f32[1024,128]{1,0:T(8,128)}, u32[]{:S(2)}) copy-start(f32[1024,128]{1,0:T(8,128)} %param.7) | copy-start | bytes 1572868
  0.6 68.3 %copy-start.2 = (f32[1024]{0:T(1024)S(1)}, f32[1024]{0:T(1024)}, u32[]{:S(2)}) copy-start(f32[1024]{0:T(1024)} %param.6) | copy-start | bytes 12292
  2.6 1.0 copy-start

commit v12 on v11

--- a/solution.py
+++ b/solution.py
@@ -193,6 +193,8 @@
             if p == 0:
                 once_ref[...] = 0.5 * (once_ref[...] + weight_ref[...] * trial_ref[...])
                 rounded[...] = once_ref[...].astype(rounded.dtype)
+            else:
+                next_ref[...] = next_ref[...] + weight_ref[...] * once_ref[...] - trial_ref[...]
             continue
         slot = i % 2
         if kind == "own":
@@ -364,8 +366,7 @@
     index = jnp.transpose(block_columns, (0, 2, 1)).reshape(-1)
     start_slab = trial_slab.reshape(shard_blocks, block_size, states)
     weights = potential.reshape(shard_blocks, block_size, 1)
-    filtered_once, coupled_next = couple_both(hamiltonian, index, start_slab, weights)
-    filtered = coupled_next + weights * filtered_once - start_slab
+    filtered_once, filtered = couple_both(hamiltonian, index, start_slab, weights)
     flat = filtered.reshape(shard_blocks * block_size, states)
     rows_total = flat.shape[0] * lax.axis_size("group") * lax.axis_size("blk")
     local_gram = jnp.dot(flat.T, flat, precision=precise) * (1.0 / rows_total)

time: 130 us -> 130 us (level)
  no operation moved by 1% of the time
where the time goes in v12:
time: 130 us; the launch traced here: 129 us
  Pallas kernels  97.6 us (75%)
  other arithmetic  23.7 us (18%)
  local copies, waits for them, and re-layouts  3.69 us (3%)
  matrix products  3 us (2%)
    pallas_call x1, Pallas kernels, couple_both(): pl.pallas_call(functools.partial(coupling_kernel, groups), out_shape=(res...  66 us
    pallas_call x1, Pallas kernels, summed_over_mesh(): pl.pallas_call(functools.partial(gram_kernel, stages), out_shape=jax.Shap...  31.5 us
    another operation x3, other arithmetic, on_device(): lower = lax.linalg.cholesky(gram, symmetrize_input=False)  13.2 us
    another operation x1, other arithmetic, on_device(): lax.linalg.triangular_solve(lower, flat, left_side=False, lower=True, tra...  9.81 us

profile of v12, /device:TPU:1, one launch (start us, length us, event | category | flops | bytes accessed | tf_op | source)
XLA Modules:
  0.0 128.6 jit_solution(4579756272938531904)
XLA Ops:
  0.6 0.9 reshape.24.index_ref
  1.5 1.0 reshape.29.weight_ref
  2.6 0.0 copy-start
  2.6 1.0 copy-done
  3.6 66.0 %shard_map.59 = (f32[16,64,128]{2,1,0:T(8,128)}, f32[16,64,128]{2,1,0:T(8,128)S(1)}) custom-call(s32[1152]{0:T(1024)S(1)} %reshape.24.index_ref, f32[16,64,128]{2,1,0:T(8,128)S(1)} %bitcast.18, f32[16,64,1]{2,1,0:T(8,128)S(1)} %reshape.29.weight_ref, bf16[16,18,64,256]{3,2,1,0:T(8,128)(2,1)} %ham_hbm.1), custom_call_target="tpu_custom_call" | custom-call | flops 2415919104 | bytes 18874368 | tf_op jit(solution)/shard_map/pallas_call | solution.py:261
  69.7 1.6 %fusion.gram_ref = f32[128,128]{1,0:T(8,128)} fusion(f32[16,64,128]{2,1,0:T(8,128)S(1)} %get-tuple-element.3), kind=kOutput, calls=%fused_computation.1 | convolution fusion | flops 201342976 | bytes 589824 | tf_op jit(solution)/shard_map/dot_general | solution.py:372
  71.3 31.5 %shard_map.60 = f32[128,128]{1,0:T(8,128)} custom-call(f32[128,128]{1,0:T(8,128)} %fusion.gram_ref), custom_call_target="tpu_custom_call" | custom-call | tf_op jit(solution)/shard_map/pallas_call | solution.py:348
  102.8 12.5 %cholesky.16 = f32[128,128]{1,0:T(8,128)S(1)} custom-call(f32[128,128]{1,0:T(8,128)} %shard_map.60), custom_call_target="Cholesky" | custom-call | tf_op jit(solution)/shard_map/cholesky | solution.py:374
  115.4 0.6 compare_reduce_fusion
  116.1 0.7 fusion.3
  116.7 0.7 copy.8
  117.4 9.8 %custom-call.5 = f32[1,128,128]{1,2,0:T(8,128)S(1)} custom-call(f32[1,128,128]{2,1,0:T(8,128)S(1)} %get-tuple-element.9), custom_call_target="InvertDiagBlocksLowerTriangular" | custom-call | tf_op jit(solution)/shard_map/triangular_solve | solution.py:375
  127.3 1.4 %fusion.1 = f32[1024,128]{1,0:T(8,128)} fusion(f32[1024,128]{1,0:T(8,128)S(1)} %bitcast.17, f32[1,128,128]{1,2,0:T(8,128)S(1)} %custom-call.5), kind=kOutput, calls=%fused_computation.2 | convolution fusion | flops 201326592 | bytes 1114112 | tf_op jit(solution)/shard_map/triangular_solve | solution.py:375
  (1 shorter events, 0.0 us)
Async XLA Ops:
  2.6 1.0 copy-start

commit v13 on v12

--- a/solution.py
+++ b/solution.py
@@ -66,10 +66,10 @@
     return level, sends
 
 
-def coupling_kernel(groups, index_ref, trial_ref, weight_ref, ham_hbm, once_ref, next_ref, *scratch):
+def coupling_kernel(groups, scale, index_ref, trial_ref, weight_ref, ham_hbm, once_ref, next_ref, gram_ref, *scratch):
     cycle = RING * RING
     held_sets = (scratch[: cycle + 1], scratch[cycle + 1 : 2 * cycle + 2])
-    start_ref, rounded, ham_buf, ham_sem, send_sem, recv_sem, side_send, side_recv = scratch[2 * cycle + 2 :]
+    start_ref, rounded, ham_buf, ham_sem, send_sem, recv_sem, side_send, side_recv, arrived, g_send, g_recv = scratch[2 * cycle + 2 :]
     shard_blocks, nsrc, block_size, width = ham_hbm.shape
     per_source = width // block_size
     part = shard_blocks // QUARTERS
@@ -132,8 +132,24 @@
     def _():
         pl.semaphore_signal(barrier, inc=1, device_id=(grp + 1, me), device_id_type=MESH)
 
+    place = {"group": grp, "blk": me}
+    stages = [("blk", 0), ("blk", 2), ("group", 0), ("group", 2)]
+
+    def field(axis, shift):
+        return (place[axis] >> shift) % QUARTERS
+
+    def peer(axis, shift, position):
+        other = dict(place)
+        other[axis] = place[axis] + (position - field(axis, shift)) * (1 << shift)
+        return (other["group"], other["blk"])
+
+    for axis, shift in stages:
+        for m in range(1, QUARTERS):
+            pl.semaphore_signal(
+                barrier, inc=1, device_id=peer(axis, shift, field(axis, shift) ^ m), device_id_type=MESH
+            )
     expected = len(NEIGHBOURS) + has_below.astype(jnp.int32) + has_above.astype(jnp.int32)
-    pl.semaphore_wait(barrier, expected)
+    pl.semaphore_wait(barrier, expected + len(stages) * (QUARTERS - 1))
 
     def send_own(p):
         for t, q, d in sends:
@@ -195,6 +211,13 @@
                 rounded[...] = once_ref[...].astype(rounded.dtype)
             else:
                 next_ref[...] = next_ref[...] + weight_ref[...] * once_ref[...] - trial_ref[...]
+                local = jnp.zeros(gram_ref.shape, jnp.float32)
+                for r in range(shard_blocks):
+                    rows = next_ref[r]
+                    local = local + jnp.dot(
+                        rows.T, rows, precision=lax.Precision.HIGHEST, preferred_element_type=jnp.float32
+                    )
+                gram_ref[...] = local * scale
             continue
         slot = i % 2
         if kind == "own":
@@ -235,6 +258,41 @@
             work()
         i += 1
 
+    for k, (axis, shift) in enumerate(stages):
+        mine = field(axis, shift)
+
+        def exchange(position, m):
+            return pltpu.make_async_remote_copy(
+                src_ref=gram_ref,
+                dst_ref=arrived.at[k, mine],
+                send_sem=g_send.at[k, m],
+                recv_sem=g_recv.at[k, mine],
+                device_id=peer(axis, shift, position),
+                device_id_type=MESH,
+            )
+
+        def incoming(position):
+            return pltpu.make_async_remote_copy(
+                src_ref=gram_ref,
+                dst_ref=arrived.at[k, position],
+                send_sem=g_send.at[k, 0],
+                recv_sem=g_recv.at[k, position],
+                device_id=peer(axis, shift, position),
+                device_id_type=MESH,
+            )
+
+        for m in range(1, QUARTERS):
+            exchange(mine ^ m, m).start()
+        arrived[k, mine] = gram_ref[...]
+        for m in range(1, QUARTERS):
+            exchange(mine ^ m, m).wait_send()
+        for m in range(1, QUARTERS):
+            incoming(mine ^ m).wait_recv()
+        total = arrived[k, 0]
+        for position in range(1, QUARTERS):
+            total = total + arrived[k, position]
+        gram_ref[...] = total
+
     for p in range(2):
         for t, q, d in sends:
             link(p, t, q, d).wait_send()
@@ -259,10 +317,10 @@
     result = jax.ShapeDtypeStruct((shard_blocks, block_size, states), jnp.float32)
     vmem = pl.BlockSpec(memory_space=pltpu.VMEM)
     return pl.pallas_call(
-        functools.partial(coupling_kernel, groups),
-        out_shape=(result, result),
+        functools.partial(coupling_kernel, groups, 1.0 / (shard_blocks * block_size * cycle * groups)),
+        out_shape=(result, result, jax.ShapeDtypeStruct((states, states), jnp.float32)),
         in_specs=[pl.BlockSpec(memory_space=pltpu.SMEM), vmem, vmem, pl.BlockSpec(memory_space=pl.ANY)],
-        out_specs=(vmem, vmem),
+        out_specs=(vmem, vmem, vmem),
         scratch_shapes=[slab] * (2 * cycle + 2)
         + [
             slab,
@@ -273,6 +331,9 @@
             pltpu.SemaphoreType.DMA((2, cycle, QUARTERS)),
             pltpu.SemaphoreType.DMA((2, 2)),
             pltpu.SemaphoreType.DMA((2, 2)),
+            pltpu.VMEM((4, 4, states, states), jnp.float32),
+            pltpu.SemaphoreType.DMA((4, 4)),
+            pltpu.SemaphoreType.DMA((4, 4)),
         ],
         compiler_params=pltpu.CompilerParams(
             collective_id=0, has_side_effects=True, vmem_limit_bytes=48 * 1024 * 1024
@@ -366,11 +427,8 @@
     index = jnp.transpose(block_columns, (0, 2, 1)).reshape(-1)
     start_slab = trial_slab.reshape(shard_blocks, block_size, states)
     weights = potential.reshape(shard_blocks, block_size, 1)
-    filtered_once, filtered = couple_both(hamiltonian, index, start_slab, weights)
+    filtered_once, filtered, gram = couple_both(hamiltonian, index, start_slab, weights)
     flat = filtered.reshape(shard_blocks * block_size, states)
-    rows_total = flat.shape[0] * lax.axis_size("group") * lax.axis_size("blk")
-    local_gram = jnp.dot(flat.T, flat, precision=precise) * (1.0 / rows_total)
-    gram = summed_over_mesh(local_gram)
     lower = lax.linalg.cholesky(gram, symmetrize_input=False)
     ortho_slab = lax.linalg.triangular_solve(
         lower, flat, left_side=False, lower=True, transpose_a=True

time: 130 us -> 125 us (0.962)
  Pallas kernels: 97.6 us -> 95.1 us
  matrix products: 3 us -> 1.36 us
    pallas_call x2 -> x1, Pallas kernels: 97.6 us -> 95.1 us  [couple_both(): pl.pallas_call(functools.partial(coupling_kernel, groups, 1.0 / (shard_bl...]
    dot_general x1 -> x0, matrix products: 1.64 us -> none  [on_device(): local_gram = jnp.dot(flat.T, flat, precision=precise) * (1.0 / rows_total)]
where the time goes in v13:
time: 125 us; the launch traced here: 124 us
  Pallas kernels  95.1 us (76%)
  other arithmetic  22.9 us (18%)
  local copies, waits for them, and re-layouts  3.69 us (3%)
  matrix products  1.36 us (1%)
    pallas_call x1, Pallas kernels, couple_both(): pl.pallas_call(functools.partial(coupling_kernel, groups, 1.0 / (shard_bl...  95.1 us
    another operation x3, other arithmetic, on_device(): lower = lax.linalg.cholesky(gram, symmetrize_input=False)  12.4 us
    another operation x1, other arithmetic, on_device(): lax.linalg.triangular_solve(lower, flat, left_side=False, lower=True, tra...  9.81 us

profile of v13, /device:TPU:1, one launch (start us, length us, event | category | flops | bytes accessed | tf_op | source)
XLA Modules:
  0.0 123.7 jit_solution(17187644127711810805)
XLA Ops:
  0.6 0.9 reshape.24.index_ref
  1.5 1.0 reshape.28.weight_ref
  2.6 0.0 copy-start
  2.6 1.0 copy-done
  3.6 95.1 %shard_map.59 = (f32[16,64,128]{2,1,0:T(8,128)}, f32[16,64,128]{2,1,0:T(8,128)S(1)}, f32[128,128]{1,0:T(8,128)S(1)}) custom-call(s32[1152]{0:T(1024)S(1)} %reshape.24.index_ref, f32[16,64,128]{2,1,0:T(8,128)S(1)} %bitcast.11, f32[16,64,1]{2,1,0:T(8,128)S(1)} %reshape.28.weight_ref, bf16[16,18,64,256]{3,2,1,0:T(8,128)(2,1)} %ham_hbm.1), custom_call_target="tpu_custom_call" | custom-call | flops 2415919104 | bytes 18874368 | tf_op jit(solution)/shard_map/pallas_call | solution.py:319
  98.8 11.7 %cholesky.16 = f32[128,128]{1,0:T(8,128)S(1)} custom-call(f32[128,128]{1,0:T(8,128)S(1)} %get-tuple-element.5), custom_call_target="Cholesky" | custom-call | tf_op jit(solution)/shard_map/cholesky | solution.py:432
  110.5 0.6 compare_reduce_fusion
  111.2 0.7 fusion.2
  111.8 0.7 copy.8
  112.5 9.8 %custom-call.5 = f32[1,128,128]{1,2,0:T(8,128)S(1)} custom-call(f32[1,128,128]{2,1,0:T(8,128)S(1)} %get-tuple-element.11), custom_call_target="InvertDiagBlocksLowerTriangular" | custom-call | tf_op jit(solution)/shard_map/triangular_solve | solution.py:433
  122.4 1.4 %fusion = f32[1024,128]{1,0:T(8,128)} fusion(f32[1024,128]{1,0:T(8,128)S(1)} %bitcast.12, f32[1,128,128]{1,2,0:T(8,128)S(1)} %custom-call.5), kind=kOutput, calls=%fused_computation | convolution fusion | flops 201326592 | bytes 1114112 | tf_op jit(solution)/shard_map/triangular_solve | solution.py:433
  (1 shorter events, 0.0 us)
Async XLA Ops:
  2.6 1.0 copy-start

commit v14 on v13

--- a/solution.py
+++ b/solution.py
@@ -238,7 +238,7 @@
                 side(p, 1, (grp, me)).wait_recv()
 
             def row(r, carry):
-                blocks = [data[index_ref[(r * per_source + j) * nsrc + source]] for j in range(per_source)]
+                blocks = [data[index_ref[r, j, source]] for j in range(per_source)]
                 picked = jnp.concatenate(blocks, axis=0)
                 out_ref[r] += jnp.dot(
                     ham_buf[slot, r], picked, preferred_element_type=jnp.float32
@@ -424,7 +424,7 @@
     shard_blocks = hamiltonian.shape[0]
     block_size = hamiltonian.shape[2]
     states = trial_slab.shape[1]
-    index = jnp.transpose(block_columns, (0, 2, 1)).reshape(-1)
+    index = jnp.transpose(block_columns, (0, 2, 1))
     start_slab = trial_slab.reshape(shard_blocks, block_size, states)
     weights = potential.reshape(shard_blocks, block_size, 1)
     filtered_once, filtered, gram = couple_both(hamiltonian, index, start_slab, weights)

time: 125 us -> 126 us (level)
    unnamed x3 -> x5, local copies, waits for them, and re-layouts: 1.77 us -> 2.52 us
where the time goes in v14:
time: 126 us; the launch traced here: 124 us
  Pallas kernels  95.6 us (76%)
  other arithmetic  22.9 us (18%)
  local copies, waits for them, and re-layouts  3.55 us (3%)
  matrix products  1.36 us (1%)
    pallas_call x1, Pallas kernels, couple_both(): pl.pallas_call(functools.partial(coupling_kernel, groups, 1.0 / (shard_bl...  95.6 us
    another operation x3, other arithmetic, on_device(): lower = lax.linalg.cholesky(gram, symmetrize_input=False)  12.4 us
    another operation x1, other arithmetic, on_device(): lax.linalg.triangular_solve(lower, flat, left_side=False, lower=True, tra...  9.81 us
    unnamed x5, local copies, waits for them, and re-layouts  2.52 us

profile of v14, /device:TPU:1, one launch (start us, length us, event | category | flops | bytes accessed | tf_op | source)
XLA Modules:
  0.0 124.0 jit_solution(5401866704879404902)
XLA Ops:
  0.6 1.0 reshape.24.weight_ref
  1.7 0.0 copy-start
  1.7 1.0 copy-done
  2.7 0.0 copy-start.1
  2.7 0.8 copy-done.1
  3.5 95.6 %shard_map.59 = (f32[16,64,128]{2,1,0:T(8,128)}, f32[16,64,128]{2,1,0:T(8,128)S(1)}, f32[128,128]{1,0:T(8,128)S(1)}) custom-call(s32[16,4,18]{2,1,0:T(4,128)S(1)} %bitcast.13, f32[16,64,128]{2,1,0:T(8,128)S(1)} %bitcast.11, f32[16,64,1]{2,1,0:T(8,128)S(1)} %reshape.24.weight_ref, bf16[16,18,64,256]{3,2,1,0:T(8,128)(2,1)} %ham_hbm.1), custom_call_target="tpu_custom_call" | custom-call | flops 2415919104 | bytes 18874368 | tf_op jit(solution)/shard_map/pallas_call | solution.py:319
  99.1 11.7 %cholesky.16 = f32[128,128]{1,0:T(8,128)S(1)} custom-call(f32[128,128]{1,0:T(8,128)S(1)} %get-tuple-element.5), custom_call_target="Cholesky" | custom-call | tf_op jit(solution)/shard_map/cholesky | solution.py:432
  110.8 0.6 compare_reduce_fusion
  111.4 0.7 fusion.2
  112.1 0.7 copy.8
  112.8 9.8 %custom-call.5 = f32[1,128,128]{1,2,0:T(8,128)S(1)} custom-call(f32[1,128,128]{2,1,0:T(8,128)S(1)} %get-tuple-element.11), custom_call_target="InvertDiagBlocksLowerTriangular" | custom-call | tf_op jit(solution)/shard_map/triangular_solve | solution.py:433
  122.7 1.4 %fusion = f32[1024,128]{1,0:T(8,128)} fusion(f32[1024,128]{1,0:T(8,128)S(1)} %bitcast.12, f32[1,128,128]{1,2,0:T(8,128)S(1)} %custom-call.5), kind=kOutput, calls=%fused_computation | convolution fusion | flops 201326592 | bytes 1114112 | tf_op jit(solution)/shard_map/triangular_solve | solution.py:433
  (1 shorter events, 0.0 us)
Async XLA Ops:
  1.7 1.0 copy-start
  2.7 0.8 copy-start.1

commit v15 on v13

--- a/solution.py
+++ b/solution.py
@@ -207,10 +207,19 @@
             continue
         if kind == "finish":
             if p == 0:
-                once_ref[...] = 0.5 * (once_ref[...] + weight_ref[...] * trial_ref[...])
+                columns = jnp.transpose(weight_ref[...])
+                rows_per = columns.shape[0] // (shard_blocks // columns.shape[1])
+                weight_col = [
+                    columns[(b % (columns.shape[0] // rows_per)) * rows_per : (b % (columns.shape[0] // rows_per) + 1) * rows_per,
+                            b // (columns.shape[0] // rows_per) : b // (columns.shape[0] // rows_per) + 1]
+                    for b in range(shard_blocks)
+                ]
+                for b in range(shard_blocks):
+                    once_ref[b] = 0.5 * (once_ref[b] + weight_col[b] * trial_ref[b])
                 rounded[...] = once_ref[...].astype(rounded.dtype)
             else:
-                next_ref[...] = next_ref[...] + weight_ref[...] * once_ref[...] - trial_ref[...]
+                for b in range(shard_blocks):
+                    next_ref[b] = next_ref[b] + weight_col[b] * once_ref[b] - trial_ref[b]
                 local = jnp.zeros(gram_ref.shape, jnp.float32)
                 for r in range(shard_blocks):
                     rows = next_ref[r]
@@ -426,7 +435,7 @@
     states = trial_slab.shape[1]
     index = jnp.transpose(block_columns, (0, 2, 1)).reshape(-1)
     start_slab = trial_slab.reshape(shard_blocks, block_size, states)
-    weights = potential.reshape(shard_blocks, block_size, 1)
+    weights = potential.reshape(-1, 128)
     filtered_once, filtered, gram = couple_both(hamiltonian, index, start_slab, weights)
     flat = filtered.reshape(shard_blocks * block_size, states)
     lower = lax.linalg.cholesky(gram, symmetrize_input=False)

time: 125 us -> 125 us (level)
  no operation moved by 1% of the time
where the time goes in v15:
time: 125 us; the launch traced here: 124 us
  Pallas kernels  95.3 us (76%)
  other arithmetic  22.9 us (18%)
  local copies, waits for them, and re-layouts  3.35 us (3%)
  matrix products  1.36 us (1%)
    pallas_call x1, Pallas kernels, couple_both(): pl.pallas_call(functools.partial(coupling_kernel, groups, 1.0 / (shard_bl...  95.3 us
    another operation x3, other arithmetic, on_device(): lower = lax.linalg.cholesky(gram, symmetrize_input=False)  12.4 us
    another operation x1, other arithmetic, on_device(): lax.linalg.triangular_solve(lower, flat, left_side=False, lower=True, tra...  9.81 us

profile of v15, /device:TPU:1, one launch (start us, length us, event | category | flops | bytes accessed | tf_op | source)
XLA Modules:
  0.0 123.6 jit_solution(12452866509042217152)
XLA Ops:
  0.6 0.9 reshape.24.index_ref
  1.5 0.0 copy-start
  1.5 1.0 copy-done
  2.6 0.0 copy-start.1
  2.6 0.7 copy-done.1
  3.3 95.3 %shard_map.59 = (f32[16,64,128]{2,1,0:T(8,128)}, f32[16,64,128]{2,1,0:T(8,128)S(1)}, f32[128,128]{1,0:T(8,128)S(1)}) custom-call(s32[1152]{0:T(1024)S(1)} %reshape.24.index_ref, f32[16,64,128]{2,1,0:T(8,128)S(1)} %bitcast.13, f32[8,128]{1,0:T(8,128)S(1)} %bitcast.14, bf16[16,18,64,256]{3,2,1,0:T(8,128)(2,1)} %ham_hbm.1), custom_call_target="tpu_custom_call" | custom-call | flops 2415919104 | bytes 18874368 | tf_op jit(solution)/shard_map/pallas_call | solution.py:328
  98.6 11.7 %cholesky.16 = f32[128,128]{1,0:T(8,128)S(1)} custom-call(f32[128,128]{1,0:T(8,128)S(1)} %get-tuple-element.5), custom_call_target="Cholesky" | custom-call | tf_op jit(solution)/shard_map/cholesky | solution.py:441
  110.3 0.6 compare_reduce_fusion
  111.0 0.7 fusion.2
  111.7 0.7 copy.6
  112.4 9.8 %custom-call.5 = f32[1,128,128]{1,2,0:T(8,128)S(1)} custom-call(f32[1,128,128]{2,1,0:T(8,128)S(1)} %get-tuple-element.9), custom_call_target="InvertDiagBlocksLowerTriangular" | custom-call | tf_op jit(solution)/shard_map/triangular_solve | solution.py:442
  122.2 1.4 %fusion = f32[1024,128]{1,0:T(8,128)} fusion(f32[1024,128]{1,0:T(8,128)S(1)} %bitcast.12, f32[1,128,128]{1,2,0:T(8,128)S(1)} %custom-call.5), kind=kOutput, calls=%fused_computation | convolution fusion | flops 201326592 | bytes 1114112 | tf_op jit(solution)/shard_map/triangular_solve | solution.py:442
  (1 shorter events, 0.0 us)
Async XLA Ops:
  1.5 1.0 copy-start
  2.6 0.7 copy-start.1
